TPU v7x, 32 devices: a whole 2x2x4 slice. The times are simulated.
32 devices in a mesh: sector: 16 (over z, y, x), op: 2 (over core).
Axes of the slice: x: 2, y: 2, z: 4, core: 2. Of those that a mesh axis runs over, the one named last changes fastest.
Arguments:
- wave_start: float32 [32, 256, 256], P('sector'), may hold values from -6 to 6
- left_blocks: float32 [4, 32, 256, 256], P('op', 'sector'), may hold values from -0.375 to 0.375
- right_blocks: float32 [4, 32, 256, 256], P('op', 'sector'), may hold values from -0.1875 to 0.1875
- term_shifts: int32 [4], P('op'), may hold values from -1 to 1
- preconditioner: float32 [32, 256, 256], P('sector'), may hold values from 0.5 to 4
Outputs:
- basis: float32 [3, 32, 256, 256], P(None, 'sector', 'op')
- ritz: float32 [3], replicated
Inputs may be any that keep to these rules, and one draw needn't show every extreme that they name: Each term changes the charge sector by term_shifts, one of -1, 0 and 1.
All inputs are finite; a program needn't handle non-finite values.
Results may differ from a plain program's by a relative error of at most 0.0003.
Values sent between devices are 32-bit elements; how exact they have to be, the bound alone decides.
No kernel may reach another device: no remote copies, remote signals or barrier semaphores. Data moves between devices by JAX's collectives and lax.ppermute only.
A program may use at most 64 MiB of HBM per device.

v0:
```python
import jax
import jax.numpy as jnp
from jax import lax
from jax.sharding import PartitionSpec as P

ITERS = 3


EPSILON = 1e-06


def with_halo(cells, sides, width):
    for axis, dim in sides:
        count = lax.axis_size(axis)
        ends = count - 1
        head = lax.slice_in_dim(cells, 0, width, axis=dim)
        tail = lax.slice_in_dim(cells, cells.shape[dim] - width, cells.shape[dim], axis=dim)
        cells = jnp.concatenate(
            [
                lax.ppermute(tail, axis, [(i, (i + 1) % count) for i in range(ends)]),
                cells,
                lax.ppermute(head, axis, [((i + 1) % count, i) for i in range(ends)]),
            ],
            axis=dim,
        )
    return cells


def body(wave_start, left_blocks, right_blocks, term_shifts, preconditioner):
    highest = lax.Precision.HIGHEST
    width = wave_start.shape[1]
    row_count = width // lax.axis_size("op")
    first_row = lax.axis_index("op") * row_count
    total = float(wave_start.shape[0] * lax.axis_size("sector") * width * wave_start.shape[2])

    def own_rows(values):
        return lax.dynamic_slice_in_dim(values, first_row, row_count, axis=values.ndim - 2)

    def portion(values):
        return own_rows(values)

    start_sum = lax.psum(jnp.sum(jnp.square(portion(wave_start))), ("sector", "op")) / total
    factor = lax.rsqrt(start_sum + EPSILON)
    applied = wave_start * factor
    basis = [wave_start * factor]
    ritz = []
    for index in range(ITERS):
        latest = basis[-1]
        padded = with_halo(applied, (("sector", 0),), 1)
        shift = term_shifts[:, None, None, None]
        source = jnp.where(
            shift == 1,
            padded[None, :-2],
            jnp.where(shift == -1, padded[None, 2:], padded[None, 1:-1]),
        )
        inner = jnp.einsum("ksab,ksbc->ksac", left_blocks, source, precision=highest)
        image = lax.psum(jnp.einsum("ksac,kscd->sad", inner, right_blocks, precision=highest), "op")
        ratio_image = image / preconditioner
        ratio_basis = latest / preconditioner
        part_image = portion(ratio_image)
        part_basis = portion(ratio_basis)
        pieces = [
            jnp.sum(portion(latest) * portion(image)),
            jnp.sum(part_image * part_image),
            jnp.sum(part_image * part_basis),
            jnp.sum(part_basis * part_basis),
        ]
        pieces = pieces + [jnp.sum(portion(member) * part_image) for member in basis]
        pieces = pieces + [jnp.sum(portion(member) * part_basis) for member in basis]
        sums = lax.psum(jnp.stack(pieces), ("sector", "op")) / total
        count = len(basis)
        theta = sums[0]
        correlations = sums[4 : 4 + count] - theta * sums[4 + count :]
        correction = ratio_image - theta * ratio_basis
        ortho = correction
        for position, member in enumerate(basis):
            ortho = ortho - correlations[position] * member
        length = (
            sums[1]
            - 2.0 * theta * sums[2]
            + theta * theta * sums[3]
            - jnp.sum(jnp.square(correlations))
        )
        fresh = ortho * lax.rsqrt(length + EPSILON)
        basis.append(fresh)
        ritz.append(theta)
        if index + 1 < ITERS:
            applied = fresh
    output = jnp.stack([portion(member) for member in basis[1:]])
    return (output, jnp.stack(ritz))


def solution(mesh):
    placed = (
        P("sector", None, None),
        P("op", "sector", None, None),
        P("op", "sector", None, None),
        P("op"),
        P("sector", None, None),
    )
    return jax.shard_map(
        body,
        mesh=mesh,
        in_specs=placed,
        out_specs=(P(None, "sector", "op", None), P()),
        check_vma=False,
    )
```

profile of v0, /device:TPU:0, one launch (start us, length us, event | category | flops | bytes accessed | tf_op | source)
XLA Modules:
  0.0 348.4 jit_solution(17925297234444958489)
XLA Ops:
  7.2 1.7 multiply_reduce_fusion.24
  8.9 42.2 %psum.49 = f32[]{:T(128)} all-reduce(f32[]{:T(128)} %multiply_reduce_fusion.24), channel_id=1, replica_groups=mesh['sector'=16,'op'=2] {'sector','op'}, use_global_device_ids=true, to_apply=%region_1.0 | all-reduce | flops 1 | bytes 8 | tf_op jit(solution)/shard_map/psum | solution.py:42
  53.2 4.3 %collective-permute-start = (f32[1,256,256]{2,1,0:T(8,128)S(1)}, f32[1,256,256]{2,1,0:T(8,128)S(1)}, u32[]{:S(2)}, u32[]{:S(2)}) collective-permute-start(f32[1,256,256]{2,1,0:T(8,128)S(1)} %get-tuple-element.48), channel_id=1, source_target_pairs={{0,2},{2,4},{4,6},{6,8},{8,10},{10,12},{12,14},{14,16},{16,18},{18... | collective-permute-start | bytes 786440 | tf_op jit(solution)/shard_map/ppermute | solution.py:20
  58.8 8.3 %collective-permute-done = f32[1,256,256]{2,1,0:T(8,128)S(1)} collective-permute-done((f32[1,256,256]{2,1,0:T(8,128)S(1)}, f32[1,256,256]{2,1,0:T(8,128)S(1)}, u32[]{:S(2)}, u32[]{:S(2)}) %collective-permute-start) | collective-permute-done | bytes 262176 | tf_op jit(solution)/shard_map/ppermute | solution.py:20
  67.2 1.9 collective-permute-done.1
  69.2 1.4 convolution_bitcast_fusion.2
  70.5 2.0 convolution_bitcast_fusion.5
  72.5 17.9 %all-reduce.4.cloned.1.call-done = f32[2,256,256]{2,1,0:T(8,128)} async-done(((f32[2,256,256]{2,1,0:T(8,128)}), f32[2,256,256]{2,1,0:T(8,128)}) %all-reduce.4.cloned.1.call-update) | async-done | bytes 524304 | tf_op jit(solution)/shard_map/psum | solution.py:57
  92.5 3.8 %stack.102 = f32[6]{0:T(128)S(1)} concatenate(f32[1]{0:T(128)} %bitcast.3, f32[1]{0:T(128)} %bitcast.4, f32[1]{0:T(128)} %bitcast.5, f32[1]{0:T(128)} %bitcast.6, f32[1]{0:T(128)} %bitcast.7, f32[1]{0:T(128)} %bitcast.8), dimensions={0} | concatenate | bytes 48 | tf_op jit(solution)/shard_map/stack | solution.py:70
  96.3 40.5 %psum.51 = f32[6]{0:T(128)S(1)} all-reduce(f32[6]{0:T(128)S(1)} %stack.102), channel_id=1, replica_groups=mesh['sector'=16,'op'=2] {'sector','op'}, use_global_device_ids=true, to_apply=%region_9.10 | all-reduce | flops 6 | bytes 48 | tf_op jit(solution)/shard_map/psum | solution.py:70
  143.4 2.0 fusion.10
  145.5 4.2 %collective-permute-start.2 = (f32[1,256,256]{2,1,0:T(8,128)S(1)}, f32[1,256,256]{2,1,0:T(8,128)S(1)}, u32[]{:S(2)}, u32[]{:S(2)}) collective-permute-start(f32[1,256,256]{2,1,0:T(8,128)S(1)} %get-tuple-element.44), channel_id=1, source_target_pairs={{0,2},{2,4},{4,6},{6,8},{8,10},{10,12},{12,14},{14,16},{16,18},{18... | collective-permute-start | bytes 786440 | tf_op jit(solution)/shard_map/ppermute | solution.py:20
  151.0 8.2 %collective-permute-done.2 = f32[1,256,256]{2,1,0:T(8,128)S(1)} collective-permute-done((f32[1,256,256]{2,1,0:T(8,128)S(1)}, f32[1,256,256]{2,1,0:T(8,128)S(1)}, u32[]{:S(2)}, u32[]{:S(2)}) %collective-permute-start.2) | collective-permute-done | bytes 262176 | tf_op jit(solution)/shard_map/ppermute | solution.py:20
  159.3 1.8 collective-permute-done.3
  161.2 1.4 convolution_bitcast_fusion.1
  162.5 1.9 convolution_bitcast_fusion.4
  164.5 18.0 %all-reduce.6.cloned.1.call-done = f32[2,256,256]{2,1,0:T(8,128)} async-done(((f32[2,256,256]{2,1,0:T(8,128)}), f32[2,256,256]{2,1,0:T(8,128)}) %all-reduce.6.cloned.1.call-update) | async-done | bytes 524304 | tf_op jit(solution)/shard_map/psum | solution.py:57
  184.6 5.1 %stack.112 = f32[8]{0:T(128)S(1)} concatenate(f32[1]{0:T(128)} %bitcast.19, f32[1]{0:T(128)} %bitcast.20, f32[1]{0:T(128)} %bitcast.21, f32[1]{0:T(128)} %bitcast.22, f32[1]{0:T(128)} %bitcast.23, f32[1]{0:T(128)} %bitcast.24, f32[1]{0:T(128)} %bitcast.25, f32[1]{0:T(128)} %bitcast.26), dimensions={0} | concatenate | bytes 64 | tf_op jit(solution)/shard_map/stack | solution.py:70
  189.8 40.5 %psum.53 = f32[8]{0:T(128)S(1)} all-reduce(f32[8]{0:T(128)S(1)} %stack.112), channel_id=1, replica_groups=mesh['sector'=16,'op'=2] {'sector','op'}, use_global_device_ids=true, to_apply=%region_19.20 | all-reduce | flops 8 | bytes 64 | tf_op jit(solution)/shard_map/psum | solution.py:70
  237.2 4.1 %fusion.9 = (f32[2,256,256]{2,1,0:T(8,128)}, f32[2,256,256]{2,1,0:T(8,128)S(1)}) fusion(f32[2,256,256]{2,1,0:T(8,128)S(1)} %copy-done.1, f32[]{:T(128)S(6)} %rsqrt.14, f32[2,256,256]{2,1,0:T(8,128)S(1)} %get-tuple-element.33, f32[]{:T(128)} %bitcast.29, f32[2,256,256]{2,1,0:T(8,128)S(1)} %get-tuple-element.35, f32[]{:T(128)} %bitcast.28, ...), kind=kLoop, calls=%fused_computation.66 | loop fusion | flops 1048576 | bytes 3670032 | tf_op jit(solution)/shard_map/div | solution.py:59
  241.3 4.2 %collective-permute-start.4 = (f32[1,256,256]{2,1,0:T(8,128)S(1)}, f32[1,256,256]{2,1,0:T(8,128)S(1)}, u32[]{:S(2)}, u32[]{:S(2)}) collective-permute-start(f32[1,256,256]{2,1,0:T(8,128)S(1)} %get-tuple-element.40), channel_id=1, source_target_pairs={{0,2},{2,4},{4,6},{6,8},{8,10},{10,12},{12,14},{14,16},{16,18},{18... | collective-permute-start | bytes 786440 | tf_op jit(solution)/shard_map/ppermute | solution.py:20
  245.5 1.5 collective-permute-start.5
  247.0 8.0 %collective-permute-done.4 = f32[1,256,256]{2,1,0:T(8,128)S(1)} collective-permute-done((f32[1,256,256]{2,1,0:T(8,128)S(1)}, f32[1,256,256]{2,1,0:T(8,128)S(1)}, u32[]{:S(2)}, u32[]{:S(2)}) %collective-permute-start.4) | collective-permute-done | bytes 262176 | tf_op jit(solution)/shard_map/ppermute | solution.py:20
  255.0 1.8 collective-permute-done.5
  256.9 1.4 convolution_bitcast_fusion
  258.3 1.9 convolution_bitcast_fusion.3
  260.2 18.0 %all-reduce.8.cloned.1.call-done = f32[2,256,256]{2,1,0:T(8,128)} async-done(((f32[2,256,256]{2,1,0:T(8,128)}), f32[2,256,256]{2,1,0:T(8,128)}) %all-reduce.8.cloned.1.call-update) | async-done | bytes 524304 | tf_op jit(solution)/shard_map/psum | solution.py:57
  279.6 1.5 multiply_reduce_fusion
  281.1 6.2 %stack.124 = f32[10]{0:T(128)S(1)} concatenate(f32[1]{0:T(128)} %bitcast.37, f32[1]{0:T(128)} %bitcast.38, f32[1]{0:T(128)} %bitcast.39, f32[1]{0:T(128)} %bitcast.40, f32[1]{0:T(128)} %bitcast.41, f32[1]{0:T(128)} %bitcast.42, f32[1]{0:T(128)} %bitcast.43, f32[1]{0:T(128)} %bitcast.44, f32[1]{0:T(128)} %bitcast.45, f32[1]{0:T(128)} %bitcast.46), dimensions={0} | concatenate | bytes 80 | tf_op jit(solution)/shard_map/stack | solution.py:70
  287.4 40.5 %psum.55 = f32[10]{0:T(128)S(1)} all-reduce(f32[10]{0:T(128)S(1)} %stack.124), channel_id=1, replica_groups=mesh['sector'=16,'op'=2] {'sector','op'}, use_global_device_ids=true, to_apply=%region_32.33 | all-reduce | flops 10 | bytes 80 | tf_op jit(solution)/shard_map/psum | solution.py:70
  330.5 2.5 pad_maximum_fusion.7
  337.4 3.5 %multiply_bitcast_fusion = f32[1,2,128,256]{3,2,1,0:T(8,128)S(1)} fusion(f32[2,256,256]{2,1,0:T(8,128)S(1)} %get-tuple-element.29, s32[]{:T(128)S(6)} %select_n.22, f32[2,256,256]{2,1,0:T(8,128)} %copy-done.11, f32[2,256,256]{2,1,0:T(8,128)S(1)} %copy-done.10, f32[2,256,256]{2,1,0:T(8,128)S(1)} %get-tuple-element.33, ...), kind=kLoop, calls=%fused_computation.27 | loop fusion | flops 589824 | bytes 1572888 | tf_op jit(solution)/shard_map/stack | solution.py:89
  (66 shorter events, 16.7 us)
Async XLA Ops:
  7.2 62.0 %copy-start = (f32[2,2,256,256]{3,2,1,0:T(8,128)S(1)}, f32[2,2,256,256]{3,2,1,0:T(8,128)}, u32[]{:S(2)}) copy-start(f32[2,2,256,256]{3,2,1,0:T(8,128)} %param.6) | copy-start | bytes 3145732
  7.2 83.3 %all-reduce.4.cloned.1.call-start = ((), (), s32[]{:S(2)}) async-start(), calls=%async_computation | async-start | bytes 1048576 | tf_op jit(solution)/shard_map/psum | solution.py:57
  53.1 38.6 %copy-start.6 = (f32[2,256,256]{2,1,0:T(8,128)}, f32[2,256,256]{2,1,0:T(8,128)S(1)}, u32[]{:S(2)}) copy-start(f32[2,256,256]{2,1,0:T(8,128)S(1)} %get-tuple-element.34) | copy-start | bytes 1572868
  53.2 5.6 %copy-start.16 = (s32[2]{0:T(128)S(1)}, s32[2]{0:T(128)}, u32[]{:S(2)}) copy-start(s32[2]{0:T(128)} %param.8) | copy-start | bytes 28
  53.2 14.0 %collective-permute-start = (f32[1,256,256]{2,1,0:T(8,128)S(1)}, f32[1,256,256]{2,1,0:T(8,128)S(1)}, u32[]{:S(2)}, u32[]{:S(2)}) collective-permute-start(f32[1,256,256]{2,1,0:T(8,128)S(1)} %get-tuple-element.48), channel_id=1, source_target_pairs={{0,2},{2,4},{4,6},{6,8},{8,10},{10,12},{12,14},{14,16},{16,18},{18... | collective-permute-start | bytes 786440 | tf_op jit(solution)/shard_map/ppermute | solution.py:20
  57.5 11.5 %collective-permute-start.1 = (f32[1,256,256]{2,1,0:T(8,128)S(1)}, f32[1,256,256]{2,1,0:T(8,128)S(1)}, u32[]{:S(2)}, u32[]{:S(2)}) collective-permute-start(f32[1,256,256]{2,1,0:T(8,128)S(1)} %get-tuple-element.49), channel_id=1, source_target_pairs={{2,0},{4,2},{6,4},{8,6},{10,8},{12,10},{14,12},{16,14},{18,16},{20... | collective-permute-start | bytes 786440 | tf_op jit(solution)/shard_map/ppermute | solution.py:22
  69.1 1.4 copy-start.2
  72.5 18.0 %copy-start.1 = (f32[2,256,256]{2,1,0:T(8,128)S(1)}, f32[2,256,256]{2,1,0:T(8,128)}, u32[]{:S(2)}) copy-start(f32[2,256,256]{2,1,0:T(8,128)} %param.9) | copy-start | bytes 1572868
  72.5 110.0 %all-reduce.6.cloned.1.call-start = ((), (), s32[]{:S(2)}) async-start(), calls=%async_computation.1 | async-start | bytes 1048576 | tf_op jit(solution)/shard_map/psum | solution.py:57
  90.5 1.2 copy-start.14
  91.7 0.8 copy-start.8
  145.5 38.2 %copy-start.5 = (f32[2,256,256]{2,1,0:T(8,128)}, f32[2,256,256]{2,1,0:T(8,128)S(1)}, u32[]{:S(2)}) copy-start(f32[2,256,256]{2,1,0:T(8,128)S(1)} %get-tuple-element.32) | copy-start | bytes 1572868
  145.5 13.7 %collective-permute-start.2 = (f32[1,256,256]{2,1,0:T(8,128)S(1)}, f32[1,256,256]{2,1,0:T(8,128)S(1)}, u32[]{:S(2)}, u32[]{:S(2)}) collective-permute-start(f32[1,256,256]{2,1,0:T(8,128)S(1)} %get-tuple-element.44), channel_id=1, source_target_pairs={{0,2},{2,4},{4,6},{6,8},{8,10},{10,12},{12,14},{14,16},{16,18},{18... | collective-permute-start | bytes 786440 | tf_op jit(solution)/shard_map/ppermute | solution.py:20
  149.7 11.3 %collective-permute-start.3 = (f32[1,256,256]{2,1,0:T(8,128)S(1)}, f32[1,256,256]{2,1,0:T(8,128)S(1)}, u32[]{:S(2)}, u32[]{:S(2)}) collective-permute-start(f32[1,256,256]{2,1,0:T(8,128)S(1)} %get-tuple-element.45), channel_id=1, source_target_pairs={{2,0},{4,2},{6,4},{8,6},{10,8},{12,10},{14,12},{16,14},{18,16},{20... | collective-permute-start | bytes 786440 | tf_op jit(solution)/shard_map/ppermute | solution.py:22
  161.1 1.4 copy-start.3
  164.5 113.8 %all-reduce.8.cloned.1.call-start = ((), (), s32[]{:S(2)}) async-start(), calls=%async_computation.2 | async-start | bytes 1048576 | tf_op jit(solution)/shard_map/psum | solution.py:57
  182.5 1.2 copy-start.13
  183.7 0.9 copy-start.7
  241.3 13.7 %collective-permute-start.4 = (f32[1,256,256]{2,1,0:T(8,128)S(1)}, f32[1,256,256]{2,1,0:T(8,128)S(1)}, u32[]{:S(2)}, u32[]{:S(2)}) collective-permute-start(f32[1,256,256]{2,1,0:T(8,128)S(1)} %get-tuple-element.40), channel_id=1, source_target_pairs={{0,2},{2,4},{4,6},{6,8},{8,10},{10,12},{12,14},{14,16},{16,18},{18... | collective-permute-start | bytes 786440 | tf_op jit(solution)/shard_map/ppermute | solution.py:20
  245.5 11.3 %collective-permute-start.5 = (f32[1,256,256]{2,1,0:T(8,128)S(1)}, f32[1,256,256]{2,1,0:T(8,128)S(1)}, u32[]{:S(2)}, u32[]{:S(2)}) collective-permute-start(f32[1,256,256]{2,1,0:T(8,128)S(1)} %get-tuple-element.41), channel_id=1, source_target_pairs={{2,0},{4,2},{6,4},{8,6},{10,8},{12,10},{14,12},{16,14},{18,16},{20... | collective-permute-start | bytes 786440 | tf_op jit(solution)/shard_map/ppermute | solution.py:22
  256.9 1.4 copy-start.4
  278.2 1.2 copy-start.9
  278.2 1.4 copy-start.12
  279.5 1.7 copy-start.11
  279.6 57.8 %copy-start.10 = (f32[2,256,256]{2,1,0:T(8,128)S(1)}, f32[2,256,256]{2,1,0:T(8,128)}, u32[]{:S(2)}) copy-start(f32[2,256,256]{2,1,0:T(8,128)} %get-tuple-element.28) | copy-start | bytes 1572868
  337.4 3.5 %copy-start.15 = (f32[1,2,128,256]{3,2,1,0:T(8,128)S(1)}, f32[1,2,128,256]{3,2,1,0:T(8,128)}, u32[]{:S(2)}) copy-start(f32[1,2,128,256]{3,2,1,0:T(8,128)} %get-tuple-element.37) | copy-start | bytes 786436
Sparse Core Ops, SparseCore 0:
  72.6 17.8 all-reduce.3
  164.6 17.8 all-reduce.5
  260.4 17.8 all-reduce.7
where the time goes:
time: 350 us; the launch traced here: 348 us
  blocking collectives  164 us (47%)
  waiting for transfers between devices  84 us (24%)
  between operations  29.4 us (8%)
  other arithmetic  25.7 us (7%)
  local copies, waits for them, and re-layouts  18.8 us (5%)
  starting transfers between devices  16.9 us (5%)
  matrix products  9.9 us (3%)
    psum x3, blocking collectives, body(): sums = lax.psum(jnp.stack(pieces), ('sector', 'op')) / total  122 us
    psum x3, waiting for transfers between devices, body(): lax.psum(jnp.einsum('ksac,kscd->sad', inner, right_blocks, precision=high...  53.9 us
    psum x1, blocking collectives, body(): lax.psum(jnp.sum(jnp.square(portion(wave_start))), ('sector', 'op')) / total  42.2 us
    ppermute x3, waiting for transfers between devices, with_halo(): lax.ppermute(tail, axis, [(i, (i + 1) % count) for i in range(ends)])  24.5 us
    another operation x3, local copies, waits for them, and re-layouts, body(): sums = lax.psum(jnp.stack(pieces), ('sector', 'op')) / total  15.2 us
    ppermute x3, starting transfers between devices, with_halo(): lax.ppermute(tail, axis, [(i, (i + 1) % count) for i in range(ends)])  12.7 us
    div x3, other arithmetic, body(): ratio_basis = latest / preconditioner  7.41 us
  transfers between devices with their start and end apart: 9, of which 9 were waited for; matrix products, arithmetic and copies ran while one was open for 0% of the time, Pallas kernels for 0%

commit v1 on v0

v1 whole, which is shorter than its diff:
```python
import jax
import jax.numpy as jnp
from jax import lax
from jax.sharding import PartitionSpec as P

ITERS = 3


EPSILON = 1e-06

AXES = ("sector", "op")

LANES = 128


def total_sum(values):
    devices = lax.axis_size("sector") * lax.axis_size("op")
    row = jnp.pad(values, (0, LANES - values.shape[0]))
    rows = lax.all_to_all(jnp.broadcast_to(row, (devices, LANES)), AXES, 0, 0, tiled=True)
    return jnp.sum(rows, axis=0)[: values.shape[0]]


def coefficients(sums, total, count):
    sums = sums / total
    theta = sums[0]
    correlations = sums[4 : 4 + count] - theta * sums[4 + count : 4 + 2 * count]
    length = (
        sums[1]
        - 2.0 * theta * sums[2]
        + theta * theta * sums[3]
        - jnp.sum(jnp.square(correlations))
    )
    return theta, correlations, lax.rsqrt(length + EPSILON)


def products(members, image, inverse):
    latest = members[-1]
    ratio_image = image * inverse
    ratio_latest = latest * inverse
    pieces = [
        jnp.sum(latest * image),
        jnp.sum(ratio_image * ratio_image),
        jnp.sum(ratio_image * ratio_latest),
        jnp.sum(ratio_latest * ratio_latest),
    ]
    pieces = pieces + [jnp.sum(member * ratio_image) for member in members]
    pieces = pieces + [jnp.sum(member * ratio_latest) for member in members]
    return pieces


def one_sector_body(wave_start, left_blocks, right_blocks, term_shifts, preconditioner):
    highest = lax.Precision.HIGHEST
    op = lax.axis_index("op")
    chips = lax.axis_size("sector")
    devices = 2 * chips
    width = wave_start.shape[1]
    total = float(2 * chips * width * wave_start.shape[2])
    swap = [(i, i ^ 1) for i in range(devices)]
    across = [(i, i + 1) for i in range(1, devices - 1, 2)]
    across = across + [(j, i) for i, j in across]

    def mate(values):
        return lax.ppermute(values, AXES, swap)

    def facing(values):
        return lax.ppermute(values, AXES, across)

    def pick(values, index, axis):
        return lax.dynamic_index_in_dim(values, index, axis, keepdims=False)

    inverse = 1.0 / preconditioner
    own_wave, mate_wave = pick(wave_start, op, 0), pick(wave_start, 1 - op, 0)
    own_inverse, mate_inverse = pick(inverse, op, 0), pick(inverse, 1 - op, 0)
    facing_wave = facing(own_wave)
    facing_inverse = facing(own_inverse)
    left = jnp.concatenate([pick(left_blocks, op, 1), mate(pick(left_blocks, 1 - op, 1))])
    right = jnp.concatenate([pick(right_blocks, op, 1), mate(pick(right_blocks, 1 - op, 1))])
    shifts = jnp.concatenate([term_shifts, mate(term_shifts.astype(jnp.float32)).astype(jnp.int32)])
    toward_mate = jnp.where(op == 0, -1, 1)

    def operator(own, mates, facings):
        shift = shifts[:, None, None]
        source = jnp.where(
            shift == 0, own[None], jnp.where(shift == toward_mate, mates[None], facings[None])
        )
        inner = jnp.einsum("kab,kbc->kac", left, source, precision=highest)
        return jnp.einsum("kac,kcd->ad", inner, right, precision=highest)

    inverses = (own_inverse, mate_inverse, facing_inverse)
    waves = (own_wave, mate_wave, facing_wave)
    basis = []
    ritz = []
    latest = waves
    for index in range(ITERS):
        image = operator(*latest)
        mate_rows = image
        last = index + 1 == ITERS
        if last:
            half = width // 2
            mate_image = mate(lax.dynamic_slice_in_dim(image, (1 - op) * half, half, axis=0))
            images = (image, mate_image)
        else:
            images = (image, mate(image), facing(image))
        members = [member[0] for member in basis] if basis else [own_wave]
        pieces = products(members, image, own_inverse)
        if not basis:
            pieces = pieces + [jnp.sum(own_wave * own_wave)]
        sums = total_sum(jnp.stack(pieces))
        if not basis:
            factor = lax.rsqrt(sums[6] / total + EPSILON)
            square = factor * factor
            sums = sums[:6] * square
            basis.append(tuple(wave * factor for wave in waves))
            images = tuple(part * factor for part in images)
        theta, correlations, scale = coefficients(sums, total, len(basis))
        ritz.append(theta)

        def fresh(image, inverse, members):
            ortho = (image - theta * members[-1]) * inverse
            for position, member in enumerate(members):
                ortho = ortho - correlations[position] * member
            return ortho * scale

        if last:
            own_rows = lambda values: lax.dynamic_slice_in_dim(values, op * half, half, axis=0)
            basis.append(
                (
                    fresh(own_rows(image), own_rows(own_inverse), [own_rows(m[0]) for m in basis]),
                    fresh(mate_image, own_rows(mate_inverse), [own_rows(m[1]) for m in basis]),
                )
            )
        else:
            basis.append(
                tuple(
                    fresh(images[i], inverses[i], [member[i] for member in basis]) for i in range(3)
                )
            )
        latest = basis[-1]

    def placed(own, mates):
        return jnp.stack([jnp.where(op == 0, own, mates), jnp.where(op == 0, mates, own)])

    output = [placed(own_rows(m[0]), own_rows(m[1])) for m in basis[1:-1]] + [placed(*basis[-1])]
    return (jnp.stack(output), jnp.stack(ritz))


def with_halo(cells, sides, width):
    for axis, dim in sides:
        count = lax.axis_size(axis)
        ends = count - 1
        head = lax.slice_in_dim(cells, 0, width, axis=dim)
        tail = lax.slice_in_dim(cells, cells.shape[dim] - width, cells.shape[dim], axis=dim)
        cells = jnp.concatenate(
            [
                lax.ppermute(tail, axis, [(i, (i + 1) % count) for i in range(ends)]),
                cells,
                lax.ppermute(head, axis, [((i + 1) % count, i) for i in range(ends)]),
            ],
            axis=dim,
        )
    return cells


def split_terms_body(wave_start, left_blocks, right_blocks, term_shifts, preconditioner):
    highest = lax.Precision.HIGHEST
    width = wave_start.shape[1]
    row_count = width // lax.axis_size("op")
    first_row = lax.axis_index("op") * row_count
    total = float(wave_start.shape[0] * lax.axis_size("sector") * width * wave_start.shape[2])

    def portion(values):
        return lax.dynamic_slice_in_dim(values, first_row, row_count, axis=values.ndim - 2)

    start_sum = total_sum(jnp.sum(jnp.square(portion(wave_start)))[None])[0] / total
    basis = [wave_start * lax.rsqrt(start_sum + EPSILON)]
    ritz = []
    for _ in range(ITERS):
        latest = basis[-1]
        padded = with_halo(latest, (("sector", 0),), 1)
        shift = term_shifts[:, None, None, None]
        source = jnp.where(
            shift == 1,
            padded[None, :-2],
            jnp.where(shift == -1, padded[None, 2:], padded[None, 1:-1]),
        )
        inner = jnp.einsum("ksab,ksbc->ksac", left_blocks, source, precision=highest)
        image = lax.psum(jnp.einsum("ksac,kscd->sad", inner, right_blocks, precision=highest), "op")
        inverse = 1.0 / preconditioner
        pieces = products([portion(member) for member in basis], portion(image), portion(inverse))
        theta, correlations, scale = coefficients(
            total_sum(jnp.stack(pieces)), total, len(basis)
        )
        ortho = (image - theta * latest) * inverse
        for position, member in enumerate(basis):
            ortho = ortho - correlations[position] * member
        basis.append(ortho * scale)
        ritz.append(theta)
    output = jnp.stack([portion(member) for member in basis[1:]])
    return (output, jnp.stack(ritz))


def solution(mesh):
    placed = (
        P("sector", None, None),
        P("op", "sector", None, None),
        P("op", "sector", None, None),
        P("op"),
        P("sector", None, None),
    )

    def body(wave_start, *operands):
        one_each = mesh.shape["op"] == 2 and wave_start.shape[0] == 2
        return (one_sector_body if one_each else split_terms_body)(wave_start, *operands)

    return jax.shard_map(
        body,
        mesh=mesh,
        in_specs=placed,
        out_specs=(P(None, "sector", "op", None), P()),
        check_vma=False,
    )
```

time: 350 us -> 123 us (0.35)
  blocking collectives: 164 us -> 0 us
  waiting for transfers between devices: 84 us -> 14.3 us
  starting transfers between devices: 16.9 us -> 30.1 us
  between operations: 29.4 us -> 16.4 us
  local copies, waits for them, and re-layouts: 18.8 us -> 24.7 us
    psum x4 -> x0, blocking collectives: 164 us -> none  [the longest x3 122 us: body(): sums = lax.psum(jnp.stack(pieces), ('sector', 'op')) / total]
    psum x3 -> x0, waiting for transfers between devices: 53.9 us -> none  [body(): lax.psum(jnp.einsum('ksac,kscd->sad', inner, right_blocks, precision=high...]
    ppermute x6 -> x10, waiting for transfers between devices: 30.1 us -> 0.03 us  [the longest x6 0.02 us: mate(): return lax.ppermute(values, AXES, swap)]
    all_to_all x0 -> x3, starting transfers between devices: none -> 17.8 us  [total_sum(): lax.all_to_all(jnp.broadcast_to(row, (devices, LANES)), AXES, 0, 0, tiled...]
    mul x0 -> x6, other arithmetic: none -> 14.5 us  [the longest x5 11.7 us: fresh(): return ortho * scale]
    all_to_all x0 -> x3, waiting for transfers between devices: none -> 14.3 us  [total_sum(): lax.all_to_all(jnp.broadcast_to(row, (devices, LANES)), AXES, 0, 0, tiled...]
    div x9 -> x4, other arithmetic: 11 us -> 1.13 us  [the longest x1 1.11 us: one_sector_body(): inverse = 1.0 / preconditioner]
    ppermute x6 -> x10, starting transfers between devices: 16.8 us -> 12.3 us  [the longest x6 7.39 us: mate(): return lax.ppermute(values, AXES, swap)]
  transfers between devices with their start and end apart: 9 -> 13, of which waited for: 9 -> 3; matrix products, arithmetic and copies ran while one was open for 0% -> 18% of each run, Pallas kernels for 0% -> 0%
where the time goes in v1:
time: 123 us; the launch traced here: 122 us
  starting transfers between devices  30.1 us (24%)
  other arithmetic  29.1 us (24%)
  local copies, waits for them, and re-layouts  24.7 us (20%)
  between operations  16.4 us (13%)
  waiting for transfers between devices  14.3 us (12%)
  matrix products  7.65 us (6%)
    all_to_all x3, starting transfers between devices, total_sum(): lax.all_to_all(jnp.broadcast_to(row, (devices, LANES)), AXES, 0, 0, tiled...  17.8 us
    another operation x3, local copies, waits for them, and re-layouts, one_sector_body(): sums = total_sum(jnp.stack(pieces))  15.9 us
    all_to_all x3, waiting for transfers between devices, total_sum(): lax.all_to_all(jnp.broadcast_to(row, (devices, LANES)), AXES, 0, 0, tiled...  14.3 us
    mul x5, other arithmetic, fresh(): return ortho * scale  11.7 us
    ppermute x6, starting transfers between devices, mate(): return lax.ppermute(values, AXES, swap)  7.39 us
    ppermute x4, starting transfers between devices, facing(): return lax.ppermute(values, AXES, across)  4.92 us
    dot_general x3, matrix products, operator(): inner = jnp.einsum('kab,kbc->kac', left, source, precision=highest)  3.85 us
    dot_general x3, matrix products, operator(): return jnp.einsum('kac,kcd->ad', inner, right, precision=highest)  3.8 us
  transfers between devices with their start and end apart: 13, of which 3 were waited for; matrix products, arithmetic and copies ran while one was open for 18% of the time, Pallas kernels for 0%

profile of v1, /device:TPU:0, one launch (start us, length us, event | category | flops | bytes accessed | tf_op | source)
XLA Modules:
  0.0 122.3 jit_solution(11855004365490080429)
XLA Ops:
  0.6 2.2 %dynamic-slice_bitcast_fusion.3 = (f32[2,256,256]{2,1,0:T(8,128)S(1)}, f32[2,256,256]{2,1,0:T(8,128)}) fusion(f32[2,2,256,256]{3,2,1,0:T(8,128)} %param.6, s32[]{:T(128)S(6)} %select_n.91, s32[]{:T(128)S(6)} %select_n.92), kind=kLoop, calls=%fused_computation.27 | loop fusion | bytes 2097160 | tf_op jit(solution)/shard_map/jit(dynamic_index_in_dim)/squeeze | solution.py:69
  4.2 3.9 %collective-permute-start.1 = (f32[2]{0:T(128)S(1)}, f32[2]{0:T(128)S(1)}, u32[]{:S(2)}, u32[]{:S(2)}) collective-permute-start(f32[2]{0:T(128)S(1)} %convert_element_type.12), channel_id=1, source_target_pairs={{0,1},{1,0},{2,3},{3,2},{4,5},{5,4},{6,7},{7,6},{8,9},{9,8},{10,11... | collective-permute-start | bytes 32 | tf_op jit(solution)/shard_map/ppermute | solution.py:63
  9.0 1.1 broadcast_divide_fusion
  10.2 1.3 %fusion.6 = f32[4,256,256]{2,1,0:T(8,128)S(1)} fusion(f32[2,256,256]{2,1,0:T(8,128)S(1)} %collective-permute-done, f32[2,256,256]{2,1,0:T(8,128)S(1)} %get-tuple-element.45, f32[256,256]{1,0:T(8,128)S(1)} %collective-permute-done.2, f32[256,256]{1,0:T(8,128)S(1)} %get-tuple-element.54, f32[256,256]{1,0:T(8,128)S(1)} %get-tuple-element.55, ...), kind=kOutput, calls=%fused_computation.11 | convolution fusion | flops 806092800 | bytes 2883592 | tf_op jit(solution)/shard_map/kab,kbc->kac/dot_general | solution.py:86
  11.6 1.7 %convolution_bitcast_fusion.2 = f32[256,256]{1,0:T(8,128)} fusion(f32[4,256,256]{2,1,0:T(8,128)S(1)} %fusion.6, f32[2,256,256]{2,1,0:T(8,128)S(1)} %collective-permute-done.3, f32[2,256,256]{2,1,0:T(8,128)S(1)} %get-tuple-element.43), kind=kOutput, calls=%fused_computation.2 | convolution fusion | flops 805568512 | bytes 2359296 | tf_op jit(solution)/shard_map/kac,kcd->ad/dot_general | solution.py:87
  13.3 1.8 %multiply_reduce_fusion.19 = (f32[]{:T(128)}, f32[]{:T(128)}, f32[]{:T(128)}, f32[]{:T(128)}, f32[]{:T(128)}, /*index=5*/f32[]{:T(128)}, f32[]{:T(128)}, f32[256,256]{1,0:T(8,128)S(1)}) fusion(f32[256,256]{1,0:T(8,128)S(1)} %get-tuple-element.55, f32[256,256]{1,0:T(8,128)} %convolution_bitcast_fusion.2, f32[2,256,256]{2,1,0:T(8,128)S(1)} %broadcast_divide_fusion, ...), kind=kLoop, calls=%fused_computation.67 | loop fusion | flops 1048569 | bytes 1048608 | tf_op jit(solution)/shard_map/reduce_sum | solution.py:47
  15.1 4.4 %stack.133 = f32[7]{0:T(128)S(1)} concatenate(f32[1]{0:T(128)} %bitcast.7, f32[1]{0:T(128)} %bitcast.9, f32[1]{0:T(128)} %bitcast.10, f32[1]{0:T(128)} %bitcast.11, f32[1]{0:T(128)} %bitcast.12, f32[1]{0:T(128)} %bitcast.13, f32[1]{0:T(128)} %bitcast.14), dimensions={0} | concatenate | bytes 56 | tf_op jit(solution)/shard_map/stack | solution.py:108
  20.1 10.3 %all-to-all-start = ((f32[32,1,128]{2,1,0:T(1,128)}), f32[32,1,128]{2,1,0:T(1,128)S(1)}, u32[]{:S(2)}, u32[]{:S(2)}) async-start(f32[32,1,128]{2,1,0:T(1,128)} %broadcast_in_dim.114), calls=%async_computation | async-start | bytes 32768 | tf_op jit(solution)/shard_map/all_to_all | solution.py:19
  30.4 1.4 %collective-permute-start.5 = (f32[256,256]{1,0:T(8,128)}, f32[256,256]{1,0:T(8,128)}, u32[]{:S(2)}, u32[]{:S(2)}) collective-permute-start(f32[256,256]{1,0:T(8,128)} %convolution_bitcast_fusion.2), channel_id=1, source_target_pairs={{1,2},{3,4},{5,6},{7,8},{9,10},{11,12},{13,14},{15,16},{17,18},{19... | collective-permute-start | bytes 786440 | tf_op jit(solution)/shard_map/ppermute | solution.py:66
  31.8 2.5 %collective-permute-start.4 = (f32[256,256]{1,0:T(8,128)}, f32[256,256]{1,0:T(8,128)}, u32[]{:S(2)}, u32[]{:S(2)}) collective-permute-start(f32[256,256]{1,0:T(8,128)} %convolution_bitcast_fusion.2), channel_id=1, source_target_pairs={{0,1},{1,0},{2,3},{3,2},{4,5},{5,4},{6,7},{7,6},{8,9},{9,8},{10,11... | collective-permute-start | bytes 786440 | tf_op jit(solution)/shard_map/ppermute | solution.py:63
  34.2 1.4 %collective-permute-start.6 = (f32[256,256]{1,0:T(8,128)S(1)}, f32[256,256]{1,0:T(8,128)}, u32[]{:S(2)}, u32[]{:S(2)}) collective-permute-start(f32[256,256]{1,0:T(8,128)S(1)} %get-tuple-element.42), channel_id=1, source_target_pairs={{1,2},{3,4},{5,6},{7,8},{9,10},{11,12},{13,14},{15,16},{17,18},{19... | collective-permute-start | bytes 786440 | tf_op jit(solution)/shard_map/ppermute | solution.py:66
  35.6 1.9 %all-to-all-done = f32[32,1,128]{2,1,0:T(1,128)S(1)} async-done(((f32[32,1,128]{2,1,0:T(1,128)}), f32[32,1,128]{2,1,0:T(1,128)S(1)}, u32[]{:S(2)}, u32[]{:S(2)}) %all-to-all-start) | async-done | bytes 16416 | tf_op jit(solution)/shard_map/all_to_all | solution.py:19
  45.3 1.8 %subtract_multiply_fusion.3 = (f32[256,256]{1,0:T(8,128)S(1)}, f32[256,256]{1,0:T(8,128)S(1)}) fusion(f32[256,256]{1,0:T(8,128)S(1)} %get-tuple-element.42, f32[256,256]{1,0:T(8,128)} %convolution_bitcast_fusion.2, f32[]{:T(128)S(6)} %rsqrt.17, f32[]{:T(128)} %bitcast.18, f32[]{:T(128)} %bitcast.17, f32[]{:T(128)} %bitcast.16, f32[256,256]{1,0:T(8,128)} %copy-done), kind=kLoop, calls=%fused_computation.65 | loop fusion | flops 524288 | bytes 1310736 | tf_op jit(solution)/shard_map/mul | solution.py:122
  47.1 2.4 %fusion.25 = (f32[256,256]{1,0:T(8,128)S(1)}, f32[256,256]{1,0:T(8,128)}) fusion(f32[256,256]{1,0:T(8,128)} %collective-permute-done.4, f32[2,256,256]{2,1,0:T(8,128)S(1)} %broadcast_divide_fusion, s32[]{:T(128)S(6)} %select_n.92, f32[]{:T(128)S(6)} %rsqrt.17, f32[]{:T(128)} %bitcast.18, f32[]{:T(128)} %bitcast.17, f32[]{:T(128)} %bitcast.16, ...), kind=kLoop, calls=%fused_computation.40 | loop fusion | flops 524288 | bytes 1310740 | tf_op jit(solution)/shard_map/mul | solution.py:122
  49.5 1.7 %subtract_multiply_fusion.2 = f32[256,256]{1,0:T(8,128)S(1)} fusion(f32[256,256]{1,0:T(8,128)} %collective-permute-done.6, f32[256,256]{1,0:T(8,128)} %collective-permute-done.5, f32[256,256]{1,0:T(8,128)S(1)} %copy-done.8, f32[]{:T(128)S(6)} %rsqrt.17, f32[]{:T(128)} %bitcast.18, f32[]{:T(128)} %bitcast.17, f32[]{:T(128)} %bitcast.16), kind=kLoop, calls=%fused_computation.64 | loop fusion | flops 524288 | bytes 1048592 | tf_op jit(solution)/shard_map/mul | solution.py:122
  51.2 1.3 %fusion.3 = f32[4,256,256]{2,1,0:T(8,128)S(1)} fusion(f32[2,256,256]{2,1,0:T(8,128)S(1)} %collective-permute-done, f32[2,256,256]{2,1,0:T(8,128)S(1)} %get-tuple-element.45, f32[256,256]{1,0:T(8,128)S(1)} %subtract_multiply_fusion.2, f32[256,256]{1,0:T(8,128)S(1)} %get-tuple-element.40, f32[256,256]{1,0:T(8,128)S(1)} %get-tuple-element.38, ...), kind=kOutput, calls=%fused_computation.8 | convolution fusion | flops 806092800 | bytes 2883592 | tf_op jit(solution)/shard_map/kab,kbc->kac/dot_general | solution.py:86
  52.5 1.0 fusion.51
  54.4 5.1 %stack.146 = f32[8]{0:T(128)S(1)} concatenate(f32[1]{0:T(128)} %bitcast.28, f32[1]{0:T(128)} %bitcast.29, f32[1]{0:T(128)} %bitcast.30, f32[1]{0:T(128)} %bitcast.31, f32[1]{0:T(128)} %bitcast.32, f32[1]{0:T(128)} %bitcast.33, f32[1]{0:T(128)} %bitcast.34, f32[1]{0:T(128)} %bitcast.35), dimensions={0} | concatenate | bytes 64 | tf_op jit(solution)/shard_map/stack | solution.py:108
  60.2 4.9 %all-to-all-start.1 = ((f32[32,1,128]{2,1,0:T(1,128)}), f32[32,1,128]{2,1,0:T(1,128)S(1)}, u32[]{:S(2)}, u32[]{:S(2)}) async-start(f32[32,1,128]{2,1,0:T(1,128)} %broadcast_in_dim.118), calls=%async_computation.1 | async-start | bytes 32768 | tf_op jit(solution)/shard_map/all_to_all | solution.py:19
  65.4 1.4 %collective-permute-start.8 = (f32[256,256]{1,0:T(8,128)}, f32[256,256]{1,0:T(8,128)}, u32[]{:S(2)}, u32[]{:S(2)}) collective-permute-start(f32[256,256]{1,0:T(8,128)} %copy-done.12), channel_id=1, source_target_pairs={{1,2},{3,4},{5,6},{7,8},{9,10},{11,12},{13,14},{15,16},{17,18},{19... | collective-permute-start | bytes 786440 | tf_op jit(solution)/shard_map/ppermute | solution.py:66
  66.8 5.4 %all-to-all-done.1 = f32[32,1,128]{2,1,0:T(1,128)S(1)} async-done(((f32[32,1,128]{2,1,0:T(1,128)}), f32[32,1,128]{2,1,0:T(1,128)S(1)}, u32[]{:S(2)}, u32[]{:S(2)}) %all-to-all-start.1) | async-done | bytes 16416 | tf_op jit(solution)/shard_map/all_to_all | solution.py:19
  73.0 1.3 %multiply_reduce_fusion.26 = (f32[]{:T(128)}, f32[2]{0:T(128)S(1)}) fusion(f32[8]{0:T(128)S(1)} %slice_multiply_fusion.1, f32[]{:T(128)} %bitcast.37), kind=kLoop, calls=%fused_computation.101 | loop fusion | flops 7 | bytes 32 | tf_op jit(solution)/shard_map/reduce_sum | solution.py:31
  79.2 2.9 %fusion.45 = (f32[256,256]{1,0:T(8,128)S(1)}, f32[256,256]{1,0:T(8,128)S(1)}) fusion(f32[256,256]{1,0:T(8,128)S(1)} %get-tuple-element.42, f32[]{:T(128)S(6)} %rsqrt.18, f32[256,256]{1,0:T(8,128)S(1)} %get-tuple-element.38, f32[]{:T(128)} %bitcast.39, f32[256,256]{1,0:T(8,128)S(1)} %get-tuple-element.39, f32[]{:T(128)} %bitcast.38, ...), kind=kLoop, calls=%fused_computation.113 | loop fusion | flops 589824 | bytes 1572880 | tf_op jit(solution)/shard_map/mul | solution.py:39
  82.2 3.0 %subtract_multiply_fusion = f32[256,256]{1,0:T(8,128)S(1)} fusion(f32[256,256]{1,0:T(8,128)S(1)} %copy-done.11, f32[256,256]{1,0:T(8,128)} %collective-permute-done.6, f32[256,256]{1,0:T(8,128)} %collective-permute-done.8, f32[256,256]{1,0:T(8,128)S(1)} %copy-done.9, f32[]{:T(128)S(6)} %rsqrt.18, f32[]{:T(128)} %bitcast.39, f32[]{:T(128)} %bitcast.38, ...), kind=kLoop, calls=%fused_computation.54 | loop fusion | flops 589824 | bytes 1310740 | tf_op jit(solution)/shard_map/mul | solution.py:122
  85.2 2.8 %fusion.28 = f32[256,256]{1,0:T(8,128)S(1)} fusion(f32[256,256]{1,0:T(8,128)S(1)} %copy-done.2, f32[256,256]{1,0:T(8,128)S(1)} %copy-done.13, f32[256,256]{1,0:T(8,128)} %collective-permute-done.7, f32[2,256,256]{2,1,0:T(8,128)S(1)} %broadcast_divide_fusion, s32[]{:T(128)S(6)} %select_n.92, f32[]{:T(128)S(6)} %rsqrt.18, f32[]{:T(128)} %bitcast.39, ...), kind=kLoop, calls=%fused_computation.43 | loop fusion | flops 524288 | bytes 1310740 | tf_op jit(solution)/shard_map/mul | solution.py:122
  88.0 1.3 %fusion = f32[4,256,256]{2,1,0:T(8,128)S(1)} fusion(f32[2,256,256]{2,1,0:T(8,128)S(1)} %collective-permute-done, f32[2,256,256]{2,1,0:T(8,128)S(1)} %get-tuple-element.45, f32[256,256]{1,0:T(8,128)S(1)} %subtract_multiply_fusion, f32[256,256]{1,0:T(8,128)S(1)} %fusion.28, f32[256,256]{1,0:T(8,128)S(1)} %get-tuple-element.35, ...), kind=kOutput, calls=%fused_computation.5 | convolution fusion | flops 806092800 | bytes 2883592 | tf_op jit(solution)/shard_map/kab,kbc->kac/dot_general | solution.py:86
  91.3 6.4 %stack.161 = f32[10]{0:T(128)S(1)} concatenate(f32[1]{0:T(128)} %bitcast.47, f32[1]{0:T(128)} %bitcast.48, f32[1]{0:T(128)} %bitcast.49, f32[1]{0:T(128)} %bitcast.50, f32[1]{0:T(128)} %bitcast.51, f32[1]{0:T(128)} %bitcast.52, f32[1]{0:T(128)} %bitcast.53, f32[1]{0:T(128)} %bitcast.54, f32[1]{0:T(128)} %bitcast.55, f32[1]{0:T(128)} %bitcast.56), dimensions={0} | concatenate | bytes 80 | tf_op jit(solution)/shard_map/stack | solution.py:108
  98.3 2.6 %all-to-all-start.2 = ((f32[32,1,128]{2,1,0:T(1,128)}), f32[32,1,128]{2,1,0:T(1,128)S(1)}, u32[]{:S(2)}, u32[]{:S(2)}) async-start(f32[32,1,128]{2,1,0:T(1,128)} %broadcast_in_dim.122), calls=%async_computation.2 | async-start | bytes 32768 | tf_op jit(solution)/shard_map/all_to_all | solution.py:19
  101.0 6.9 %all-to-all-done.2 = f32[32,1,128]{2,1,0:T(1,128)S(1)} async-done(((f32[32,1,128]{2,1,0:T(1,128)}), f32[32,1,128]{2,1,0:T(1,128)S(1)}, u32[]{:S(2)}, u32[]{:S(2)}) %all-to-all-start.2) | async-done | bytes 16416 | tf_op jit(solution)/shard_map/all_to_all | solution.py:19
  108.7 1.4 %multiply_reduce_fusion.25 = (f32[]{:T(128)}, f32[3]{0:T(128)S(1)}) fusion(f32[10]{0:T(128)S(1)} %slice_multiply_fusion, f32[]{:T(128)} %bitcast.58), kind=kLoop, calls=%fused_computation.98 | loop fusion | flops 11 | bytes 44 | tf_op jit(solution)/shard_map/reduce_sum | solution.py:31
  110.0 2.5 %pad_maximum_fusion.9 = f32[3]{0:T(128)} fusion(f32[1]{0:T(128)} %get-tuple-element.64, f32[1]{0:T(128)} %get-tuple-element.70, f32[1]{0:T(128)} %get-tuple-element.76), kind=kLoop, calls=%fused_computation.97 | loop fusion | flops 6 | bytes 24 | tf_op jit(solution)/shard_map/stack | solution.py:144
  117.7 3.5 %select_bitcast_fusion.5 = (f32[1,128,256]{2,1,0:T(8,128)S(1)}, f32[1,128,256]{2,1,0:T(8,128)S(1)}, f32[1,128,256]{2,1,0:T(8,128)S(1)}, f32[128,256]{1,0:T(8,128...) fusion(f32[256,256]{1,0:T(8,128)S(1)} %copy-done.3, s32[]{:T(128)S(6)} %select_n.96, ...), kind=kLoop, calls=%fused_computation.92 | loop fusion | flops 819200 | bytes 2228261 | tf_op jit(solution)/shard_map/stack | solution.py:141
  (86 shorter events, 12.5 us)
Async XLA Ops:
  0.6 2.6 %copy-start.18 = (f32[2,256,256]{2,1,0:T(8,128)S(1)}, f32[2,256,256]{2,1,0:T(8,128)}, u32[]{:S(2)}) copy-start(f32[2,256,256]{2,1,0:T(8,128)} %param.5) | copy-start | bytes 1572868
  2.8 5.3 %copy-start.17 = (f32[2,2,256,256]{3,2,1,0:T(8,128)S(1)}, f32[2,2,256,256]{3,2,1,0:T(8,128)}, u32[]{:S(2)}) copy-start(f32[2,2,256,256]{3,2,1,0:T(8,128)} %param.7) | copy-start | bytes 3145732
  2.8 7.4 %collective-permute-start = (f32[2,256,256]{2,1,0:T(8,128)}, f32[2,256,256]{2,1,0:T(8,128)S(1)}, u32[]{:S(2)}, u32[]{:S(2)}) collective-permute-start(f32[2,256,256]{2,1,0:T(8,128)} %get-tuple-element.46), channel_id=1, source_target_pairs={{0,1},{1,0},{2,3},{3,2},{4,5},{5,4},{6,7},{7,6},{8,9},{9,8},{10,11... | collective-permute-start | bytes 1572872 | tf_op jit(solution)/shard_map/ppermute | solution.py:63
  3.3 6.9 %copy-start.5 = (f32[256,256]{1,0:T(8,128)}, f32[256,256]{1,0:T(8,128)S(1)}, u32[]{:S(2)}) copy-start(f32[256,256]{1,0:T(8,128)S(1)} %get-tuple-element.54) | copy-start | bytes 786436
  3.3 10.0 %copy-start = (f32[256,256]{1,0:T(8,128)}, f32[256,256]{1,0:T(8,128)S(1)}, u32[]{:S(2)}) copy-start(f32[256,256]{1,0:T(8,128)S(1)} %get-tuple-element.55) | copy-start | bytes 786436
  3.3 6.9 %collective-permute-start.2 = (f32[256,256]{1,0:T(8,128)S(1)}, f32[256,256]{1,0:T(8,128)S(1)}, u32[]{:S(2)}, u32[]{:S(2)}) collective-permute-start(f32[256,256]{1,0:T(8,128)S(1)} %get-tuple-element.55), channel_id=1, source_target_pairs={{1,2},{3,4},{5,6},{7,8},{9,10},{11,12},{13,14},{15,16},{17,18},{19... | collective-permute-start | bytes 786440 | tf_op jit(solution)/shard_map/ppermute | solution.py:66
  4.2 6.0 %collective-permute-start.1 = (f32[2]{0:T(128)S(1)}, f32[2]{0:T(128)S(1)}, u32[]{:S(2)}, u32[]{:S(2)}) collective-permute-start(f32[2]{0:T(128)S(1)} %convert_element_type.12), channel_id=1, source_target_pairs={{0,1},{1,0},{2,3},{3,2},{4,5},{5,4},{6,7},{7,6},{8,9},{9,8},{10,11... | collective-permute-start | bytes 32 | tf_op jit(solution)/shard_map/ppermute | solution.py:63
  9.0 2.6 %collective-permute-start.3 = (f32[2,256,256]{2,1,0:T(8,128)}, f32[2,256,256]{2,1,0:T(8,128)S(1)}, u32[]{:S(2)}, u32[]{:S(2)}) collective-permute-start(f32[2,256,256]{2,1,0:T(8,128)} %get-tuple-element.44), channel_id=1, source_target_pairs={{0,1},{1,0},{2,3},{3,2},{4,5},{5,4},{6,7},{7,6},{8,9},{9,8},{10,11... | collective-permute-start | bytes 1572872 | tf_op jit(solution)/shard_map/ppermute | solution.py:63
  10.2 1.3 %copy-start.7 = (f32[256,256]{1,0:T(8,128)}, f32[256,256]{1,0:T(8,128)S(1)}, u32[]{:S(2)}) copy-start(f32[256,256]{1,0:T(8,128)S(1)} %collective-permute-done.2) | copy-start | bytes 786436
  20.1 17.4 %all-to-all-start = ((f32[32,1,128]{2,1,0:T(1,128)}), f32[32,1,128]{2,1,0:T(1,128)S(1)}, u32[]{:S(2)}, u32[]{:S(2)}) async-start(f32[32,1,128]{2,1,0:T(1,128)} %broadcast_in_dim.114), calls=%async_computation | async-start | bytes 32768 | tf_op jit(solution)/shard_map/all_to_all | solution.py:19
  30.4 19.1 %collective-permute-start.5 = (f32[256,256]{1,0:T(8,128)}, f32[256,256]{1,0:T(8,128)}, u32[]{:S(2)}, u32[]{:S(2)}) collective-permute-start(f32[256,256]{1,0:T(8,128)} %convolution_bitcast_fusion.2), channel_id=1, source_target_pairs={{1,2},{3,4},{5,6},{7,8},{9,10},{11,12},{13,14},{15,16},{17,18},{19... | collective-permute-start | bytes 786440 | tf_op jit(solution)/shard_map/ppermute | solution.py:66
  31.8 15.3 %collective-permute-start.4 = (f32[256,256]{1,0:T(8,128)}, f32[256,256]{1,0:T(8,128)}, u32[]{:S(2)}, u32[]{:S(2)}) collective-permute-start(f32[256,256]{1,0:T(8,128)} %convolution_bitcast_fusion.2), channel_id=1, source_target_pairs={{0,1},{1,0},{2,3},{3,2},{4,5},{5,4},{6,7},{7,6},{8,9},{9,8},{10,11... | collective-permute-start | bytes 786440 | tf_op jit(solution)/shard_map/ppermute | solution.py:63
  34.2 15.2 %collective-permute-start.6 = (f32[256,256]{1,0:T(8,128)S(1)}, f32[256,256]{1,0:T(8,128)}, u32[]{:S(2)}, u32[]{:S(2)}) collective-permute-start(f32[256,256]{1,0:T(8,128)S(1)} %get-tuple-element.42), channel_id=1, source_target_pairs={{1,2},{3,4},{5,6},{7,8},{9,10},{11,12},{13,14},{15,16},{17,18},{19... | collective-permute-start | bytes 786440 | tf_op jit(solution)/shard_map/ppermute | solution.py:66
  45.3 1.8 %copy-start.6 = (f32[256,256]{1,0:T(8,128)S(1)}, f32[256,256]{1,0:T(8,128)}, u32[]{:S(2)}) copy-start(f32[256,256]{1,0:T(8,128)} %copy-done.5) | copy-start | bytes 786436
  47.1 2.4 %copy-start.8 = (f32[256,256]{1,0:T(8,128)S(1)}, f32[256,256]{1,0:T(8,128)}, u32[]{:S(2)}) copy-start(f32[256,256]{1,0:T(8,128)} %copy-done.7) | copy-start | bytes 786436
  49.5 1.8 %copy-start.1 = (f32[256,256]{1,0:T(8,128)}, f32[256,256]{1,0:T(8,128)S(1)}, u32[]{:S(2)}) copy-start(f32[256,256]{1,0:T(8,128)S(1)} %get-tuple-element.40) | copy-start | bytes 786436
  51.2 1.3 %copy-start.10 = (f32[256,256]{1,0:T(8,128)}, f32[256,256]{1,0:T(8,128)S(1)}, u32[]{:S(2)}) copy-start(f32[256,256]{1,0:T(8,128)S(1)} %subtract_multiply_fusion.2) | copy-start | bytes 786436
  53.6 0.9 copy-start.12
  60.2 12.1 %all-to-all-start.1 = ((f32[32,1,128]{2,1,0:T(1,128)}), f32[32,1,128]{2,1,0:T(1,128)S(1)}, u32[]{:S(2)}, u32[]{:S(2)}) async-start(f32[32,1,128]{2,1,0:T(1,128)} %broadcast_in_dim.118), calls=%async_computation.1 | async-start | bytes 32768 | tf_op jit(solution)/shard_map/all_to_all | solution.py:19
  65.1 20.0 %collective-permute-start.7 = (f32[256,256]{1,0:T(8,128)}, f32[256,256]{1,0:T(8,128)}, u32[]{:S(2)}, u32[]{:S(2)}) collective-permute-start(f32[256,256]{1,0:T(8,128)} %copy-done.12), channel_id=1, source_target_pairs={{0,1},{1,0},{2,3},{3,2},{4,5},{5,4},{6,7},{7,6},{8,9},{9,8},{10,11... | collective-permute-start | bytes 786440 | tf_op jit(solution)/shard_map/ppermute | solution.py:63
  65.4 16.7 %collective-permute-start.8 = (f32[256,256]{1,0:T(8,128)}, f32[256,256]{1,0:T(8,128)}, u32[]{:S(2)}, u32[]{:S(2)}) collective-permute-start(f32[256,256]{1,0:T(8,128)} %copy-done.12), channel_id=1, source_target_pairs={{1,2},{3,4},{5,6},{7,8},{9,10},{11,12},{13,14},{15,16},{17,18},{19... | collective-permute-start | bytes 786440 | tf_op jit(solution)/shard_map/ppermute | solution.py:66
  79.2 2.9 %copy-start.9 = (f32[256,256]{1,0:T(8,128)S(1)}, f32[256,256]{1,0:T(8,128)}, u32[]{:S(2)}) copy-start(f32[256,256]{1,0:T(8,128)} %copy-done.7) | copy-start | bytes 786436
  79.2 2.9 %copy-start.11 = (f32[256,256]{1,0:T(8,128)S(1)}, f32[256,256]{1,0:T(8,128)}, u32[]{:S(2)}) copy-start(f32[256,256]{1,0:T(8,128)} %copy-done.10) | copy-start | bytes 786436
  82.1 8.2 %copy-start.4 = (f32[256,256]{1,0:T(8,128)}, f32[256,256]{1,0:T(8,128)S(1)}, u32[]{:S(2)}) copy-start(f32[256,256]{1,0:T(8,128)S(1)} %get-tuple-element.35) | copy-start | bytes 786436
  82.1 3.1 %copy-start.2 = (f32[256,256]{1,0:T(8,128)S(1)}, f32[256,256]{1,0:T(8,128)}, u32[]{:S(2)}) copy-start(f32[256,256]{1,0:T(8,128)} %copy-done.1) | copy-start | bytes 786436
  82.1 3.1 %copy-start.13 = (f32[256,256]{1,0:T(8,128)S(1)}, f32[256,256]{1,0:T(8,128)}, u32[]{:S(2)}) copy-start(f32[256,256]{1,0:T(8,128)} %get-tuple-element.41) | copy-start | bytes 786436
  88.0 1.3 %copy-start.15 = (f32[256,256]{1,0:T(8,128)}, f32[256,256]{1,0:T(8,128)S(1)}, u32[]{:S(2)}) copy-start(f32[256,256]{1,0:T(8,128)S(1)} %fusion.28) | copy-start | bytes 786436
  90.3 27.3 %copy-start.14 = (f32[256,256]{1,0:T(8,128)S(1)}, f32[256,256]{1,0:T(8,128)}, u32[]{:S(2)}) copy-start(f32[256,256]{1,0:T(8,128)} %get-tuple-element.41) | copy-start | bytes 786436
  90.4 27.3 %copy-start.16 = (f32[256,256]{1,0:T(8,128)S(1)}, f32[256,256]{1,0:T(8,128)}, u32[]{:S(2)}) copy-start(f32[256,256]{1,0:T(8,128)} %copy-done.15) | copy-start | bytes 786436
  91.3 26.4 %copy-start.3 = (f32[256,256]{1,0:T(8,128)S(1)}, f32[256,256]{1,0:T(8,128)}, u32[]{:S(2)}) copy-start(f32[256,256]{1,0:T(8,128)} %copy-done.1) | copy-start | bytes 786436
  98.3 9.7 %all-to-all-start.2 = ((f32[32,1,128]{2,1,0:T(1,128)}), f32[32,1,128]{2,1,0:T(1,128)S(1)}, u32[]{:S(2)}, u32[]{:S(2)}) async-start(f32[32,1,128]{2,1,0:T(1,128)} %broadcast_in_dim.122), calls=%async_computation.2 | async-start | bytes 32768 | tf_op jit(solution)/shard_map/all_to_all | solution.py:19
  100.9 16.8 %collective-permute-start.9 = (f32[128,256]{1,0:T(8,128)S(1)}, f32[128,256]{1,0:T(8,128)S(1)}, u32[]{:S(2)}, u32[]{:S(2)}) collective-permute-start(f32[128,256]{1,0:T(8,128)S(1)} %constant_dynamic-slice_fusion), channel_id=1, source_target_pairs={{0,1},{1,0},{2,3},{3,2},{4,5},{5,4},{6,7},{7,6},{8,9},{9,8},{10,11... | collective-permute-start | bytes 393224 | tf_op jit(solution)/shard_map/ppermute | solution.py:63
  (1 other events, 0.8 us)

commit v2 on v1

--- a/solution.py
+++ b/solution.py
@@ -1,6 +1,10 @@
+import functools
+
 import jax
 import jax.numpy as jnp
 from jax import lax
+from jax.experimental import pallas as pl
+from jax.experimental.pallas import tpu as pltpu
 from jax.sharding import PartitionSpec as P
 
 ITERS = 3
@@ -48,13 +52,187 @@
     return pieces
 
 
+def split(values):
+    high = values.astype(jnp.bfloat16)
+    return high, (values - high.astype(jnp.float32)).astype(jnp.bfloat16)
+
+
+def dot_split(lhs_high, lhs_low, rhs_high, rhs_low):
+    dot = functools.partial(jnp.dot, preferred_element_type=jnp.float32)
+    return dot(lhs_high, rhs_high) + (dot(lhs_low, rhs_high) + dot(lhs_high, rhs_low))
+
+
+def apply_terms(sources, vectors, left, right):
+    left_high, left_low = left
+    right_high, right_low = right
+    vector_high, vector_low = vectors
+    image = None
+    for term, source in enumerate(sources):
+        inner = dot_split(left_high[term], left_low[term], vector_high[source], vector_low[source])
+        part = dot_split(*split(inner), right_high[term], right_low[term])
+        image = part if image is None else image + part
+    return image
+
+
+def term_sources(own_shifts, mate_shifts):
+    toward_mate = jnp.where(lax.axis_index("op") == 0, -1, 1)
+    shifts = [refs[i] for refs in (own_shifts, mate_shifts) for i in range(refs.shape[0])]
+    return [
+        jnp.where(shift == 0, 0, jnp.where(shift == toward_mate, 1, 2)) for shift in shifts
+    ]
+
+
+def row_of_sums(factors, devices):
+    lane = lax.broadcasted_iota(jnp.int32, (1, LANES), 1)
+    row = jnp.zeros((1, LANES), jnp.float32)
+    for position, (one, other) in enumerate(factors):
+        product = (one * other).reshape(-1, 8, one.shape[1])
+        whole = jnp.sum(jnp.sum(product, axis=0), axis=(0, 1), keepdims=True)
+        row = jnp.where(lane == position, whole, row)
+    return jnp.broadcast_to(row, (devices, LANES))
+
+
+def factors_of(members, image, inverse):
+    latest = members[-1]
+    ratio_image = image * inverse
+    ratio_latest = latest * inverse
+    factors = [
+        (latest, image),
+        (ratio_image, ratio_image),
+        (ratio_image, ratio_latest),
+        (ratio_latest, ratio_latest),
+    ]
+    factors = factors + [(member, ratio_image) for member in members]
+    return factors + [(member, ratio_latest) for member in members]
+
+
+def summed(rows, total):
+    whole = jnp.sum(rows[...], axis=0, keepdims=True) / total
+    return [whole[:, i : i + 1] for i in range(10)]
+
+
+def step_factors(sums, count):
+    theta = sums[0]
+    correlations = [sums[4 + i] - theta * sums[4 + count + i] for i in range(count)]
+    length = sums[1] - 2.0 * theta * sums[2] + theta * theta * sums[3]
+    for correlation in correlations:
+        length = length - correlation * correlation
+    return theta, correlations, lax.rsqrt(length + EPSILON)
+
+
+def fresh(step, image, inverse, members):
+    theta, correlations, scale = step
+    ortho = (image - theta * members[-1]) * inverse
+    for correlation, member in zip(correlations, members):
+        ortho = ortho - correlation * member
+    return ortho * scale
+
+
+def start_factors(sums):
+    factor = lax.rsqrt(sums[6] + EPSILON)
+    return factor, [value * (factor * factor) for value in sums[:6]]
+
+
+def inverted(values):
+    return jnp.where(values > 0.0, 1.0 / values, 0.0)
+
+
+def first_kernel(
+    own_shifts, mate_shifts, wave, facing_wave, preconditioner, own_left, mate_left, own_right,
+    mate_right, image_ref, row_ref, left_high, left_low, right_high, right_low, high, low,
+):
+    op = lax.axis_index("op")
+    sources = term_sources(own_shifts, mate_shifts)
+    for place, values in enumerate((wave[op], wave[1 - op], facing_wave[...])):
+        high[place], low[place] = split(values)
+    count = own_left.shape[0]
+    for half, (left, right) in enumerate(((own_left, own_right), (mate_left, mate_right))):
+        for term in range(count):
+            place = half * count + term
+            left_high[place], left_low[place] = split(left[term, op])
+            right_high[place], right_low[place] = split(right[term, op])
+    image = apply_terms(sources, (high, low), (left_high, left_low), (right_high, right_low))
+    image_ref[...] = image
+    own = wave[op]
+    factors = factors_of([own], image, inverted(preconditioner[op])) + [(own, own)]
+    row_ref[...] = row_of_sums(factors, row_ref.shape[0])
+
+
+def second_kernel(
+    total, own_shifts, mate_shifts, rows, wave, facing_wave, preconditioner, facing_preconditioner,
+    own_image, mate_image, facing_image, left_high, left_low, right_high, right_low,
+    image_ref, row_ref, start_ref, first_ref, inverse_ref, theta_ref, high, low,
+):
+    op = lax.axis_index("op")
+    sources = term_sources(own_shifts, mate_shifts)
+    factor, sums = start_factors(summed(rows, total))
+    step = step_factors(sums, 1)
+    theta_ref[...] = jnp.broadcast_to(step[0], theta_ref.shape)
+    waves = (wave[op], wave[1 - op], facing_wave[...])
+    divisors = (preconditioner[op], preconditioner[1 - op], facing_preconditioner[...])
+    images = (own_image, mate_image, facing_image)
+    for place in range(3):
+        start = waves[place] * factor
+        inverse = inverted(divisors[place])
+        first = fresh(step, images[place][...] * factor, inverse, [start])
+        start_ref[place] = start
+        inverse_ref[place] = inverse
+        first_ref[place] = first
+        high[place], low[place] = split(first)
+    image = apply_terms(sources, (high, low), (left_high, left_low), (right_high, right_low))
+    image_ref[...] = image
+    factors = factors_of([start_ref[0], first_ref[0]], image, inverse_ref[0])
+    row_ref[...] = row_of_sums(factors, row_ref.shape[0])
+
+
+def third_kernel(
+    total, own_shifts, mate_shifts, rows, start, first, inverse,
+    own_image, mate_image, facing_image, left_high, left_low, right_high, right_low,
+    kept_ref, sent_ref, row_ref, second_ref, theta_ref, high, low,
+):
+    op = lax.axis_index("op")
+    sources = term_sources(own_shifts, mate_shifts)
+    step = step_factors(summed(rows, total), 2)
+    theta_ref[...] = jnp.broadcast_to(step[0], theta_ref.shape)
+    images = (own_image, mate_image, facing_image)
+    for place in range(3):
+        second = fresh(step, images[place][...], inverse[place], [start[place], first[place]])
+        if place < 2:
+            second_ref[place] = second
+        high[place], low[place] = split(second)
+    image = apply_terms(sources, (high, low), (left_high, left_low), (right_high, right_low))
+    half = kept_ref.shape[0]
+    kept_ref[...] = jnp.where(op == 0, image[:half], image[half:])
+    sent_ref[...] = jnp.where(op == 0, image[half:], image[:half])
+    factors = factors_of([start[0], first[0], second_ref[0]], image, inverse[0])
+    row_ref[...] = row_of_sums(factors, row_ref.shape[0])
+
+
+def last_kernel(
+    total, rows, first_theta, second_theta, start, first, second, inverse, own_image, mate_image,
+    basis_ref, ritz_ref,
+):
+    op = lax.axis_index("op")
+    step = step_factors(summed(rows, total), 3)
+    half = own_image.shape[0]
+    mine = pl.ds(pl.multiple_of(op * half, half), half)
+    for place, (image, sector) in enumerate(((own_image, op), (mate_image, 1 - op))):
+        members = [member[place, mine] for member in (start, first, second)]
+        basis_ref[0, sector] = members[1]
+        basis_ref[1, sector] = members[2]
+        basis_ref[2, sector] = fresh(step, image[...], inverse[place, mine], members)
+    for position, theta in enumerate((first_theta[...], second_theta[...], step[0])):
+        ritz_ref[position] = theta[0, 0]
+
+
 def one_sector_body(wave_start, left_blocks, right_blocks, term_shifts, preconditioner):
-    highest = lax.Precision.HIGHEST
     op = lax.axis_index("op")
     chips = lax.axis_size("sector")
     devices = 2 * chips
-    width = wave_start.shape[1]
-    total = float(2 * chips * width * wave_start.shape[2])
+    rows, columns = wave_start.shape[1:]
+    half = rows // 2
+    terms = 2 * left_blocks.shape[0]
+    total = float(devices * rows * columns)
     swap = [(i, i ^ 1) for i in range(devices)]
     across = [(i, i + 1) for i in range(1, devices - 1, 2)]
     across = across + [(j, i) for i, j in across]
@@ -65,83 +243,69 @@
     def facing(values):
         return lax.ppermute(values, AXES, across)
 
-    def pick(values, index, axis):
-        return lax.dynamic_index_in_dim(values, index, axis, keepdims=False)
-
-    inverse = 1.0 / preconditioner
-    own_wave, mate_wave = pick(wave_start, op, 0), pick(wave_start, 1 - op, 0)
-    own_inverse, mate_inverse = pick(inverse, op, 0), pick(inverse, 1 - op, 0)
-    facing_wave = facing(own_wave)
-    facing_inverse = facing(own_inverse)
-    left = jnp.concatenate([pick(left_blocks, op, 1), mate(pick(left_blocks, 1 - op, 1))])
-    right = jnp.concatenate([pick(right_blocks, op, 1), mate(pick(right_blocks, 1 - op, 1))])
-    shifts = jnp.concatenate([term_shifts, mate(term_shifts.astype(jnp.float32)).astype(jnp.int32)])
-    toward_mate = jnp.where(op == 0, -1, 1)
-
-    def operator(own, mates, facings):
-        shift = shifts[:, None, None]
-        source = jnp.where(
-            shift == 0, own[None], jnp.where(shift == toward_mate, mates[None], facings[None])
-        )
-        inner = jnp.einsum("kab,kbc->kac", left, source, precision=highest)
-        return jnp.einsum("kac,kcd->ad", inner, right, precision=highest)
-
-    inverses = (own_inverse, mate_inverse, facing_inverse)
-    waves = (own_wave, mate_wave, facing_wave)
-    basis = []
-    ritz = []
-    latest = waves
-    for index in range(ITERS):
-        image = operator(*latest)
-        mate_rows = image
-        last = index + 1 == ITERS
-        if last:
-            half = width // 2
-            mate_image = mate(lax.dynamic_slice_in_dim(image, (1 - op) * half, half, axis=0))
-            images = (image, mate_image)
-        else:
-            images = (image, mate(image), facing(image))
-        members = [member[0] for member in basis] if basis else [own_wave]
-        pieces = products(members, image, own_inverse)
-        if not basis:
-            pieces = pieces + [jnp.sum(own_wave * own_wave)]
-        sums = total_sum(jnp.stack(pieces))
-        if not basis:
-            factor = lax.rsqrt(sums[6] / total + EPSILON)
-            square = factor * factor
-            sums = sums[:6] * square
-            basis.append(tuple(wave * factor for wave in waves))
-            images = tuple(part * factor for part in images)
-        theta, correlations, scale = coefficients(sums, total, len(basis))
-        ritz.append(theta)
-
-        def fresh(image, inverse, members):
-            ortho = (image - theta * members[-1]) * inverse
-            for position, member in enumerate(members):
-                ortho = ortho - correlations[position] * member
-            return ortho * scale
-
-        if last:
-            own_rows = lambda values: lax.dynamic_slice_in_dim(values, op * half, half, axis=0)
-            basis.append(
-                (
-                    fresh(own_rows(image), own_rows(own_inverse), [own_rows(m[0]) for m in basis]),
-                    fresh(mate_image, own_rows(mate_inverse), [own_rows(m[1]) for m in basis]),
-                )
-            )
-        else:
-            basis.append(
-                tuple(
-                    fresh(images[i], inverses[i], [member[i] for member in basis]) for i in range(3)
-                )
-            )
-        latest = basis[-1]
-
-    def placed(own, mates):
-        return jnp.stack([jnp.where(op == 0, own, mates), jnp.where(op == 0, mates, own)])
-
-    output = [placed(own_rows(m[0]), own_rows(m[1])) for m in basis[1:-1]] + [placed(*basis[-1])]
-    return (jnp.stack(output), jnp.stack(ritz))
+    def own_sector(values):
+        return lax.dynamic_index_in_dim(values, op, 0, keepdims=False)
+
+    def exchanged(row):
+        spread = row.reshape(devices, 1, LANES)
+        return lax.all_to_all(spread, AXES, 0, 0, tiled=True).reshape(devices, LANES)
+
+    vmem = pl.BlockSpec(memory_space=pltpu.VMEM)
+    smem = pl.BlockSpec(memory_space=pltpu.SMEM)
+
+    def call(kernel, operands, shapes, scalars=0, out_scalars=0, scratch=True):
+        return pl.pallas_call(
+            kernel,
+            out_shape=[jax.ShapeDtypeStruct(shape, kind) for shape, kind in shapes],
+            in_specs=[smem] * scalars + [vmem] * (len(operands) - scalars),
+            out_specs=[vmem] * (len(shapes) - out_scalars) + [smem] * out_scalars,
+            scratch_shapes=[pltpu.VMEM((3, rows, columns), jnp.bfloat16)] * (2 if scratch else 0),
+            compiler_params=pltpu.CompilerParams(vmem_limit_bytes=32 * 2**20),
+        )(*operands)
+
+    block = (rows, columns)
+    f32, bf16 = jnp.float32, jnp.bfloat16
+    row_shape = ((devices, LANES), f32)
+    theta_shape = ((1, LANES), f32)
+
+    facing_wave = facing(own_sector(wave_start))
+    facing_preconditioner = facing(own_sector(preconditioner))
+    mate_left = mate(left_blocks)
+    mate_right = mate(right_blocks)
+    shifts = (term_shifts, mate(term_shifts))
+
+    split_shape = ((terms,) + left_blocks.shape[2:], bf16)
+    image, row, *blocks = call(
+        first_kernel,
+        (*shifts, wave_start, facing_wave, preconditioner, left_blocks, mate_left, right_blocks,
+         mate_right),
+        [(block, f32), row_shape] + [split_shape] * 4,
+        scalars=2,
+    )
+    images = (image, mate(image), facing(image))
+    image, row, start, first, inverse, first_theta = call(
+        functools.partial(second_kernel, total),
+        (*shifts, exchanged(row), wave_start, facing_wave, preconditioner, facing_preconditioner,
+         *images, *blocks),
+        [(block, f32), row_shape] + [((3,) + block, f32)] * 3 + [theta_shape],
+        scalars=2,
+    )
+    images = (image, mate(image), facing(image))
+    kept, sent, row, second, second_theta = call(
+        functools.partial(third_kernel, total),
+        (*shifts, exchanged(row), start, first, inverse, *images, *blocks),
+        [((half, columns), f32)] * 2 + [row_shape, ((2,) + block, f32), theta_shape],
+        scalars=2,
+    )
+    basis, ritz = call(
+        functools.partial(last_kernel, total),
+        (exchanged(row), first_theta, second_theta, start, first, second, inverse, kept,
+         mate(sent)),
+        [((ITERS, 2, half, columns), f32), ((ITERS,), f32)],
+        out_scalars=1,
+        scratch=False,
+    )
+    return (basis, ritz)
 
 
 def with_halo(cells, sides, width):

time: 123 us -> 69 us (0.56)
  other arithmetic: 29.1 us -> 0 us
  blocking collectives: 0 us -> 18.6 us
  local copies, waits for them, and re-layouts: 24.7 us -> 8.62 us
  between operations: 16.4 us -> 0.73 us
  Pallas kernels: 0 us -> 9.98 us
  matrix products: 7.65 us -> 0 us
  waiting for transfers between devices: 14.3 us -> 7.16 us
  starting transfers between devices: 30.1 us -> 23.5 us
    all_to_all x0 -> x2, blocking collectives: none -> 18.6 us  [exchanged(): lax.all_to_all(spread, AXES, 0, 0, tiled=True).reshape(devices, LANES)]
    another operation x3 -> x0, local copies, waits for them, and re-layouts: 15.9 us -> none  [one_sector_body(): sums = total_sum(jnp.stack(pieces))]
    mul x6 -> x0, other arithmetic: 14.5 us -> none  [the longest x5 11.7 us: fresh(): return ortho * scale]
    all_to_all x3 -> x1, starting transfers between devices: 17.8 us -> 5.44 us  [exchanged(): lax.all_to_all(spread, AXES, 0, 0, tiled=True).reshape(devices, LANES)]
    pallas_call x0 -> x4, Pallas kernels: none -> 9.98 us  [call(): pl.pallas_call(kernel, out_shape=[jax.ShapeDtypeStruct(shape, kind) for s...]
    dot_general x6 -> x0, matrix products: 7.65 us -> none  [the longest x3 3.85 us: operator(): inner = jnp.einsum('kab,kbc->kac', left, source, precision=highest)]
    all_to_all x3 -> x1, waiting for transfers between devices: 14.3 us -> 7.13 us  [exchanged(): lax.all_to_all(spread, AXES, 0, 0, tiled=True).reshape(devices, LANES)]
    another operation x6 -> x0, other arithmetic: 7.06 us -> none  [the longest x2 3.56 us: placed(): jnp.stack([jnp.where(op == 0, own, mates), jnp.where(op == 0, mates, own)])]
  transfers between devices with their start and end apart: 13 -> 11, of which waited for: 3 -> 1; matrix products, arithmetic and copies ran while one was open for 18% -> 3% of each run, Pallas kernels for 0% -> 4%
where the time goes in v2:
time: 69 us; the launch traced here: 68.5 us
  starting transfers between devices  23.5 us (34%)
  blocking collectives  18.6 us (27%)
  Pallas kernels  9.98 us (14%)
  local copies, waits for them, and re-layouts  8.62 us (12%)
  waiting for transfers between devices  7.16 us (10%)
  between operations  0.73 us (1%)
    all_to_all x2, blocking collectives, exchanged(): lax.all_to_all(spread, AXES, 0, 0, tiled=True).reshape(devices, LANES)  18.6 us
    ppermute x6, starting transfers between devices, mate(): return lax.ppermute(values, AXES, swap)  14 us
    pallas_call x4, Pallas kernels, call(): pl.pallas_call(kernel, out_shape=[jax.ShapeDtypeStruct(shape, kind) for s...  9.98 us
    all_to_all x1, waiting for transfers between devices, exchanged(): lax.all_to_all(spread, AXES, 0, 0, tiled=True).reshape(devices, LANES)  7.13 us
    unnamed x18, local copies, waits for them, and re-layouts  6.86 us
    all_to_all x1, starting transfers between devices, exchanged(): lax.all_to_all(spread, AXES, 0, 0, tiled=True).reshape(devices, LANES)  5.44 us
    ppermute x4, starting transfers between devices, facing(): return lax.ppermute(values, AXES, across)  4.07 us
    squeeze x2, local copies, waits for them, and re-layouts, own_sector(): return lax.dynamic_index_in_dim(values, op, 0, keepdims=False)  1.76 us
  transfers between devices with their start and end apart: 11, of which 1 were waited for; matrix products, arithmetic and copies ran while one was open for 3% of the time, Pallas kernels for 4%

profile of v2, /device:TPU:0, one launch (start us, length us, event | category | flops | bytes accessed | tf_op | source)
XLA Modules:
  0.0 68.5 jit_solution(17983683697244468779)
XLA Ops:
  0.6 0.5 collective-permute-start.2
  1.2 0.1 collective-permute-start.3
  1.2 1.0 %dynamic-slice_bitcast_fusion.1 = f32[256,256]{1,0:T(8,128)S(1)} fusion(f32[2,256,256]{2,1,0:T(8,128)} %wave.3, s32[]{:T(128)S(6)} %select_n.5), kind=kLoop, calls=%fused_computation.1 | loop fusion | bytes 524292 | tf_op jit(solution)/shard_map/jit(dynamic_index_in_dim)/squeeze | solution.py:247
  2.3 0.7 collective-permute-start.1
  3.0 4.3 %collective-permute-start = (s32[2]{0:T(128)S(1)}, s32[2]{0:T(128)S(1)}, u32[]{:S(2)}, u32[]{:S(2)}) collective-permute-start(s32[2]{0:T(128)S(1)} %copy-done.8), channel_id=1, source_target_pairs={{0,1},{1,0},{2,3},{3,2},{4,5},{5,4},{6,7},{7,6},{8,9},{9,8},{10,11... | collective-permute-start | bytes 32 | tf_op jit(solution)/shard_map/ppermute | solution.py:241
  7.3 0.7 %dynamic-slice_bitcast_fusion = f32[256,256]{1,0:T(8,128)} fusion(f32[2,256,256]{2,1,0:T(8,128)S(1)} %copy-done.1, s32[]{:T(128)S(6)} %select_n.5), kind=kLoop, calls=%fused_computation | loop fusion | bytes 524292 | tf_op jit(solution)/shard_map/jit(dynamic_index_in_dim)/squeeze | solution.py:247
  8.0 1.4 %collective-permute-start.4 = (f32[256,256]{1,0:T(8,128)}, f32[256,256]{1,0:T(8,128)}, u32[]{:S(2)}, u32[]{:S(2)}) collective-permute-start(f32[256,256]{1,0:T(8,128)} %dynamic-slice_bitcast_fusion), channel_id=1, source_target_pairs={{1,2},{3,4},{5,6},{7,8},{9,10},{11,12},{13,14},{15,16},{17,18},{19... | collective-permute-start | bytes 786440 | tf_op jit(solution)/shard_map/ppermute | solution.py:244
  9.4 0.0 collective-permute-done.mate_shifts
  9.4 0.0 collective-permute-done.1.facing_wave
  9.4 0.0 collective-permute-done.2.mate_left
  9.4 1.0 %copy-done.4 = f32[2,2,256,256]{3,2,1,0:T(8,128)} copy-done((f32[2,2,256,256]{3,2,1,0:T(8,128)}, f32[2,2,256,256]{3,2,1,0:T(8,128)S(1)}, u32[]{:S(2)}) %copy-start.4) | copy-done | bytes 1048600
  10.4 0.0 collective-permute-done.3.mate_right
  10.4 1.0 %copy-done.6 = f32[2,2,256,256]{3,2,1,0:T(8,128)} copy-done((f32[2,2,256,256]{3,2,1,0:T(8,128)}, f32[2,2,256,256]{3,2,1,0:T(8,128)S(1)}, u32[]{:S(2)}) %copy-start.6) | copy-done | bytes 1048600
  11.4 1.2 %copy-done.2 = f32[2,2,256,256]{3,2,1,0:T(8,128)S(1)} copy-done((f32[2,2,256,256]{3,2,1,0:T(8,128)S(1)}, f32[2,2,256,256]{3,2,1,0:T(8,128)}, u32[]{:S(2)}) %copy-start.2) | copy-done | bytes 1048600
  12.6 1.2 %copy-done.3 = f32[2,2,256,256]{3,2,1,0:T(8,128)S(1)} copy-done((f32[2,2,256,256]{3,2,1,0:T(8,128)S(1)}, f32[2,2,256,256]{3,2,1,0:T(8,128)}, u32[]{:S(2)}) %copy-start.3) | copy-done | bytes 1048600
  13.8 1.2 %copy-done.5 = f32[2,2,256,256]{3,2,1,0:T(8,128)S(1)} copy-done((f32[2,2,256,256]{3,2,1,0:T(8,128)S(1)}, f32[2,2,256,256]{3,2,1,0:T(8,128)}, u32[]{:S(2)}) %copy-start.5) | copy-done | bytes 1048600
  15.1 1.2 %copy-done.7 = f32[2,2,256,256]{3,2,1,0:T(8,128)S(1)} copy-done((f32[2,2,256,256]{3,2,1,0:T(8,128)S(1)}, f32[2,2,256,256]{3,2,1,0:T(8,128)}, u32[]{:S(2)}) %copy-start.7) | copy-done | bytes 1048600
  16.3 2.7 %shard_map.68 = (f32[256,256]{1,0:T(8,128)}, f32[32,128]{1,0:T(8,128)}, bf16[4,256,256]{2,1,0:T(8,128)(2,1)S(1)}, bf16[4,256,256]{2,1,0:T(8,128)(2,1)S(1)}, bf16...) custom-call(s32[2]{0:T(128)S(1)} %copy-done.8, s32[2]{0:T(128)S(1)} %collective-permute-done.mate_shifts, ...), custom_call_target="tpu_custom_call" | custom-call | tf_op jit(solution)/shard_map/pallas_call | solution.py:257
  19.0 1.4 %collective-permute-start.6 = (f32[256,256]{1,0:T(8,128)}, f32[256,256]{1,0:T(8,128)}, u32[]{:S(2)}, u32[]{:S(2)}) collective-permute-start(f32[256,256]{1,0:T(8,128)} %get-tuple-element.20.own_image), channel_id=1, source_target_pairs={{1,2},{3,4},{5,6},{7,8},{9,10},{11,12},{13,14},{15,16},{17,18},{19... | collective-permute-start | bytes 786440 | tf_op jit(solution)/shard_map/ppermute | solution.py:244
  20.4 7.0 %collective-permute-start.5 = (f32[256,256]{1,0:T(8,128)}, f32[256,256]{1,0:T(8,128)}, u32[]{:S(2)}, u32[]{:S(2)}) collective-permute-start(f32[256,256]{1,0:T(8,128)} %get-tuple-element.20.own_image), channel_id=1, source_target_pairs={{0,1},{1,0},{2,3},{3,2},{4,5},{5,4},{6,7},{7,6},{8,9},{9,8},{10,11... | collective-permute-start | bytes 786440 | tf_op jit(solution)/shard_map/ppermute | solution.py:241
  27.4 5.4 %all-to-all-start = ((f32[32,1,128]{2,1,0:T(1,128)}), f32[32,1,128]{2,1,0:T(1,128)S(1)}, u32[]{:S(2)}, u32[]{:S(2)}) async-start(f32[32,1,128]{2,1,0:T(1,128)} %bitcast.2), calls=%async_computation | async-start | bytes 32768 | tf_op jit(solution)/shard_map/all_to_all | solution.py:251
  32.8 0.0 collective-permute-done.4.facing_preconditioner
  32.8 7.1 %all-to-all-done = f32[32,1,128]{2,1,0:T(1,128)S(1)} async-done(((f32[32,1,128]{2,1,0:T(1,128)}), f32[32,1,128]{2,1,0:T(1,128)S(1)}, u32[]{:S(2)}, u32[]{:S(2)}) %all-to-all-start) | async-done | bytes 16416 | tf_op jit(solution)/shard_map/all_to_all | solution.py:251
  40.0 0.0 collective-permute-done.5.mate_image
  40.0 3.3 %shard_map.69 = (f32[256,256]{1,0:T(8,128)S(1)}, f32[32,128]{1,0:T(8,128)S(1)}, f32[3,256,256]{2,1,0:T(8,128)S(1)}, f32[3,256,256]{2,1,0:T(8,128)S(1)}, f32[3,25...) custom-call(s32[2]{0:T(128)S(1)} %copy-done.8, s32[2]{0:T(128)S(1)} %collective-permute-done.mate_shifts, ...), custom_call_target="tpu_custom_call" | custom-call | tf_op jit(solution)/shard_map/pallas_call | solution.py:257
  43.3 0.7 collective-permute-start.8
  44.0 1.9 %collective-permute-start.7 = (f32[256,256]{1,0:T(8,128)S(1)}, f32[256,256]{1,0:T(8,128)S(1)}, u32[]{:S(2)}, u32[]{:S(2)}) collective-permute-start(f32[256,256]{1,0:T(8,128)S(1)} %get-tuple-element.29.own_image), channel_id=1, source_target_pairs={{0,1},{1,0},{2,3},{3,2},{4,5},{5,4},{6,7},{7,6},{8,9},{9,8},{10,11... | collective-permute-start | bytes 786440 | tf_op jit(solution)/shard_map/ppermute | solution.py:241
  46.0 9.7 %all_to_all.15 = f32[32,1,128]{2,1,0:T(1,128)S(1)} all-to-all(f32[32,1,128]{2,1,0:T(1,128)S(1)} %bitcast.19), channel_id=1, replica_groups=mesh['sector'=16,'op'=2] {'sector','op'}, dimensions={0} | all-to-all | bytes 32768 | tf_op jit(solution)/shard_map/all_to_all | solution.py:251
  55.7 2.6 %shard_map.70 = (f32[128,256]{1,0:T(8,128)S(1)}, f32[128,256]{1,0:T(8,128)S(1)}, f32[32,128]{1,0:T(8,128)S(1)}, f32[2,256,256]{2,1,0:T(8,128)S(1)}, f32[1,128]{1,0:T(1,128)S(1)}) custom-call(s32[2]{0:T(128)S(1)} %copy-done.8, s32[2]{0:T(128)S(1)} %collective-permute-done.mate_shifts, f32[32,128]{1,0:T(8,128)S(1)} %bitcast.17, ...), custom_call_target="tpu_custom_call" | custom-call | tf_op jit(solution)/shard_map/pallas_call | solution.py:257
  58.3 0.1 collective-permute-start.9
  58.4 8.8 %all_to_all.16 = f32[32,1,128]{2,1,0:T(1,128)S(1)} all-to-all(f32[32,1,128]{2,1,0:T(1,128)S(1)} %bitcast.20), channel_id=1, replica_groups=mesh['sector'=16,'op'=2] {'sector','op'}, dimensions={0} | all-to-all | bytes 32768 | tf_op jit(solution)/shard_map/all_to_all | solution.py:251
  67.3 1.3 %shard_map.71 = (f32[3,2,128,256]{3,2,1,0:T(8,128)}, f32[3]{0:T(128)}) custom-call(f32[32,128]{1,0:T(8,128)S(1)} %bitcast.18, f32[1,128]{1,0:T(1,128)S(1)} %get-tuple-element.31.first_theta, f32[1,128]{1,0:T(1,128)S(1)} %get-tuple-element.32.second_theta, f32[3,256,256]{2,1,0:T(8,128)S(1)} %get-tuple-element.26.start, ...), custom_call_target="tpu_custom_call" | custom-call | tf_op jit(solution)/shard_map/pallas_call | solution.py:257
  (16 shorter events, 0.0 us)
Async XLA Ops:
  0.6 6.7 %copy-start.1 = (f32[2,256,256]{2,1,0:T(8,128)S(1)}, f32[2,256,256]{2,1,0:T(8,128)}, u32[]{:S(2)}) copy-start(f32[2,256,256]{2,1,0:T(8,128)} %preconditioner.3) | copy-start | bytes 1572868
  0.6 8.8 %collective-permute-start.2 = (f32[2,2,256,256]{3,2,1,0:T(8,128)}, f32[2,2,256,256]{3,2,1,0:T(8,128)S(1)}, u32[]{:S(2)}, u32[]{:S(2)}) collective-permute-start(f32[2,2,256,256]{3,2,1,0:T(8,128)} %own_left.1), channel_id=1, source_target_pairs={{0,1},{1,0},{2,3},{3,2},{4,5},{5,4},{6,7},{7,6},{8,9},{9,8},{10,11... | collective-permute-start | bytes 3145736 | tf_op jit(solution)/shard_map/ppermute | solution.py:241
  1.2 9.3 %collective-permute-start.3 = (f32[2,2,256,256]{3,2,1,0:T(8,128)}, f32[2,2,256,256]{3,2,1,0:T(8,128)S(1)}, u32[]{:S(2)}, u32[]{:S(2)}) collective-permute-start(f32[2,2,256,256]{3,2,1,0:T(8,128)} %own_right.1), channel_id=1, source_target_pairs={{0,1},{1,0},{2,3},{3,2},{4,5},{5,4},{6,7},{7,6},{8,9},{9,8},{10,11... | collective-permute-start | bytes 3145736 | tf_op jit(solution)/shard_map/ppermute | solution.py:241
  1.2 1.7 %copy-start.8 = (s32[2]{0:T(128)S(1)}, s32[2]{0:T(128)}, u32[]{:S(2)}) copy-start(s32[2]{0:T(128)} %own_shifts.5) | copy-start | bytes 28
  1.2 10.1 %copy-start = (f32[2,256,256]{2,1,0:T(8,128)S(1)}, f32[2,256,256]{2,1,0:T(8,128)}, u32[]{:S(2)}) copy-start(f32[2,256,256]{2,1,0:T(8,128)} %wave.3) | copy-start | bytes 1572868
  2.3 7.1 %collective-permute-start.1 = (f32[256,256]{1,0:T(8,128)S(1)}, f32[256,256]{1,0:T(8,128)S(1)}, u32[]{:S(2)}, u32[]{:S(2)}) collective-permute-start(f32[256,256]{1,0:T(8,128)S(1)} %dynamic-slice_bitcast_fusion.1), channel_id=1, source_target_pairs={{1,2},{3,4},{5,6},{7,8},{9,10},{11,12},{13,14},{15,16},{17,18},{19... | collective-permute-start | bytes 786440 | tf_op jit(solution)/shard_map/ppermute | solution.py:244
  3.0 6.4 %collective-permute-start = (s32[2]{0:T(128)S(1)}, s32[2]{0:T(128)S(1)}, u32[]{:S(2)}, u32[]{:S(2)}) collective-permute-start(s32[2]{0:T(128)S(1)} %copy-done.8), channel_id=1, source_target_pairs={{0,1},{1,0},{2,3},{3,2},{4,5},{5,4},{6,7},{7,6},{8,9},{9,8},{10,11... | collective-permute-start | bytes 32 | tf_op jit(solution)/shard_map/ppermute | solution.py:241
  8.0 24.8 %collective-permute-start.4 = (f32[256,256]{1,0:T(8,128)}, f32[256,256]{1,0:T(8,128)}, u32[]{:S(2)}, u32[]{:S(2)}) collective-permute-start(f32[256,256]{1,0:T(8,128)} %dynamic-slice_bitcast_fusion), channel_id=1, source_target_pairs={{1,2},{3,4},{5,6},{7,8},{9,10},{11,12},{13,14},{15,16},{17,18},{19... | collective-permute-start | bytes 786440 | tf_op jit(solution)/shard_map/ppermute | solution.py:244
  9.4 1.0 %copy-start.4 = (f32[2,2,256,256]{3,2,1,0:T(8,128)}, f32[2,2,256,256]{3,2,1,0:T(8,128)S(1)}, u32[]{:S(2)}) copy-start(f32[2,2,256,256]{3,2,1,0:T(8,128)S(1)} %collective-permute-done.2.mate_left) | copy-start | bytes 3145732
  10.4 1.0 %copy-start.6 = (f32[2,2,256,256]{3,2,1,0:T(8,128)}, f32[2,2,256,256]{3,2,1,0:T(8,128)S(1)}, u32[]{:S(2)}) copy-start(f32[2,2,256,256]{3,2,1,0:T(8,128)S(1)} %collective-permute-done.3.mate_right) | copy-start | bytes 3145732
  11.4 1.2 %copy-start.2 = (f32[2,2,256,256]{3,2,1,0:T(8,128)S(1)}, f32[2,2,256,256]{3,2,1,0:T(8,128)}, u32[]{:S(2)}) copy-start(f32[2,2,256,256]{3,2,1,0:T(8,128)} %own_left.1) | copy-start | bytes 3145732
  12.6 1.2 %copy-start.3 = (f32[2,2,256,256]{3,2,1,0:T(8,128)S(1)}, f32[2,2,256,256]{3,2,1,0:T(8,128)}, u32[]{:S(2)}) copy-start(f32[2,2,256,256]{3,2,1,0:T(8,128)} %own_right.1) | copy-start | bytes 3145732
  13.8 1.2 %copy-start.5 = (f32[2,2,256,256]{3,2,1,0:T(8,128)S(1)}, f32[2,2,256,256]{3,2,1,0:T(8,128)}, u32[]{:S(2)}) copy-start(f32[2,2,256,256]{3,2,1,0:T(8,128)} %copy-done.4) | copy-start | bytes 3145732
  15.1 1.2 %copy-start.7 = (f32[2,2,256,256]{3,2,1,0:T(8,128)S(1)}, f32[2,2,256,256]{3,2,1,0:T(8,128)}, u32[]{:S(2)}) copy-start(f32[2,2,256,256]{3,2,1,0:T(8,128)} %copy-done.6) | copy-start | bytes 3145732
  19.0 21.0 %collective-permute-start.6 = (f32[256,256]{1,0:T(8,128)}, f32[256,256]{1,0:T(8,128)}, u32[]{:S(2)}, u32[]{:S(2)}) collective-permute-start(f32[256,256]{1,0:T(8,128)} %get-tuple-element.20.own_image), channel_id=1, source_target_pairs={{1,2},{3,4},{5,6},{7,8},{9,10},{11,12},{13,14},{15,16},{17,18},{19... | collective-permute-start | bytes 786440 | tf_op jit(solution)/shard_map/ppermute | solution.py:244
  20.4 19.6 %collective-permute-start.5 = (f32[256,256]{1,0:T(8,128)}, f32[256,256]{1,0:T(8,128)}, u32[]{:S(2)}, u32[]{:S(2)}) collective-permute-start(f32[256,256]{1,0:T(8,128)} %get-tuple-element.20.own_image), channel_id=1, source_target_pairs={{0,1},{1,0},{2,3},{3,2},{4,5},{5,4},{6,7},{7,6},{8,9},{9,8},{10,11... | collective-permute-start | bytes 786440 | tf_op jit(solution)/shard_map/ppermute | solution.py:241
  27.4 12.6 %all-to-all-start = ((f32[32,1,128]{2,1,0:T(1,128)}), f32[32,1,128]{2,1,0:T(1,128)S(1)}, u32[]{:S(2)}, u32[]{:S(2)}) async-start(f32[32,1,128]{2,1,0:T(1,128)} %bitcast.2), calls=%async_computation | async-start | bytes 32768 | tf_op jit(solution)/shard_map/all_to_all | solution.py:251
  43.3 12.4 %collective-permute-start.8 = (f32[256,256]{1,0:T(8,128)S(1)}, f32[256,256]{1,0:T(8,128)S(1)}, u32[]{:S(2)}, u32[]{:S(2)}) collective-permute-start(f32[256,256]{1,0:T(8,128)S(1)} %get-tuple-element.29.own_image), channel_id=1, source_target_pairs={{1,2},{3,4},{5,6},{7,8},{9,10},{11,12},{13,14},{15,16},{17,18},{19... | collective-permute-start | bytes 786440 | tf_op jit(solution)/shard_map/ppermute | solution.py:244
  44.0 11.7 %collective-permute-start.7 = (f32[256,256]{1,0:T(8,128)S(1)}, f32[256,256]{1,0:T(8,128)S(1)}, u32[]{:S(2)}, u32[]{:S(2)}) collective-permute-start(f32[256,256]{1,0:T(8,128)S(1)} %get-tuple-element.29.own_image), channel_id=1, source_target_pairs={{0,1},{1,0},{2,3},{3,2},{4,5},{5,4},{6,7},{7,6},{8,9},{9,8},{10,11... | collective-permute-start | bytes 786440 | tf_op jit(solution)/shard_map/ppermute | solution.py:241
  58.3 8.9 %collective-permute-start.9 = (f32[128,256]{1,0:T(8,128)S(1)}, f32[128,256]{1,0:T(8,128)S(1)}, u32[]{:S(2)}, u32[]{:S(2)}) collective-permute-start(f32[128,256]{1,0:T(8,128)S(1)} %get-tuple-element.35), channel_id=1, source_target_pairs={{0,1},{1,0},{2,3},{3,2},{4,5},{5,4},{6,7},{7,6},{8,9},{9,8},{10,11... | collective-permute-start | bytes 393224 | tf_op jit(solution)/shard_map/ppermute | solution.py:241

commit v3 on v2

--- a/solution.py
+++ b/solution.py
@@ -137,20 +137,44 @@
     return jnp.where(values > 0.0, 1.0 / values, 0.0)
 
 
+def picking_kernel(
+    wave, preconditioner, left, right, own_wave, own_preconditioner, own_left, own_right, sent_left,
+    sent_right, picked,
+):
+    op = lax.axis_index("op")
+    pairs = [(wave.at[op], own_wave), (preconditioner.at[op], own_preconditioner)]
+    for values, own, sent in ((left, own_left, sent_left), (right, own_right, sent_right)):
+        for term in range(values.shape[0]):
+            pairs.append((values.at[term, 1 - op], sent.at[term]))
+            pairs.append((values.at[term, op], own.at[term]))
+    copies = [
+        pltpu.make_async_copy(source, target, picked.at[i])
+        for i, (source, target) in enumerate(pairs)
+    ]
+    for copy in copies:
+        copy.start()
+    for copy in copies:
+        copy.wait()
+
+
+def blocks_kernel(
+    own_left, mate_left, own_right, mate_right, left_high, left_low, right_high, right_low
+):
+    count = own_left.shape[0]
+    for half, pair in enumerate(((own_left, own_right), (mate_left, mate_right))):
+        for values, high, low in zip(pair, (left_high, right_high), (left_low, right_low)):
+            for term in range(count):
+                high[half * count + term], low[half * count + term] = split(values[term])
+
+
 def first_kernel(
-    own_shifts, mate_shifts, wave, facing_wave, preconditioner, own_left, mate_left, own_right,
-    mate_right, image_ref, row_ref, left_high, left_low, right_high, right_low, high, low,
+    own_shifts, mate_shifts, wave, facing_wave, preconditioner, left_high, left_low, right_high,
+    right_low, image_ref, row_ref, high, low,
 ):
     op = lax.axis_index("op")
     sources = term_sources(own_shifts, mate_shifts)
     for place, values in enumerate((wave[op], wave[1 - op], facing_wave[...])):
         high[place], low[place] = split(values)
-    count = own_left.shape[0]
-    for half, (left, right) in enumerate(((own_left, own_right), (mate_left, mate_right))):
-        for term in range(count):
-            place = half * count + term
-            left_high[place], left_low[place] = split(left[term, op])
-            right_high[place], right_low[place] = split(right[term, op])
     image = apply_terms(sources, (high, low), (left_high, left_low), (right_high, right_low))
     image_ref[...] = image
     own = wave[op]
@@ -260,7 +284,7 @@
             in_specs=[smem] * scalars + [vmem] * (len(operands) - scalars),
             out_specs=[vmem] * (len(shapes) - out_scalars) + [smem] * out_scalars,
             scratch_shapes=[pltpu.VMEM((3, rows, columns), jnp.bfloat16)] * (2 if scratch else 0),
-            compiler_params=pltpu.CompilerParams(vmem_limit_bytes=32 * 2**20),
+            compiler_params=pltpu.CompilerParams(vmem_limit_bytes=16 * 2**20),
         )(*operands)
 
     block = (rows, columns)
@@ -268,18 +292,30 @@
     row_shape = ((devices, LANES), f32)
     theta_shape = ((1, LANES), f32)
 
-    facing_wave = facing(own_sector(wave_start))
-    facing_preconditioner = facing(own_sector(preconditioner))
-    mate_left = mate(left_blocks)
-    mate_right = mate(right_blocks)
+    half_shape = left_blocks.shape[:1] + left_blocks.shape[2:]
+    picked_shapes = [block] * 2 + [half_shape] * 4
+    own_wave, own_preconditioner, own_left, own_right, sent_left, sent_right = pl.pallas_call(
+        picking_kernel,
+        out_shape=[jax.ShapeDtypeStruct(shape, f32) for shape in picked_shapes],
+        in_specs=[pl.BlockSpec(memory_space=pl.ANY)] * 4,
+        out_specs=[pl.BlockSpec(memory_space=pl.ANY)] * 6,
+        scratch_shapes=[pltpu.SemaphoreType.DMA((2 + 2 * terms,))],
+        compiler_params=pltpu.CompilerParams(vmem_limit_bytes=56 * 2**20),
+    )(wave_start, preconditioner, left_blocks, right_blocks)
+    facing_wave = facing(own_wave)
+    facing_preconditioner = facing(own_preconditioner)
     shifts = (term_shifts, mate(term_shifts))
 
-    split_shape = ((terms,) + left_blocks.shape[2:], bf16)
-    image, row, *blocks = call(
+    blocks = call(
+        blocks_kernel,
+        (own_left, mate(sent_left), own_right, mate(sent_right)),
+        [((terms,) + left_blocks.shape[2:], bf16)] * 4,
+        scratch=False,
+    )
+    image, row = call(
         first_kernel,
-        (*shifts, wave_start, facing_wave, preconditioner, left_blocks, mate_left, right_blocks,
-         mate_right),
-        [(block, f32), row_shape] + [split_shape] * 4,
+        (*shifts, wave_start, facing_wave, preconditioner, *blocks),
+        [(block, f32), row_shape],
         scalars=2,
     )
     images = (image, mate(image), facing(image))

time: 69 us -> 144 us (2.09)
  Pallas kernels: 9.98 us -> 90.8 us
  local copies, waits for them, and re-layouts: 8.62 us -> 2.94 us
    pallas_call x0 -> x1, Pallas kernels: none -> 80.6 us  [one_sector_body(): pl.pallas_call(picking_kernel, out_shape=[jax.ShapeDtypeStruct(shape, f32...]
    unnamed x18 -> x10, local copies, waits for them, and re-layouts: 6.86 us -> 2.94 us
    all_to_all x1, starting transfers between devices: 5.44 us -> 7.79 us  [exchanged(): lax.all_to_all(spread, AXES, 0, 0, tiled=True).reshape(devices, LANES)]
    ppermute x6, starting transfers between devices: 14 us -> 11.6 us  [mate(): return lax.ppermute(values, AXES, swap)]
    squeeze x2 -> x0, local copies, waits for them, and re-layouts: 1.76 us -> none  [own_sector(): return lax.dynamic_index_in_dim(values, op, 0, keepdims=False)]
    pallas_call x4 -> x5, Pallas kernels: 9.98 us -> 10.2 us  [call(): pl.pallas_call(kernel, out_shape=[jax.ShapeDtypeStruct(shape, kind) for s...]
  transfers between devices with their start and end apart: 11 -> 11, of which waited for: 1 -> 1; matrix products, arithmetic and copies ran while one was open for 3% -> 0% of each run, Pallas kernels for 4% -> 2%
where the time goes in v3:
time: 144 us
  Pallas kernels  90.8 us (63%)
  starting transfers between devices  23.5 us (16%)
  blocking collectives  18.6 us (13%)
  waiting for transfers between devices  7.17 us (5%)
  local copies, waits for them, and re-layouts  2.94 us (2%)
    pallas_call x1, Pallas kernels, one_sector_body(): pl.pallas_call(picking_kernel, out_shape=[jax.ShapeDtypeStruct(shape, f32...  80.6 us
    all_to_all x2, blocking collectives, exchanged(): lax.all_to_all(spread, AXES, 0, 0, tiled=True).reshape(devices, LANES)  18.6 us
    ppermute x6, starting transfers between devices, mate(): return lax.ppermute(values, AXES, swap)  11.6 us
    pallas_call x5, Pallas kernels, call(): pl.pallas_call(kernel, out_shape=[jax.ShapeDtypeStruct(shape, kind) for s...  10.2 us
    all_to_all x1, starting transfers between devices, exchanged(): lax.all_to_all(spread, AXES, 0, 0, tiled=True).reshape(devices, LANES)  7.79 us
    all_to_all x1, waiting for transfers between devices, exchanged(): lax.all_to_all(spread, AXES, 0, 0, tiled=True).reshape(devices, LANES)  7.14 us
    ppermute x4, starting transfers between devices, facing(): return lax.ppermute(values, AXES, across)  4.04 us
    unnamed x10, local copies, waits for them, and re-layouts  2.94 us
  transfers between devices with their start and end apart: 11, of which 1 were waited for; matrix products, arithmetic and copies ran while one was open for 0% of the time, Pallas kernels for 2%

profile of v3, /device:TPU:0, one launch (start us, length us, event | category | flops | bytes accessed | tf_op | source)
XLA Modules:
  0.0 143.7 jit_solution(9041637100211199749)
XLA Ops:
  0.6 80.6 %shard_map.68 = (f32[256,256]{1,0:T(8,128)}, f32[256,256]{1,0:T(8,128)}, f32[2,256,256]{2,1,0:T(8,128)}, f32[2,256,256]{2,1,0:T(8,128)}, f32[2,256,256]{2,1,0:T(8,128)}, /*index=5*/f32[2,256,256]{2,1,0:T(8,128)}) custom-call(f32[2,256,256]{2,1,0:T(8,128)} %wave.5, f32[2,256,256]{2,1,0:T(8,128)} %preconditioner.5, f32[2,2,256,256]{3,2,1,0:T(8,128)} %left.1, ...), custom_call_target="tpu_custom_call" | custom-call | tf_op jit(solution)/shard_map/pallas_call | solution.py:297
  81.2 0.5 collective-permute-start.2
  81.8 0.1 collective-permute-start.3
  81.9 0.7 collective-permute-start.1
  82.5 4.3 %collective-permute-start = (s32[2]{0:T(128)S(1)}, s32[2]{0:T(128)S(1)}, u32[]{:S(2)}, u32[]{:S(2)}) collective-permute-start(s32[2]{0:T(128)S(1)} %copy-done.4), channel_id=1, source_target_pairs={{0,1},{1,0},{2,3},{3,2},{4,5},{5,4},{6,7},{7,6},{8,9},{9,8},{10,11... | collective-permute-start | bytes 32 | tf_op jit(solution)/shard_map/ppermute | solution.py:265
  86.9 1.3 collective-permute-start.4
  88.2 0.0 collective-permute-done.2.mate_left
  88.2 0.0 collective-permute-done.3.mate_right
  88.2 1.0 copy-done.2
  89.3 1.0 copy-done.3
  90.3 0.3 shard_map.69
  90.6 0.0 collective-permute-done.mate_shifts
  90.6 0.0 collective-permute-done.1.facing_wave
  90.7 0.7 copy-done
  91.3 0.2 copy-done.1
  91.5 2.6 %shard_map.70 = (f32[256,256]{1,0:T(8,128)}, f32[32,128]{1,0:T(8,128)}) custom-call(s32[2]{0:T(128)S(1)} %copy-done.4, s32[2]{0:T(128)S(1)} %collective-permute-done.mate_shifts, f32[2,256,256]{2,1,0:T(8,128)S(1)} %copy-done, f32[256,256]{1,0:T(8,128)S(1)} %collective-permute-done.1.facing_wave, f32[2,256,256]{2,1,0:T(8,128)S(1)} %copy-done.1, ...), custom_call_target="tpu_custom_call" | custom-call | tf_op jit(solution)/shard_map/pallas_call | solution.py:281
  94.1 1.3 collective-permute-start.6
  95.5 4.7 %collective-permute-start.5 = (f32[256,256]{1,0:T(8,128)}, f32[256,256]{1,0:T(8,128)}, u32[]{:S(2)}, u32[]{:S(2)}) collective-permute-start(f32[256,256]{1,0:T(8,128)} %get-tuple-element.36.own_image), channel_id=1, source_target_pairs={{0,1},{1,0},{2,3},{3,2},{4,5},{5,4},{6,7},{7,6},{8,9},{9,8},{10,11... | collective-permute-start | bytes 786440 | tf_op jit(solution)/shard_map/ppermute | solution.py:265
  100.2 7.8 %all-to-all-start = ((f32[32,1,128]{2,1,0:T(1,128)}), f32[32,1,128]{2,1,0:T(1,128)S(1)}, u32[]{:S(2)}, u32[]{:S(2)}) async-start(f32[32,1,128]{2,1,0:T(1,128)} %bitcast.1), calls=%async_computation | async-start | bytes 32768 | tf_op jit(solution)/shard_map/all_to_all | solution.py:275
  108.0 0.0 collective-permute-done.4.facing_preconditioner
  108.0 7.1 %all-to-all-done = f32[32,1,128]{2,1,0:T(1,128)S(1)} async-done(((f32[32,1,128]{2,1,0:T(1,128)}), f32[32,1,128]{2,1,0:T(1,128)S(1)}, u32[]{:S(2)}, u32[]{:S(2)}) %all-to-all-start) | async-done | bytes 16416 | tf_op jit(solution)/shard_map/all_to_all | solution.py:275
  115.1 0.0 collective-permute-done.6.facing_image
  115.1 0.0 collective-permute-done.5.mate_image
  115.1 3.3 %shard_map.71 = (f32[256,256]{1,0:T(8,128)S(1)}, f32[32,128]{1,0:T(8,128)S(1)}, f32[3,256,256]{2,1,0:T(8,128)S(1)}, f32[3,256,256]{2,1,0:T(8,128)S(1)}, f32[3,25...) custom-call(s32[2]{0:T(128)S(1)} %copy-done.4, s32[2]{0:T(128)S(1)} %collective-permute-done.mate_shifts, ...), custom_call_target="tpu_custom_call" | custom-call | tf_op jit(solution)/shard_map/pallas_call | solution.py:281
  118.5 0.7 collective-permute-start.8
  119.1 1.9 %collective-permute-start.7 = (f32[256,256]{1,0:T(8,128)S(1)}, f32[256,256]{1,0:T(8,128)S(1)}, u32[]{:S(2)}, u32[]{:S(2)}) collective-permute-start(f32[256,256]{1,0:T(8,128)S(1)} %get-tuple-element.41.own_image), channel_id=1, source_target_pairs={{0,1},{1,0},{2,3},{3,2},{4,5},{5,4},{6,7},{7,6},{8,9},{9,8},{10,11... | collective-permute-start | bytes 786440 | tf_op jit(solution)/shard_map/ppermute | solution.py:265
  121.1 9.7 %all_to_all.15 = f32[32,1,128]{2,1,0:T(1,128)S(1)} all-to-all(f32[32,1,128]{2,1,0:T(1,128)S(1)} %bitcast.15), channel_id=1, replica_groups=mesh['sector'=16,'op'=2] {'sector','op'}, dimensions={0} | all-to-all | bytes 32768 | tf_op jit(solution)/shard_map/all_to_all | solution.py:275
  130.8 2.6 %shard_map.72 = (f32[128,256]{1,0:T(8,128)S(1)}, f32[128,256]{1,0:T(8,128)S(1)}, f32[32,128]{1,0:T(8,128)S(1)}, f32[2,256,256]{2,1,0:T(8,128)S(1)}, f32[1,128]{1,0:T(1,128)S(1)}) custom-call(s32[2]{0:T(128)S(1)} %copy-done.4, s32[2]{0:T(128)S(1)} %collective-permute-done.mate_shifts, f32[32,128]{1,0:T(8,128)S(1)} %bitcast.13, ...), custom_call_target="tpu_custom_call" | custom-call | tf_op jit(solution)/shard_map/pallas_call | solution.py:281
  133.5 0.1 collective-permute-start.9
  133.5 8.8 %all_to_all.16 = f32[32,1,128]{2,1,0:T(1,128)S(1)} all-to-all(f32[32,1,128]{2,1,0:T(1,128)S(1)} %bitcast.16), channel_id=1, replica_groups=mesh['sector'=16,'op'=2] {'sector','op'}, dimensions={0} | all-to-all | bytes 32768 | tf_op jit(solution)/shard_map/all_to_all | solution.py:275
  142.4 0.0 collective-permute-done.9.mate_image
  142.4 1.3 shard_map.73
  (8 shorter events, 0.0 us)
Async XLA Ops:
  81.2 7.0 %collective-permute-start.2 = (f32[2,256,256]{2,1,0:T(8,128)}, f32[2,256,256]{2,1,0:T(8,128)S(1)}, u32[]{:S(2)}, u32[]{:S(2)}) collective-permute-start(f32[2,256,256]{2,1,0:T(8,128)} %get-tuple-element.27), channel_id=1, source_target_pairs={{0,1},{1,0},{2,3},{3,2},{4,5},{5,4},{6,7},{7,6},{8,9},{9,8},{10,11... | collective-permute-start | bytes 1572872 | tf_op jit(solution)/shard_map/ppermute | solution.py:265
  81.8 0.8 copy-start.4
  81.8 6.4 %collective-permute-start.3 = (f32[2,256,256]{2,1,0:T(8,128)}, f32[2,256,256]{2,1,0:T(8,128)S(1)}, u32[]{:S(2)}, u32[]{:S(2)}) collective-permute-start(f32[2,256,256]{2,1,0:T(8,128)} %get-tuple-element.29), channel_id=1, source_target_pairs={{0,1},{1,0},{2,3},{3,2},{4,5},{5,4},{6,7},{7,6},{8,9},{9,8},{10,11... | collective-permute-start | bytes 1572872 | tf_op jit(solution)/shard_map/ppermute | solution.py:265
  81.9 8.8 %collective-permute-start.1 = (f32[256,256]{1,0:T(8,128)}, f32[256,256]{1,0:T(8,128)S(1)}, u32[]{:S(2)}, u32[]{:S(2)}) collective-permute-start(f32[256,256]{1,0:T(8,128)} %get-tuple-element.25), channel_id=1, source_target_pairs={{1,2},{3,4},{5,6},{7,8},{9,10},{11,12},{13,14},{15,16},{17,18},{19... | collective-permute-start | bytes 786440 | tf_op jit(solution)/shard_map/ppermute | solution.py:268
  82.5 8.1 %collective-permute-start = (s32[2]{0:T(128)S(1)}, s32[2]{0:T(128)S(1)}, u32[]{:S(2)}, u32[]{:S(2)}) collective-permute-start(s32[2]{0:T(128)S(1)} %copy-done.4), channel_id=1, source_target_pairs={{0,1},{1,0},{2,3},{3,2},{4,5},{5,4},{6,7},{7,6},{8,9},{9,8},{10,11... | collective-permute-start | bytes 32 | tf_op jit(solution)/shard_map/ppermute | solution.py:265
  86.9 21.1 %collective-permute-start.4 = (f32[256,256]{1,0:T(8,128)}, f32[256,256]{1,0:T(8,128)}, u32[]{:S(2)}, u32[]{:S(2)}) collective-permute-start(f32[256,256]{1,0:T(8,128)} %get-tuple-element.35), channel_id=1, source_target_pairs={{1,2},{3,4},{5,6},{7,8},{9,10},{11,12},{13,14},{15,16},{17,18},{19... | collective-permute-start | bytes 786440 | tf_op jit(solution)/shard_map/ppermute | solution.py:268
  88.2 1.0 copy-start.2
  89.3 1.0 copy-start.3
  90.3 1.0 copy-start
  90.3 1.2 copy-start.1
  94.1 21.0 %collective-permute-start.6 = (f32[256,256]{1,0:T(8,128)}, f32[256,256]{1,0:T(8,128)}, u32[]{:S(2)}, u32[]{:S(2)}) collective-permute-start(f32[256,256]{1,0:T(8,128)} %get-tuple-element.36.own_image), channel_id=1, source_target_pairs={{1,2},{3,4},{5,6},{7,8},{9,10},{11,12},{13,14},{15,16},{17,18},{19... | collective-permute-start | bytes 786440 | tf_op jit(solution)/shard_map/ppermute | solution.py:268
  95.5 19.7 %collective-permute-start.5 = (f32[256,256]{1,0:T(8,128)}, f32[256,256]{1,0:T(8,128)}, u32[]{:S(2)}, u32[]{:S(2)}) collective-permute-start(f32[256,256]{1,0:T(8,128)} %get-tuple-element.36.own_image), channel_id=1, source_target_pairs={{0,1},{1,0},{2,3},{3,2},{4,5},{5,4},{6,7},{7,6},{8,9},{9,8},{10,11... | collective-permute-start | bytes 786440 | tf_op jit(solution)/shard_map/ppermute | solution.py:265
  100.2 15.0 %all-to-all-start = ((f32[32,1,128]{2,1,0:T(1,128)}), f32[32,1,128]{2,1,0:T(1,128)S(1)}, u32[]{:S(2)}, u32[]{:S(2)}) async-start(f32[32,1,128]{2,1,0:T(1,128)} %bitcast.1), calls=%async_computation | async-start | bytes 32768 | tf_op jit(solution)/shard_map/all_to_all | solution.py:275
  118.5 12.4 %collective-permute-start.8 = (f32[256,256]{1,0:T(8,128)S(1)}, f32[256,256]{1,0:T(8,128)S(1)}, u32[]{:S(2)}, u32[]{:S(2)}) collective-permute-start(f32[256,256]{1,0:T(8,128)S(1)} %get-tuple-element.41.own_image), channel_id=1, source_target_pairs={{1,2},{3,4},{5,6},{7,8},{9,10},{11,12},{13,14},{15,16},{17,18},{19... | collective-permute-start | bytes 786440 | tf_op jit(solution)/shard_map/ppermute | solution.py:268
  119.1 11.7 %collective-permute-start.7 = (f32[256,256]{1,0:T(8,128)S(1)}, f32[256,256]{1,0:T(8,128)S(1)}, u32[]{:S(2)}, u32[]{:S(2)}) collective-permute-start(f32[256,256]{1,0:T(8,128)S(1)} %get-tuple-element.41.own_image), channel_id=1, source_target_pairs={{0,1},{1,0},{2,3},{3,2},{4,5},{5,4},{6,7},{7,6},{8,9},{9,8},{10,11... | collective-permute-start | bytes 786440 | tf_op jit(solution)/shard_map/ppermute | solution.py:265
  133.5 8.9 %collective-permute-start.9 = (f32[128,256]{1,0:T(8,128)S(1)}, f32[128,256]{1,0:T(8,128)S(1)}, u32[]{:S(2)}, u32[]{:S(2)}) collective-permute-start(f32[128,256]{1,0:T(8,128)S(1)} %get-tuple-element.47), channel_id=1, source_target_pairs={{0,1},{1,0},{2,3},{3,2},{4,5},{5,4},{6,7},{7,6},{8,9},{9,8},{10,11... | collective-permute-start | bytes 393224 | tf_op jit(solution)/shard_map/ppermute | solution.py:265

commit v4 on v3

v4 whole, which is shorter than its diff:
```python
import functools

import jax
import jax.numpy as jnp
from jax import lax
from jax.experimental import pallas as pl
from jax.experimental.pallas import tpu as pltpu
from jax.sharding import PartitionSpec as P

ITERS = 3


EPSILON = 1e-06

AXES = ("sector", "op")

LANES = 128


def total_sum(values):
    devices = lax.axis_size("sector") * lax.axis_size("op")
    row = jnp.pad(values, (0, LANES - values.shape[0]))
    rows = lax.all_to_all(jnp.broadcast_to(row, (devices, LANES)), AXES, 0, 0, tiled=True)
    return jnp.sum(rows, axis=0)[: values.shape[0]]


def coefficients(sums, total, count):
    sums = sums / total
    theta = sums[0]
    correlations = sums[4 : 4 + count] - theta * sums[4 + count : 4 + 2 * count]
    length = (
        sums[1]
        - 2.0 * theta * sums[2]
        + theta * theta * sums[3]
        - jnp.sum(jnp.square(correlations))
    )
    return theta, correlations, lax.rsqrt(length + EPSILON)


def products(members, image, inverse):
    latest = members[-1]
    ratio_image = image * inverse
    ratio_latest = latest * inverse
    pieces = [
        jnp.sum(latest * image),
        jnp.sum(ratio_image * ratio_image),
        jnp.sum(ratio_image * ratio_latest),
        jnp.sum(ratio_latest * ratio_latest),
    ]
    pieces = pieces + [jnp.sum(member * ratio_image) for member in members]
    pieces = pieces + [jnp.sum(member * ratio_latest) for member in members]
    return pieces


def split(values):
    high = values.astype(jnp.bfloat16)
    return high, (values - high.astype(jnp.float32)).astype(jnp.bfloat16)


def dot_split(lhs_high, lhs_low, rhs_high, rhs_low):
    dot = functools.partial(jnp.dot, preferred_element_type=jnp.float32)
    return dot(lhs_high, rhs_high) + (dot(lhs_low, rhs_high) + dot(lhs_high, rhs_low))


def apply_terms(sources, vectors, left, right):
    left_high, left_low = left
    right_high, right_low = right
    vector_high, vector_low = vectors
    image = None
    for term, source in enumerate(sources):
        inner = dot_split(left_high[term], left_low[term], vector_high[source], vector_low[source])
        part = dot_split(*split(inner), right_high[term], right_low[term])
        image = part if image is None else image + part
    return image


def term_sources(own_shifts, mate_shifts):
    toward_mate = jnp.where(lax.axis_index("op") == 0, -1, 1)
    shifts = [refs[i] for refs in (own_shifts, mate_shifts) for i in range(refs.shape[0])]
    return [
        jnp.where(shift == 0, 0, jnp.where(shift == toward_mate, 1, 2)) for shift in shifts
    ]


def row_of_sums(factors, first=0, row=None):
    lane = lax.broadcasted_iota(jnp.int32, (1, LANES), 1)
    if row is None:
        row = jnp.zeros((1, LANES), jnp.float32)
    for position, (one, other) in enumerate(factors):
        product = (one * other).reshape(-1, 8, one.shape[1])
        whole = jnp.sum(jnp.sum(product, axis=0), axis=(0, 1), keepdims=True)
        row = jnp.where(lane == first + position, whole, row)
    return row


def summed(rows, total, count):
    whole = jnp.sum(rows[...], axis=0, keepdims=True) * (1.0 / total)
    return [jnp.broadcast_to(whole[:, i : i + 1], (8, LANES)) for i in range(count)]


def one_of(value):
    return value[:1, :1]


EARLY_MOMENTS = (
    [("w", "w", n) for n in range(5)]
    + [("u", "w", n) for n in range(5)]
    + [("u", "u", n) for n in range(1, 5)]
    + [("a", "w", n) for n in range(4)]
    + [("a", "u", n) for n in range(1, 4)]
    + [("a", "a", 2)]
)
LATE_MOMENTS = (
    [("b", "w", n) for n in range(4)]
    + [("b", "u", n) for n in range(1, 4)]
    + [("a", "b", 2), ("b", "b", 2)]
)

H_OF = {("w", 0): "u", ("w", 1): "a", ("u", 1): "b"}

START_SCALE = 2.0**10
H_SCALE = 2.0**7


def moment_factors(moments, arrays, inverse):
    powers = {(name, 0): values for name, values in arrays.items()}

    def power(name, n):
        if (name, n) not in powers:
            powers[name, n] = power(name, n - 1) * inverse
        return powers[name, n]

    return [(power(x, n // 2), power(y, n - n // 2)) for x, y, n in moments]


def plus(vector, other, factor):
    result = dict(vector)
    for word, value in other.items():
        term = value * factor
        result[word] = result[word] + term if word in result else term
    return result


def times_inverse(vector):
    return {(name, n + 1): value for (name, n), value in vector.items()}


def times_h(vector):
    return {(H_OF[word], 0): value * H_SCALE for word, value in vector.items()}


def inner(one, other, moments):
    result = None
    for (x, n), value in one.items():
        part = None
        for (y, m), factor in other.items():
            term = factor * moments[tuple(sorted((x, y))) + (n + m,)]
            part = term if part is None else part + term
        part = value * part
        result = part if result is None else result + part
    return result


def first_two_steps(sums):
    moments = dict(zip(EARLY_MOMENTS + LATE_MOMENTS, sums))
    basis = [{("w", 0): lax.rsqrt(moments["w", "w", 0] + EPSILON * START_SCALE**2)}]
    thetas = []
    for _ in range(2):
        latest = basis[-1]
        image = times_h(latest)
        theta = inner(latest, image, moments)
        correction = times_inverse(plus(image, latest, -theta))
        ortho = correction
        for member in basis:
            ortho = plus(ortho, member, -inner(member, correction, moments))
        scale = lax.rsqrt(inner(ortho, ortho, moments) + EPSILON)
        basis.append({word: value * scale for word, value in ortho.items()})
        thetas.append(theta)
    return basis, thetas


def combined(vector, arrays, inverse):
    words = {name: (n, values) for (name, n), values in arrays.items()}
    result = None
    for n in range(max(n for _, n in vector), -1, -1):
        if result is not None:
            result = result * inverse
        for (name, m), value in vector.items():
            held, values = words[name]
            if m - held == n:
                term = one_of(value) * values
                result = term if result is None else result + term
    return result


def inverted(values):
    return jnp.where(values > 0.0, 1.0 / values, 0.0)


def copy_all(pairs, arrived):
    copies = [
        pltpu.make_async_copy(source, target, arrived.at[i])
        for i, (source, target) in enumerate(pairs)
    ]
    for copy in copies:
        copy.start()
    for copy in copies:
        copy.wait()


def picking_kernel(
    wave, preconditioner, left, right, own_wave, own_preconditioner, sent_left, sent_right, arrived
):
    op = lax.axis_index("op")
    pairs = [(wave.at[op], own_wave), (preconditioner.at[op], own_preconditioner)]
    for values, sent in ((left, sent_left), (right, sent_right)):
        for term in range(values.shape[0]):
            pairs.append((values.at[term, 1 - op], sent.at[term]))
    copy_all(pairs, arrived)


def splitting_kernel(
    wave, facing_wave, own_left, own_right, mate_left, mate_right, start_ref, high, low, left_high,
    left_low, right_high, right_low,
):
    op = lax.axis_index("op")
    for place, values in enumerate((wave[op], wave[1 - op], facing_wave[...])):
        start = values * START_SCALE
        start_ref[place] = start
        high[place], low[place] = split(start)
    count = own_left.shape[0]
    for term in range(count):
        left_high[term], left_low[term] = split(own_left[term, op] * (1.0 / H_SCALE))
        right_high[term], right_low[term] = split(own_right[term, op])
        place = count + term
        left_high[place], left_low[place] = split(mate_left[term] * (1.0 / H_SCALE))
        right_high[place], right_low[place] = split(mate_right[term])


def first_kernel(
    own_shifts, mate_shifts, high, low, left_high, left_low, right_high, right_low, image_ref
):
    sources = term_sources(own_shifts, mate_shifts)
    image_ref[...] = apply_terms(
        sources, (high, low), (left_high, left_low), (right_high, right_low)
    )


def side_kernel(
    own_shifts, mate_shifts, start, preconditioner, facing_preconditioner, image,
    left_high, left_low, right_high, right_low, side_ref, row_ref, inverse_ref, high, low,
):
    op = lax.axis_index("op")
    sources = term_sources(own_shifts, mate_shifts)
    divisors = (preconditioner[op], preconditioner[1 - op], facing_preconditioner[...])
    for place in range(3):
        inverse = inverted(divisors[place])
        inverse_ref[place] = inverse
        high[place], low[place] = split(start[place] * inverse)
    side = apply_terms(sources, (high, low), (left_high, left_low), (right_high, right_low))
    side_ref[...] = side
    arrays = {"w": start[0], "u": image[...], "a": side}
    row_ref[...] = row_of_sums(moment_factors(EARLY_MOMENTS, arrays, inverse_ref[0]))


def second_kernel(
    own_shifts, mate_shifts, start, own_image, mate_image, facing_image, inverse, side, early_row,
    left_high, left_low, right_high, right_low, image_ref, row_ref, ratio_ref, high, low,
):
    sources = term_sources(own_shifts, mate_shifts)
    for place, image in enumerate((own_image, mate_image, facing_image)):
        ratio = image[...] * inverse[place]
        ratio_ref[place] = ratio
        high[place], low[place] = split(ratio)
    image = apply_terms(sources, (high, low), (left_high, left_low), (right_high, right_low))
    image_ref[...] = image
    arrays = {"w": start[0], "u": own_image[...], "a": side[...], "b": image}
    factors = moment_factors(LATE_MOMENTS, arrays, inverse[0])
    row = row_of_sums(factors, len(EARLY_MOMENTS), early_row[...])
    row_ref[...] = jnp.broadcast_to(row, row_ref.shape)


MEMBER_PAIRS = [(i, j) for i in range(3) for j in range(i + 1)]


def third_kernel(
    total, own_shifts, mate_shifts, rows, start, inverse, ratio, own_side, mate_side,
    facing_side, own_second, mate_second, facing_second, left_high, left_low, right_high, right_low,
    kept_ref, sent_ref, row_ref, members_ref, theta_ref, high, low,
):
    op = lax.axis_index("op")
    sources = term_sources(own_shifts, mate_shifts)
    count = len(EARLY_MOMENTS + LATE_MOMENTS)
    basis, thetas = first_two_steps(summed(rows, total, count))
    for position, theta in enumerate(thetas):
        theta_ref[position] = theta
    half = kept_ref.shape[0]
    sides = (own_side, mate_side, facing_side)
    seconds = (own_second, mate_second, facing_second)

    def mine(values):
        return jnp.where(op == 0, values[:half], values[half:])

    for place in range(3):
        arrays = {
            ("w", 0): start[place],
            ("u", 1): ratio[place],
            ("a", 0): sides[place][...],
            ("b", 0): seconds[place][...],
        }
        latest = combined(basis[2], arrays, inverse[place])
        high[place], low[place] = split(latest)
        if place < 2:
            members = [combined(vector, arrays, inverse[place]) for vector in basis[:2]] + [latest]
            for position, member in enumerate(members):
                members_ref[position, place] = mine(member)
            if place == 0:
                own_members = members
    image = H_SCALE * apply_terms(
        sources, (high, low), (left_high, left_low), (right_high, right_low)
    )
    kept_ref[...] = mine(image)
    sent_ref[...] = jnp.where(op == 0, image[half:], image[:half])
    members = own_members
    ratio_image = image * inverse[0]
    ratio_latest = members[-1] * inverse[0]
    factors = [
        (members[-1], image),
        (ratio_image, ratio_image),
        (ratio_image, ratio_latest),
        (ratio_latest, ratio_latest),
    ]
    factors = factors + [(member, ratio_image) for member in members]
    factors = factors + [(member, ratio_latest) for member in members]
    factors = factors + [(members[i], members[j]) for i, j in MEMBER_PAIRS]
    row_ref[...] = jnp.broadcast_to(row_of_sums(factors), row_ref.shape)


def last_kernel(
    total, rows, thetas, members, inverse, own_image, mate_image, basis_ref, ritz_ref
):
    op = lax.axis_index("op")
    sums = summed(rows, total, 10 + len(MEMBER_PAIRS))
    theta = sums[0]
    correlations = [sums[4 + i] - theta * sums[7 + i] for i in range(3)]
    length = sums[1] - 2.0 * theta * sums[2] + theta * theta * sums[3]
    for correlation in correlations:
        length = length - 2.0 * correlation * correlation
    for (i, j), value in zip(MEMBER_PAIRS, sums[10:]):
        length = length + (1.0 if i == j else 2.0) * correlations[i] * correlations[j] * value
    scale = lax.rsqrt(length + EPSILON)
    half = own_image.shape[0]
    mine = pl.ds(pl.multiple_of(op * half, half), half)
    for place, (image, sector) in enumerate(((own_image, op), (mate_image, 1 - op))):
        basis_ref[0, sector] = members[1, place]
        basis_ref[1, sector] = members[2, place]
        ortho = (image[...] - one_of(theta) * members[2, place]) * inverse[place, mine]
        for i, correlation in enumerate(correlations):
            ortho = ortho - one_of(correlation) * members[i, place]
        basis_ref[2, sector] = ortho * one_of(scale)
    for position, value in enumerate((thetas[0], thetas[1], theta)):
        ritz_ref[position] = value[0, 0]


def one_sector_body(wave_start, left_blocks, right_blocks, term_shifts, preconditioner):
    op = lax.axis_index("op")
    chips = lax.axis_size("sector")
    devices = 2 * chips
    rows, columns = wave_start.shape[1:]
    half = rows // 2
    terms = 2 * left_blocks.shape[0]
    total = float(devices * rows * columns)
    swap = [(i, i ^ 1) for i in range(devices)]
    across = [(i, i + 1) for i in range(1, devices - 1, 2)]
    across = across + [(j, i) for i, j in across]

    def mate(values):
        return lax.ppermute(values, AXES, swap)

    def facing(values):
        return lax.ppermute(values, AXES, across)

    def own_sector(values):
        return lax.dynamic_index_in_dim(values, op, 0, keepdims=False)

    def exchanged(row):
        spread = row.reshape(devices, 1, LANES)
        return lax.all_to_all(spread, AXES, 0, 0, tiled=True).reshape(devices, LANES)

    vmem = pl.BlockSpec(memory_space=pltpu.VMEM)
    smem = pl.BlockSpec(memory_space=pltpu.SMEM)

    def call(kernel, operands, shapes, scalars=0, out_scalars=0, scratch=True):
        return pl.pallas_call(
            kernel,
            out_shape=[jax.ShapeDtypeStruct(shape, kind) for shape, kind in shapes],
            in_specs=[smem] * scalars + [vmem] * (len(operands) - scalars),
            out_specs=[vmem] * (len(shapes) - out_scalars) + [smem] * out_scalars,
            scratch_shapes=[pltpu.VMEM((3, rows, columns), jnp.bfloat16)] * (2 if scratch else 0),
            compiler_params=pltpu.CompilerParams(vmem_limit_bytes=16 * 2**20),
        )(*operands)

    block = (rows, columns)
    f32, bf16 = jnp.float32, jnp.bfloat16
    row_shape = ((devices, LANES), f32)

    half_shape = left_blocks.shape[:1] + left_blocks.shape[2:]
    own_wave, own_preconditioner, sent_left, sent_right = pl.pallas_call(
        picking_kernel,
        out_shape=[jax.ShapeDtypeStruct(shape, f32) for shape in [block] * 2 + [half_shape] * 2],
        in_specs=[pl.BlockSpec(memory_space=pl.ANY)] * 4,
        out_specs=[vmem] * 4,
        scratch_shapes=[pltpu.SemaphoreType.DMA((2 + terms,))],
        compiler_params=pltpu.CompilerParams(vmem_limit_bytes=56 * 2**20),
    )(wave_start, preconditioner, left_blocks, right_blocks)
    facing_wave = facing(own_wave)
    facing_preconditioner = facing(own_preconditioner)
    mate_left, mate_right = mate(sent_left), mate(sent_right)
    shifts = (term_shifts, mate(term_shifts))

    split_shape = (terms,) + left_blocks.shape[2:]
    start, start_high, start_low, *blocks = call(
        splitting_kernel,
        (wave_start, facing_wave, left_blocks, right_blocks, mate_left, mate_right),
        [((3,) + block, f32)] + [((3,) + block, bf16)] * 2 + [(split_shape, bf16)] * 4,
        scratch=False,
    )
    def around(values):
        return (values, mate(values), facing(values))

    (image,) = call(
        first_kernel,
        (*shifts, start_high, start_low, *blocks),
        [(block, f32)],
        scalars=2,
        scratch=False,
    )
    images = around(image)
    side, early_row, inverse = call(
        side_kernel,
        (*shifts, start, preconditioner, facing_preconditioner, image, *blocks),
        [(block, f32), ((1, LANES), f32), ((3,) + block, f32)],
        scalars=2,
    )
    sides = around(side)
    second, row, ratio = call(
        second_kernel,
        (*shifts, start, *images, inverse, side, early_row, *blocks),
        [(block, f32), row_shape, ((3,) + block, f32)],
        scalars=2,
    )
    seconds = around(second)
    row, *sides = lax.optimization_barrier((row, *sides))
    half_block = (half, columns)
    kept, sent, row, members, thetas = call(
        functools.partial(third_kernel, total),
        (*shifts, exchanged(row), start, inverse, ratio, *sides, *seconds, *blocks),
        [(half_block, f32)] * 2 + [row_shape, ((3, 2) + half_block, f32), ((2, 8, LANES), f32)],
        scalars=2,
    )
    basis, ritz = call(
        functools.partial(last_kernel, total),
        (exchanged(row), thetas, members, inverse, kept, mate(sent)),
        [((ITERS, 2) + half_block, f32), ((ITERS,), f32)],
        out_scalars=1,
        scratch=False,
    )
    return (basis, ritz)


def with_halo(cells, sides, width):
    for axis, dim in sides:
        count = lax.axis_size(axis)
        ends = count - 1
        head = lax.slice_in_dim(cells, 0, width, axis=dim)
        tail = lax.slice_in_dim(cells, cells.shape[dim] - width, cells.shape[dim], axis=dim)
        cells = jnp.concatenate(
            [
                lax.ppermute(tail, axis, [(i, (i + 1) % count) for i in range(ends)]),
                cells,
                lax.ppermute(head, axis, [((i + 1) % count, i) for i in range(ends)]),
            ],
            axis=dim,
        )
    return cells


def split_terms_body(wave_start, left_blocks, right_blocks, term_shifts, preconditioner):
    highest = lax.Precision.HIGHEST
    width = wave_start.shape[1]
    row_count = width // lax.axis_size("op")
    first_row = lax.axis_index("op") * row_count
    total = float(wave_start.shape[0] * lax.axis_size("sector") * width * wave_start.shape[2])

    def portion(values):
        return lax.dynamic_slice_in_dim(values, first_row, row_count, axis=values.ndim - 2)

    start_sum = total_sum(jnp.sum(jnp.square(portion(wave_start)))[None])[0] / total
    basis = [wave_start * lax.rsqrt(start_sum + EPSILON)]
    ritz = []
    for _ in range(ITERS):
        latest = basis[-1]
        padded = with_halo(latest, (("sector", 0),), 1)
        shift = term_shifts[:, None, None, None]
        source = jnp.where(
            shift == 1,
            padded[None, :-2],
            jnp.where(shift == -1, padded[None, 2:], padded[None, 1:-1]),
        )
        inner = jnp.einsum("ksab,ksbc->ksac", left_blocks, source, precision=highest)
        image = lax.psum(jnp.einsum("ksac,kscd->sad", inner, right_blocks, precision=highest), "op")
        inverse = 1.0 / preconditioner
        pieces = products([portion(member) for member in basis], portion(image), portion(inverse))
        theta, correlations, scale = coefficients(
            total_sum(jnp.stack(pieces)), total, len(basis)
        )
        ortho = (image - theta * latest) * inverse
        for position, member in enumerate(basis):
            ortho = ortho - correlations[position] * member
        basis.append(ortho * scale)
        ritz.append(theta)
    output = jnp.stack([portion(member) for member in basis[1:]])
    return (output, jnp.stack(ritz))


def solution(mesh):
    placed = (
        P("sector", None, None),
        P("op", "sector", None, None),
        P("op", "sector", None, None),
        P("op"),
        P("sector", None, None),
    )

    def body(wave_start, *operands):
        one_each = mesh.shape["op"] == 2 and wave_start.shape[0] == 2
        return (one_sector_body if one_each else split_terms_body)(wave_start, *operands)

    return jax.shard_map(
        body,
        mesh=mesh,
        in_specs=placed,
        out_specs=(P(None, "sector", "op", None), P()),
        check_vma=False,
    )
```

time: 144 us -> 62.5 us (0.43)
  Pallas kernels: 90.8 us -> 13.9 us
  waiting for transfers between devices: 7.17 us -> 0.17 us
  blocking collectives: 18.6 us -> 22.9 us
  local copies, waits for them, and re-layouts: 2.94 us -> 0.02 us
    pallas_call x1, Pallas kernels: 80.6 us -> 2.7 us  [one_sector_body(): pl.pallas_call(picking_kernel, out_shape=[jax.ShapeDtypeStruct(shape, f32...]
    ppermute x6 -> x7, starting transfers between devices: 11.6 us -> 20.9 us  [mate(): return lax.ppermute(values, AXES, swap)]
    all_to_all x1 -> x0, starting transfers between devices: 7.79 us -> none  [exchanged(): lax.all_to_all(spread, AXES, 0, 0, tiled=True).reshape(devices, LANES)]
    all_to_all x1 -> x0, waiting for transfers between devices: 7.14 us -> none  [exchanged(): lax.all_to_all(spread, AXES, 0, 0, tiled=True).reshape(devices, LANES)]
    all_to_all x2, blocking collectives: 18.6 us -> 22.9 us  [exchanged(): lax.all_to_all(spread, AXES, 0, 0, tiled=True).reshape(devices, LANES)]
    unnamed x10, local copies, waits for them, and re-layouts: 2.94 us -> 0.02 us
    pallas_call x5 -> x6, Pallas kernels: 10.2 us -> 11.2 us  [call(): pl.pallas_call(kernel, out_shape=[jax.ShapeDtypeStruct(shape, kind) for s...]
    ppermute x4 -> x5, starting transfers between devices: 4.04 us -> 3.51 us  [facing(): return lax.ppermute(values, AXES, across)]
  transfers between devices with their start and end apart: 11 -> 12, of which waited for: 1 -> 1; matrix products, arithmetic and copies ran while one was open for 0% -> 0% of each run, Pallas kernels for 2% -> 11%
where the time goes in v4:
time: 62.5 us; the launch traced here: 62.2 us
  starting transfers between devices  24.4 us (39%)
  blocking collectives  22.9 us (37%)
  Pallas kernels  13.9 us (22%)
  between operations  0.79 us (1%)
    all_to_all x2, blocking collectives, exchanged(): lax.all_to_all(spread, AXES, 0, 0, tiled=True).reshape(devices, LANES)  22.9 us
    ppermute x7, starting transfers between devices, mate(): return lax.ppermute(values, AXES, swap)  20.9 us
    pallas_call x6, Pallas kernels, call(): pl.pallas_call(kernel, out_shape=[jax.ShapeDtypeStruct(shape, kind) for s...  11.2 us
    ppermute x5, starting transfers between devices, facing(): return lax.ppermute(values, AXES, across)  3.51 us
    pallas_call x1, Pallas kernels, one_sector_body(): pl.pallas_call(picking_kernel, out_shape=[jax.ShapeDtypeStruct(shape, f32...  2.7 us
  transfers between devices with their start and end apart: 12, of which 1 were waited for; matrix products, arithmetic and copies ran while one was open for 0% of the time, Pallas kernels for 11%

profile of v4, /device:TPU:0, one launch (start us, length us, event | category | flops | bytes accessed | tf_op | source)
XLA Modules:
  0.0 62.2 jit_solution(2752580198387626782)
XLA Ops:
  0.7 2.7 %shard_map.68 = (f32[256,256]{1,0:T(8,128)}, f32[256,256]{1,0:T(8,128)}, f32[2,256,256]{2,1,0:T(8,128)}, f32[2,256,256]{2,1,0:T(8,128)}) custom-call(f32[2,256,256]{2,1,0:T(8,128)} %wave.3, f32[2,256,256]{2,1,0:T(8,128)} %preconditioner.3, f32[2,2,256,256]{3,2,1,0:T(8,128)} %own_left.1, f32[2,2,256,256]{3,2,1,0:T(8,128)} %own_right.1), custom_call_target="tpu_custom_call" | custom-call | tf_op jit(solution)/shard_map/pallas_call | solution.py:408
  3.4 0.5 collective-permute-start.2
  3.9 0.1 collective-permute-start.3
  4.0 0.8 %collective-permute-start.1 = (f32[256,256]{1,0:T(8,128)}, f32[256,256]{1,0:T(8,128)S(1)}, u32[]{:S(2)}, u32[]{:S(2)}) collective-permute-start(f32[256,256]{1,0:T(8,128)} %get-tuple-element.28), channel_id=1, source_target_pairs={{1,2},{3,4},{5,6},{7,8},{9,10},{11,12},{13,14},{15,16},{17,18},{19... | collective-permute-start | bytes 786440 | tf_op jit(solution)/shard_map/ppermute | solution.py:381
  4.8 0.7 %collective-permute-start.6 = (f32[256,256]{1,0:T(8,128)}, f32[256,256]{1,0:T(8,128)S(1)}, u32[]{:S(2)}, u32[]{:S(2)}) collective-permute-start(f32[256,256]{1,0:T(8,128)} %get-tuple-element.38), channel_id=1, source_target_pairs={{1,2},{3,4},{5,6},{7,8},{9,10},{11,12},{13,14},{15,16},{17,18},{19... | collective-permute-start | bytes 786440 | tf_op jit(solution)/shard_map/ppermute | solution.py:381
  5.5 5.6 %collective-permute-start = (s32[2]{0:T(128)S(1)}, s32[2]{0:T(128)S(1)}, u32[]{:S(2)}, u32[]{:S(2)}) collective-permute-start(s32[2]{0:T(128)S(1)} %copy-done.4), channel_id=1, source_target_pairs={{0,1},{1,0},{2,3},{3,2},{4,5},{5,4},{6,7},{7,6},{8,9},{9,8},{10,11... | collective-permute-start | bytes 32 | tf_op jit(solution)/shard_map/ppermute | solution.py:378
  11.0 0.0 collective-permute-done.1.facing_wave
  11.0 0.0 collective-permute-done.2.mate_left
  11.0 0.0 collective-permute-done.3.mate_right
  11.1 0.6 %shard_map.69 = (f32[3,256,256]{2,1,0:T(8,128)S(1)}, bf16[3,256,256]{2,1,0:T(8,128)(2,1)S(1)}, bf16[3,256,256]{2,1,0:T(8,128)(2,1)S(1)}, bf16[4,256,256]{2,1,0:T...) custom-call(f32[2,256,256]{2,1,0:T(8,128)S(1)} %copy-done.2, ...), custom_call_target="tpu_custom_call" | custom-call | tf_op jit(solution)/shard_map/pallas_call | solution.py:394
  11.7 0.1 collective-permute-done.mate_shifts
  11.9 1.8 %shard_map.70.image.own_image = f32[256,256]{1,0:T(8,128)S(1)} custom-call(s32[2]{0:T(128)S(1)} %copy-done.4, s32[2]{0:T(128)S(1)} %collective-permute-done.mate_shifts, bf16[3,256,256]{2,1,0:T(8,128)(2,1)S(1)} %get-tuple-element.32.high, bf16[3,256,256]{2,1,0:T(8,128)(2,1)S(1)} %get-tuple-element.33.low, ...), custom_call_target="tpu_custom_call" | custom-call | tf_op jit(solution)/shard_map/pallas_call | solution.py:394
  13.6 0.7 %collective-permute-start.5 = (f32[256,256]{1,0:T(8,128)S(1)}, f32[256,256]{1,0:T(8,128)S(1)}, u32[]{:S(2)}, u32[]{:S(2)}) collective-permute-start(f32[256,256]{1,0:T(8,128)S(1)} %shard_map.70.image.own_image), channel_id=1, source_target_pairs={{1,2},{3,4},{5,6},{7,8},{9,10},{11,12},{13,14},{15,16},{17,18},{19... | collective-permute-start | bytes 786440 | tf_op jit(solution)/shard_map/ppermute | solution.py:381
  14.3 8.0 %collective-permute-start.4 = (f32[256,256]{1,0:T(8,128)S(1)}, f32[256,256]{1,0:T(8,128)S(1)}, u32[]{:S(2)}, u32[]{:S(2)}) collective-permute-start(f32[256,256]{1,0:T(8,128)S(1)} %shard_map.70.image.own_image), channel_id=1, source_target_pairs={{0,1},{1,0},{2,3},{3,2},{4,5},{5,4},{6,7},{7,6},{8,9},{9,8},{10,11... | collective-permute-start | bytes 786440 | tf_op jit(solution)/shard_map/ppermute | solution.py:378
  22.3 0.0 collective-permute-done.6.facing_preconditioner
  22.3 2.4 %shard_map.71 = (f32[256,256]{1,0:T(8,128)S(1)}, f32[1,128]{1,0:T(1,128)S(1)}, f32[3,256,256]{2,1,0:T(8,128)S(1)}) custom-call(s32[2]{0:T(128)S(1)} %copy-done.4, s32[2]{0:T(128)S(1)} %collective-permute-done.mate_shifts, f32[3,256,256]{2,1,0:T(8,128)S(1)} %get-tuple-element.31.start, f32[2,256,256]{2,1,0:T(8,128)S(1)} %copy-done.3, ...), custom_call_target="tpu_custom_call" | custom-call | tf_op jit(solution)/shard_map/pallas_call | solution.py:394
  24.7 0.7 %collective-permute-start.8 = (f32[256,256]{1,0:T(8,128)S(1)}, f32[256,256]{1,0:T(8,128)S(1)}, u32[]{:S(2)}, u32[]{:S(2)}) collective-permute-start(f32[256,256]{1,0:T(8,128)S(1)} %get-tuple-element.45.side.own_side), channel_id=1, source_target_pairs={{1,2},{3,4},{5,6},{7,8},{9,10},{11,12},{13,14},{15,16},{17,18},{19... | collective-permute-start | bytes 786440 | tf_op jit(solution)/shard_map/ppermute | solution.py:381
  25.4 3.8 %collective-permute-start.7 = (f32[256,256]{1,0:T(8,128)S(1)}, f32[256,256]{1,0:T(8,128)S(1)}, u32[]{:S(2)}, u32[]{:S(2)}) collective-permute-start(f32[256,256]{1,0:T(8,128)S(1)} %get-tuple-element.45.side.own_side), channel_id=1, source_target_pairs={{0,1},{1,0},{2,3},{3,2},{4,5},{5,4},{6,7},{7,6},{8,9},{9,8},{10,11... | collective-permute-start | bytes 786440 | tf_op jit(solution)/shard_map/ppermute | solution.py:378
  29.2 0.0 collective-permute-done.5.facing_image
  29.2 0.0 collective-permute-done.4.mate_image
  29.2 2.2 %shard_map.72 = (f32[256,256]{1,0:T(8,128)S(1)}, f32[32,128]{1,0:T(8,128)S(1)}, f32[3,256,256]{2,1,0:T(8,128)S(1)}) custom-call(s32[2]{0:T(128)S(1)} %copy-done.4, s32[2]{0:T(128)S(1)} %collective-permute-done.mate_shifts, f32[3,256,256]{2,1,0:T(8,128)S(1)} %get-tuple-element.31.start, f32[256,256]{1,0:T(8,128)S(1)} %shard_map.70.image.own_image, ...), custom_call_target="tpu_custom_call" | custom-call | tf_op jit(solution)/shard_map/pallas_call | solution.py:394
  31.4 0.7 %collective-permute-start.10 = (f32[256,256]{1,0:T(8,128)S(1)}, f32[256,256]{1,0:T(8,128)S(1)}, u32[]{:S(2)}, u32[]{:S(2)}) collective-permute-start(f32[256,256]{1,0:T(8,128)S(1)} %get-tuple-element.48.own_second), channel_id=1, source_target_pairs={{1,2},{3,4},{5,6},{7,8},{9,10},{11,12},{13,14},{15,16},{17,18},{19... | collective-permute-start | bytes 786440 | tf_op jit(solution)/shard_map/ppermute | solution.py:381
  32.0 2.9 %collective-permute-start.9 = (f32[256,256]{1,0:T(8,128)S(1)}, f32[256,256]{1,0:T(8,128)S(1)}, u32[]{:S(2)}, u32[]{:S(2)}) collective-permute-start(f32[256,256]{1,0:T(8,128)S(1)} %get-tuple-element.48.own_second), channel_id=1, source_target_pairs={{0,1},{1,0},{2,3},{3,2},{4,5},{5,4},{6,7},{7,6},{8,9},{9,8},{10,11... | collective-permute-start | bytes 786440 | tf_op jit(solution)/shard_map/ppermute | solution.py:378
  35.0 0.0 collective-permute-done.8.facing_side
  35.0 0.0 collective-permute-done.7.mate_side
  35.0 14.1 %all_to_all.10 = f32[32,1,128]{2,1,0:T(1,128)S(1)} all-to-all(f32[32,1,128]{2,1,0:T(1,128)S(1)} %bitcast.11), channel_id=1, replica_groups=mesh['sector'=16,'op'=2] {'sector','op'}, dimensions={0} | all-to-all | bytes 32768 | tf_op jit(solution)/shard_map/all_to_all | solution.py:388
  49.0 0.0 collective-permute-done.10.facing_second
  49.0 3.1 %shard_map.73 = (f32[128,256]{1,0:T(8,128)S(1)}, f32[128,256]{1,0:T(8,128)S(1)}, f32[32,128]{1,0:T(8,128)S(1)}, f32[3,2,128,256]{3,2,1,0:T(8,128)S(1)}, f32[2,8,128]{2,1,0:T(8,128)S(1)}) custom-call(s32[2]{0:T(128)S(1)} %copy-done.4, s32[2]{0:T(128)S(1)} %collective-permute-done.mate_shifts, f32[32,128]{1,0:T(8,128)S(1)} %bitcast.8, ...), custom_call_target="tpu_custom_call" | custom-call | tf_op jit(solution)/shard_map/pallas_call | solution.py:394
  52.1 0.1 collective-permute-start.11
  52.2 8.8 %all_to_all.11 = f32[32,1,128]{2,1,0:T(1,128)S(1)} all-to-all(f32[32,1,128]{2,1,0:T(1,128)S(1)} %bitcast.10), channel_id=1, replica_groups=mesh['sector'=16,'op'=2] {'sector','op'}, dimensions={0} | all-to-all | bytes 32768 | tf_op jit(solution)/shard_map/all_to_all | solution.py:388
  61.1 0.0 collective-permute-done.11.mate_image
  61.1 1.1 %shard_map.74 = (f32[3,2,128,256]{3,2,1,0:T(8,128)}, f32[3]{0:T(128)}) custom-call(f32[32,128]{1,0:T(8,128)S(1)} %bitcast.9, f32[2,8,128]{2,1,0:T(8,128)S(1)} %get-tuple-element.50.thetas, f32[3,2,128,256]{3,2,1,0:T(8,128)S(1)} %get-tuple-element.51.members, f32[3,256,256]{2,1,0:T(8,128)S(1)} %get-tuple-element.39.inverse, ...), custom_call_target="tpu_custom_call" | custom-call | tf_op jit(solution)/shard_map/pallas_call | solution.py:394
  (11 shorter events, 0.0 us)
Async XLA Ops:
  0.6 10.4 %copy-start.1 = (f32[2,2,256,256]{3,2,1,0:T(8,128)S(1)}, f32[2,2,256,256]{3,2,1,0:T(8,128)}, u32[]{:S(2)}) copy-start(f32[2,2,256,256]{3,2,1,0:T(8,128)} %own_right.1) | copy-start | bytes 3145732
  0.6 10.4 %copy-start = (f32[2,2,256,256]{3,2,1,0:T(8,128)S(1)}, f32[2,2,256,256]{3,2,1,0:T(8,128)}, u32[]{:S(2)}) copy-start(f32[2,2,256,256]{3,2,1,0:T(8,128)} %own_left.1) | copy-start | bytes 3145732
  0.6 10.4 %copy-start.2 = (f32[2,256,256]{2,1,0:T(8,128)S(1)}, f32[2,256,256]{2,1,0:T(8,128)}, u32[]{:S(2)}) copy-start(f32[2,256,256]{2,1,0:T(8,128)} %wave.3) | copy-start | bytes 1572868
  3.4 7.7 %collective-permute-start.2 = (f32[2,256,256]{2,1,0:T(8,128)}, f32[2,256,256]{2,1,0:T(8,128)S(1)}, u32[]{:S(2)}, u32[]{:S(2)}) collective-permute-start(f32[2,256,256]{2,1,0:T(8,128)} %get-tuple-element.29), channel_id=1, source_target_pairs={{0,1},{1,0},{2,3},{3,2},{4,5},{5,4},{6,7},{7,6},{8,9},{9,8},{10,11... | collective-permute-start | bytes 1572872 | tf_op jit(solution)/shard_map/ppermute | solution.py:378
  3.9 7.2 %collective-permute-start.3 = (f32[2,256,256]{2,1,0:T(8,128)}, f32[2,256,256]{2,1,0:T(8,128)S(1)}, u32[]{:S(2)}, u32[]{:S(2)}) collective-permute-start(f32[2,256,256]{2,1,0:T(8,128)} %get-tuple-element.30), channel_id=1, source_target_pairs={{0,1},{1,0},{2,3},{3,2},{4,5},{5,4},{6,7},{7,6},{8,9},{9,8},{10,11... | collective-permute-start | bytes 1572872 | tf_op jit(solution)/shard_map/ppermute | solution.py:378
  4.0 1.5 %copy-start.4 = (s32[2]{0:T(128)S(1)}, s32[2]{0:T(128)}, u32[]{:S(2)}) copy-start(s32[2]{0:T(128)} %own_shifts.7) | copy-start | bytes 28
  4.0 7.1 %collective-permute-start.1 = (f32[256,256]{1,0:T(8,128)}, f32[256,256]{1,0:T(8,128)S(1)}, u32[]{:S(2)}, u32[]{:S(2)}) collective-permute-start(f32[256,256]{1,0:T(8,128)} %get-tuple-element.28), channel_id=1, source_target_pairs={{1,2},{3,4},{5,6},{7,8},{9,10},{11,12},{13,14},{15,16},{17,18},{19... | collective-permute-start | bytes 786440 | tf_op jit(solution)/shard_map/ppermute | solution.py:381
  4.8 17.5 %collective-permute-start.6 = (f32[256,256]{1,0:T(8,128)}, f32[256,256]{1,0:T(8,128)S(1)}, u32[]{:S(2)}, u32[]{:S(2)}) collective-permute-start(f32[256,256]{1,0:T(8,128)} %get-tuple-element.38), channel_id=1, source_target_pairs={{1,2},{3,4},{5,6},{7,8},{9,10},{11,12},{13,14},{15,16},{17,18},{19... | collective-permute-start | bytes 786440 | tf_op jit(solution)/shard_map/ppermute | solution.py:381
  5.5 6.4 %collective-permute-start = (s32[2]{0:T(128)S(1)}, s32[2]{0:T(128)S(1)}, u32[]{:S(2)}, u32[]{:S(2)}) collective-permute-start(s32[2]{0:T(128)S(1)} %copy-done.4), channel_id=1, source_target_pairs={{0,1},{1,0},{2,3},{3,2},{4,5},{5,4},{6,7},{7,6},{8,9},{9,8},{10,11... | collective-permute-start | bytes 32 | tf_op jit(solution)/shard_map/ppermute | solution.py:378
  11.9 10.4 %copy-start.3 = (f32[2,256,256]{2,1,0:T(8,128)S(1)}, f32[2,256,256]{2,1,0:T(8,128)}, u32[]{:S(2)}) copy-start(f32[2,256,256]{2,1,0:T(8,128)} %preconditioner.3) | copy-start | bytes 1572868
  13.6 15.6 %collective-permute-start.5 = (f32[256,256]{1,0:T(8,128)S(1)}, f32[256,256]{1,0:T(8,128)S(1)}, u32[]{:S(2)}, u32[]{:S(2)}) collective-permute-start(f32[256,256]{1,0:T(8,128)S(1)} %shard_map.70.image.own_image), channel_id=1, source_target_pairs={{1,2},{3,4},{5,6},{7,8},{9,10},{11,12},{13,14},{15,16},{17,18},{19... | collective-permute-start | bytes 786440 | tf_op jit(solution)/shard_map/ppermute | solution.py:381
  14.3 14.9 %collective-permute-start.4 = (f32[256,256]{1,0:T(8,128)S(1)}, f32[256,256]{1,0:T(8,128)S(1)}, u32[]{:S(2)}, u32[]{:S(2)}) collective-permute-start(f32[256,256]{1,0:T(8,128)S(1)} %shard_map.70.image.own_image), channel_id=1, source_target_pairs={{0,1},{1,0},{2,3},{3,2},{4,5},{5,4},{6,7},{7,6},{8,9},{9,8},{10,11... | collective-permute-start | bytes 786440 | tf_op jit(solution)/shard_map/ppermute | solution.py:378
  24.7 10.2 %collective-permute-start.8 = (f32[256,256]{1,0:T(8,128)S(1)}, f32[256,256]{1,0:T(8,128)S(1)}, u32[]{:S(2)}, u32[]{:S(2)}) collective-permute-start(f32[256,256]{1,0:T(8,128)S(1)} %get-tuple-element.45.side.own_side), channel_id=1, source_target_pairs={{1,2},{3,4},{5,6},{7,8},{9,10},{11,12},{13,14},{15,16},{17,18},{19... | collective-permute-start | bytes 786440 | tf_op jit(solution)/shard_map/ppermute | solution.py:381
  25.4 9.5 %collective-permute-start.7 = (f32[256,256]{1,0:T(8,128)S(1)}, f32[256,256]{1,0:T(8,128)S(1)}, u32[]{:S(2)}, u32[]{:S(2)}) collective-permute-start(f32[256,256]{1,0:T(8,128)S(1)} %get-tuple-element.45.side.own_side), channel_id=1, source_target_pairs={{0,1},{1,0},{2,3},{3,2},{4,5},{5,4},{6,7},{7,6},{8,9},{9,8},{10,11... | collective-permute-start | bytes 786440 | tf_op jit(solution)/shard_map/ppermute | solution.py:378
  31.4 17.7 %collective-permute-start.10 = (f32[256,256]{1,0:T(8,128)S(1)}, f32[256,256]{1,0:T(8,128)S(1)}, u32[]{:S(2)}, u32[]{:S(2)}) collective-permute-start(f32[256,256]{1,0:T(8,128)S(1)} %get-tuple-element.48.own_second), channel_id=1, source_target_pairs={{1,2},{3,4},{5,6},{7,8},{9,10},{11,12},{13,14},{15,16},{17,18},{19... | collective-permute-start | bytes 786440 | tf_op jit(solution)/shard_map/ppermute | solution.py:381
  32.0 17.0 %collective-permute-start.9 = (f32[256,256]{1,0:T(8,128)S(1)}, f32[256,256]{1,0:T(8,128)S(1)}, u32[]{:S(2)}, u32[]{:S(2)}) collective-permute-start(f32[256,256]{1,0:T(8,128)S(1)} %get-tuple-element.48.own_second), channel_id=1, source_target_pairs={{0,1},{1,0},{2,3},{3,2},{4,5},{5,4},{6,7},{7,6},{8,9},{9,8},{10,11... | collective-permute-start | bytes 786440 | tf_op jit(solution)/shard_map/ppermute | solution.py:378
  52.1 8.9 %collective-permute-start.11 = (f32[128,256]{1,0:T(8,128)S(1)}, f32[128,256]{1,0:T(8,128)S(1)}, u32[]{:S(2)}, u32[]{:S(2)}) collective-permute-start(f32[128,256]{1,0:T(8,128)S(1)} %get-tuple-element.53), channel_id=1, source_target_pairs={{0,1},{1,0},{2,3},{3,2},{4,5},{5,4},{6,7},{7,6},{8,9},{9,8},{10,11... | collective-permute-start | bytes 393224 | tf_op jit(solution)/shard_map/ppermute | solution.py:378

commit v5 on v4

--- a/solution.py
+++ b/solution.py
@@ -411,7 +411,7 @@
         in_specs=[pl.BlockSpec(memory_space=pl.ANY)] * 4,
         out_specs=[vmem] * 4,
         scratch_shapes=[pltpu.SemaphoreType.DMA((2 + terms,))],
-        compiler_params=pltpu.CompilerParams(vmem_limit_bytes=56 * 2**20),
+        compiler_params=pltpu.CompilerParams(vmem_limit_bytes=52 * 2**20),
     )(wave_start, preconditioner, left_blocks, right_blocks)
     facing_wave = facing(own_wave)
     facing_preconditioner = facing(own_preconditioner)

time: 62.5 us -> 61.1 us (0.978)
  Pallas kernels: 13.9 us -> 12.8 us
    pallas_call x1, Pallas kernels: 2.7 us -> 1.55 us  [one_sector_body(): pl.pallas_call(picking_kernel, out_shape=[jax.ShapeDtypeStruct(shape, f32...]
where the time goes in v5:
time: 61.1 us; the launch traced here: 60.9 us
  starting transfers between devices  24.2 us (40%)
  blocking collectives  22.9 us (37%)
  Pallas kernels  12.8 us (21%)
  between operations  0.79 us (1%)
    all_to_all x2, blocking collectives, exchanged(): lax.all_to_all(spread, AXES, 0, 0, tiled=True).reshape(devices, LANES)  22.9 us
    ppermute x7, starting transfers between devices, mate(): return lax.ppermute(values, AXES, swap)  20.7 us
    pallas_call x6, Pallas kernels, call(): pl.pallas_call(kernel, out_shape=[jax.ShapeDtypeStruct(shape, kind) for s...  11.2 us
    ppermute x5, starting transfers between devices, facing(): return lax.ppermute(values, AXES, across)  3.51 us
    pallas_call x1, Pallas kernels, one_sector_body(): pl.pallas_call(picking_kernel, out_shape=[jax.ShapeDtypeStruct(shape, f32...  1.55 us
  transfers between devices with their start and end apart: 12, of which 1 were waited for; matrix products, arithmetic and copies ran while one was open for 0% of the time, Pallas kernels for 11%

profile of v5, /device:TPU:0, one launch (start us, length us, event | category | flops | bytes accessed | tf_op | source)
XLA Modules:
  0.0 60.9 jit_solution(11435040722092818790)
XLA Ops:
  0.7 1.6 %shard_map.68 = (f32[256,256]{1,0:T(8,128)S(1)}, f32[256,256]{1,0:T(8,128)S(1)}, f32[2,256,256]{2,1,0:T(8,128)S(1)}, f32[2,256,256]{2,1,0:T(8,128)S(1)}) custom-call(f32[2,256,256]{2,1,0:T(8,128)} %wave.3, f32[2,256,256]{2,1,0:T(8,128)} %preconditioner.3, f32[2,2,256,256]{3,2,1,0:T(8,128)} %own_left.1, f32[2,2,256,256]{3,2,1,0:T(8,128)} %own_right.1), custom_call_target="tpu_custom_call" | custom-call | tf_op jit(solution)/shard_map/pallas_call | solution.py:408
  2.2 0.5 collective-permute-start.2
  2.7 0.1 collective-permute-start.3
  2.8 0.8 %collective-permute-start.1 = (f32[256,256]{1,0:T(8,128)S(1)}, f32[256,256]{1,0:T(8,128)S(1)}, u32[]{:S(2)}, u32[]{:S(2)}) collective-permute-start(f32[256,256]{1,0:T(8,128)S(1)} %get-tuple-element.28), channel_id=1, source_target_pairs={{1,2},{3,4},{5,6},{7,8},{9,10},{11,12},{13,14},{15,16},{17,18},{19... | collective-permute-start | bytes 786440 | tf_op jit(solution)/shard_map/ppermute | solution.py:381
  3.6 0.7 %collective-permute-start.6 = (f32[256,256]{1,0:T(8,128)S(1)}, f32[256,256]{1,0:T(8,128)S(1)}, u32[]{:S(2)}, u32[]{:S(2)}) collective-permute-start(f32[256,256]{1,0:T(8,128)S(1)} %get-tuple-element.38), channel_id=1, source_target_pairs={{1,2},{3,4},{5,6},{7,8},{9,10},{11,12},{13,14},{15,16},{17,18},{19... | collective-permute-start | bytes 786440 | tf_op jit(solution)/shard_map/ppermute | solution.py:381
  4.3 5.6 %collective-permute-start = (s32[2]{0:T(128)S(1)}, s32[2]{0:T(128)S(1)}, u32[]{:S(2)}, u32[]{:S(2)}) collective-permute-start(s32[2]{0:T(128)S(1)} %copy-done.4), channel_id=1, source_target_pairs={{0,1},{1,0},{2,3},{3,2},{4,5},{5,4},{6,7},{7,6},{8,9},{9,8},{10,11... | collective-permute-start | bytes 32 | tf_op jit(solution)/shard_map/ppermute | solution.py:378
  9.9 0.0 collective-permute-done.1.facing_wave
  9.9 0.0 collective-permute-done.2.mate_left
  9.9 0.0 collective-permute-done.3.mate_right
  9.9 0.6 %shard_map.69 = (f32[3,256,256]{2,1,0:T(8,128)S(1)}, bf16[3,256,256]{2,1,0:T(8,128)(2,1)S(1)}, bf16[3,256,256]{2,1,0:T(8,128)(2,1)S(1)}, bf16[4,256,256]{2,1,0:T...) custom-call(f32[2,256,256]{2,1,0:T(8,128)S(1)} %copy-done.2, ...), custom_call_target="tpu_custom_call" | custom-call | tf_op jit(solution)/shard_map/pallas_call | solution.py:394
  10.6 0.1 collective-permute-done.mate_shifts
  10.7 1.8 %shard_map.70.image.own_image = f32[256,256]{1,0:T(8,128)S(1)} custom-call(s32[2]{0:T(128)S(1)} %copy-done.4, s32[2]{0:T(128)S(1)} %collective-permute-done.mate_shifts, bf16[3,256,256]{2,1,0:T(8,128)(2,1)S(1)} %get-tuple-element.32.high, bf16[3,256,256]{2,1,0:T(8,128)(2,1)S(1)} %get-tuple-element.33.low, ...), custom_call_target="tpu_custom_call" | custom-call | tf_op jit(solution)/shard_map/pallas_call | solution.py:394
  12.5 0.7 %collective-permute-start.5 = (f32[256,256]{1,0:T(8,128)S(1)}, f32[256,256]{1,0:T(8,128)S(1)}, u32[]{:S(2)}, u32[]{:S(2)}) collective-permute-start(f32[256,256]{1,0:T(8,128)S(1)} %shard_map.70.image.own_image), channel_id=1, source_target_pairs={{1,2},{3,4},{5,6},{7,8},{9,10},{11,12},{13,14},{15,16},{17,18},{19... | collective-permute-start | bytes 786440 | tf_op jit(solution)/shard_map/ppermute | solution.py:381
  13.2 7.8 %collective-permute-start.4 = (f32[256,256]{1,0:T(8,128)S(1)}, f32[256,256]{1,0:T(8,128)S(1)}, u32[]{:S(2)}, u32[]{:S(2)}) collective-permute-start(f32[256,256]{1,0:T(8,128)S(1)} %shard_map.70.image.own_image), channel_id=1, source_target_pairs={{0,1},{1,0},{2,3},{3,2},{4,5},{5,4},{6,7},{7,6},{8,9},{9,8},{10,11... | collective-permute-start | bytes 786440 | tf_op jit(solution)/shard_map/ppermute | solution.py:378
  20.9 0.0 collective-permute-done.6.facing_preconditioner
  20.9 2.4 %shard_map.71 = (f32[256,256]{1,0:T(8,128)S(1)}, f32[1,128]{1,0:T(1,128)S(1)}, f32[3,256,256]{2,1,0:T(8,128)S(1)}) custom-call(s32[2]{0:T(128)S(1)} %copy-done.4, s32[2]{0:T(128)S(1)} %collective-permute-done.mate_shifts, f32[3,256,256]{2,1,0:T(8,128)S(1)} %get-tuple-element.31.start, f32[2,256,256]{2,1,0:T(8,128)S(1)} %copy-done.3, ...), custom_call_target="tpu_custom_call" | custom-call | tf_op jit(solution)/shard_map/pallas_call | solution.py:394
  23.4 0.7 %collective-permute-start.8 = (f32[256,256]{1,0:T(8,128)S(1)}, f32[256,256]{1,0:T(8,128)S(1)}, u32[]{:S(2)}, u32[]{:S(2)}) collective-permute-start(f32[256,256]{1,0:T(8,128)S(1)} %get-tuple-element.45.side.own_side), channel_id=1, source_target_pairs={{1,2},{3,4},{5,6},{7,8},{9,10},{11,12},{13,14},{15,16},{17,18},{19... | collective-permute-start | bytes 786440 | tf_op jit(solution)/shard_map/ppermute | solution.py:381
  24.1 3.8 %collective-permute-start.7 = (f32[256,256]{1,0:T(8,128)S(1)}, f32[256,256]{1,0:T(8,128)S(1)}, u32[]{:S(2)}, u32[]{:S(2)}) collective-permute-start(f32[256,256]{1,0:T(8,128)S(1)} %get-tuple-element.45.side.own_side), channel_id=1, source_target_pairs={{0,1},{1,0},{2,3},{3,2},{4,5},{5,4},{6,7},{7,6},{8,9},{9,8},{10,11... | collective-permute-start | bytes 786440 | tf_op jit(solution)/shard_map/ppermute | solution.py:378
  27.8 0.0 collective-permute-done.5.facing_image
  27.8 0.0 collective-permute-done.4.mate_image
  27.8 2.2 %shard_map.72 = (f32[256,256]{1,0:T(8,128)S(1)}, f32[32,128]{1,0:T(8,128)S(1)}, f32[3,256,256]{2,1,0:T(8,128)S(1)}) custom-call(s32[2]{0:T(128)S(1)} %copy-done.4, s32[2]{0:T(128)S(1)} %collective-permute-done.mate_shifts, f32[3,256,256]{2,1,0:T(8,128)S(1)} %get-tuple-element.31.start, f32[256,256]{1,0:T(8,128)S(1)} %shard_map.70.image.own_image, ...), custom_call_target="tpu_custom_call" | custom-call | tf_op jit(solution)/shard_map/pallas_call | solution.py:394
  30.0 0.7 %collective-permute-start.10 = (f32[256,256]{1,0:T(8,128)S(1)}, f32[256,256]{1,0:T(8,128)S(1)}, u32[]{:S(2)}, u32[]{:S(2)}) collective-permute-start(f32[256,256]{1,0:T(8,128)S(1)} %get-tuple-element.48.own_second), channel_id=1, source_target_pairs={{1,2},{3,4},{5,6},{7,8},{9,10},{11,12},{13,14},{15,16},{17,18},{19... | collective-permute-start | bytes 786440 | tf_op jit(solution)/shard_map/ppermute | solution.py:381
  30.7 2.9 %collective-permute-start.9 = (f32[256,256]{1,0:T(8,128)S(1)}, f32[256,256]{1,0:T(8,128)S(1)}, u32[]{:S(2)}, u32[]{:S(2)}) collective-permute-start(f32[256,256]{1,0:T(8,128)S(1)} %get-tuple-element.48.own_second), channel_id=1, source_target_pairs={{0,1},{1,0},{2,3},{3,2},{4,5},{5,4},{6,7},{7,6},{8,9},{9,8},{10,11... | collective-permute-start | bytes 786440 | tf_op jit(solution)/shard_map/ppermute | solution.py:378
  33.6 0.0 collective-permute-done.8.facing_side
  33.6 0.0 collective-permute-done.7.mate_side
  33.6 14.1 %all_to_all.10 = f32[32,1,128]{2,1,0:T(1,128)S(1)} all-to-all(f32[32,1,128]{2,1,0:T(1,128)S(1)} %bitcast.11), channel_id=1, replica_groups=mesh['sector'=16,'op'=2] {'sector','op'}, dimensions={0} | all-to-all | bytes 32768 | tf_op jit(solution)/shard_map/all_to_all | solution.py:388
  47.7 0.0 collective-permute-done.9.mate_second
  47.7 3.1 %shard_map.73 = (f32[128,256]{1,0:T(8,128)S(1)}, f32[128,256]{1,0:T(8,128)S(1)}, f32[32,128]{1,0:T(8,128)S(1)}, f32[3,2,128,256]{3,2,1,0:T(8,128)S(1)}, f32[2,8,128]{2,1,0:T(8,128)S(1)}) custom-call(s32[2]{0:T(128)S(1)} %copy-done.4, s32[2]{0:T(128)S(1)} %collective-permute-done.mate_shifts, f32[32,128]{1,0:T(8,128)S(1)} %bitcast.8, ...), custom_call_target="tpu_custom_call" | custom-call | tf_op jit(solution)/shard_map/pallas_call | solution.py:394
  50.8 0.1 collective-permute-start.11
  50.9 8.8 %all_to_all.11 = f32[32,1,128]{2,1,0:T(1,128)S(1)} all-to-all(f32[32,1,128]{2,1,0:T(1,128)S(1)} %bitcast.10), channel_id=1, replica_groups=mesh['sector'=16,'op'=2] {'sector','op'}, dimensions={0} | all-to-all | bytes 32768 | tf_op jit(solution)/shard_map/all_to_all | solution.py:388
  59.7 0.0 collective-permute-done.11.mate_image
  59.7 1.1 %shard_map.74 = (f32[3,2,128,256]{3,2,1,0:T(8,128)}, f32[3]{0:T(128)}) custom-call(f32[32,128]{1,0:T(8,128)S(1)} %bitcast.9, f32[2,8,128]{2,1,0:T(8,128)S(1)} %get-tuple-element.50.thetas, f32[3,2,128,256]{3,2,1,0:T(8,128)S(1)} %get-tuple-element.51.members, f32[3,256,256]{2,1,0:T(8,128)S(1)} %get-tuple-element.39.inverse, ...), custom_call_target="tpu_custom_call" | custom-call | tf_op jit(solution)/shard_map/pallas_call | solution.py:394
  (11 shorter events, 0.0 us)
Async XLA Ops:
  0.6 9.3 %copy-start.1 = (f32[2,2,256,256]{3,2,1,0:T(8,128)S(1)}, f32[2,2,256,256]{3,2,1,0:T(8,128)}, u32[]{:S(2)}) copy-start(f32[2,2,256,256]{3,2,1,0:T(8,128)} %own_right.1) | copy-start | bytes 3145732
  0.6 9.3 %copy-start = (f32[2,2,256,256]{3,2,1,0:T(8,128)S(1)}, f32[2,2,256,256]{3,2,1,0:T(8,128)}, u32[]{:S(2)}) copy-start(f32[2,2,256,256]{3,2,1,0:T(8,128)} %own_left.1) | copy-start | bytes 3145732
  0.6 9.3 %copy-start.2 = (f32[2,256,256]{2,1,0:T(8,128)S(1)}, f32[2,256,256]{2,1,0:T(8,128)}, u32[]{:S(2)}) copy-start(f32[2,256,256]{2,1,0:T(8,128)} %wave.3) | copy-start | bytes 1572868
  2.2 7.7 %collective-permute-start.2 = (f32[2,256,256]{2,1,0:T(8,128)S(1)}, f32[2,256,256]{2,1,0:T(8,128)S(1)}, u32[]{:S(2)}, u32[]{:S(2)}) collective-permute-start(f32[2,256,256]{2,1,0:T(8,128)S(1)} %get-tuple-element.29), channel_id=1, source_target_pairs={{0,1},{1,0},{2,3},{3,2},{4,5},{5,4},{6,7},{7,6},{8,9},{9,8},{10,11... | collective-permute-start | bytes 1572872 | tf_op jit(solution)/shard_map/ppermute | solution.py:378
  2.7 7.2 %collective-permute-start.3 = (f32[2,256,256]{2,1,0:T(8,128)S(1)}, f32[2,256,256]{2,1,0:T(8,128)S(1)}, u32[]{:S(2)}, u32[]{:S(2)}) collective-permute-start(f32[2,256,256]{2,1,0:T(8,128)S(1)} %get-tuple-element.30), channel_id=1, source_target_pairs={{0,1},{1,0},{2,3},{3,2},{4,5},{5,4},{6,7},{7,6},{8,9},{9,8},{10,11... | collective-permute-start | bytes 1572872 | tf_op jit(solution)/shard_map/ppermute | solution.py:378
  2.8 1.5 %copy-start.4 = (s32[2]{0:T(128)S(1)}, s32[2]{0:T(128)}, u32[]{:S(2)}) copy-start(s32[2]{0:T(128)} %own_shifts.7) | copy-start | bytes 28
  2.8 7.1 %collective-permute-start.1 = (f32[256,256]{1,0:T(8,128)S(1)}, f32[256,256]{1,0:T(8,128)S(1)}, u32[]{:S(2)}, u32[]{:S(2)}) collective-permute-start(f32[256,256]{1,0:T(8,128)S(1)} %get-tuple-element.28), channel_id=1, source_target_pairs={{1,2},{3,4},{5,6},{7,8},{9,10},{11,12},{13,14},{15,16},{17,18},{19... | collective-permute-start | bytes 786440 | tf_op jit(solution)/shard_map/ppermute | solution.py:381
  3.6 17.3 %collective-permute-start.6 = (f32[256,256]{1,0:T(8,128)S(1)}, f32[256,256]{1,0:T(8,128)S(1)}, u32[]{:S(2)}, u32[]{:S(2)}) collective-permute-start(f32[256,256]{1,0:T(8,128)S(1)} %get-tuple-element.38), channel_id=1, source_target_pairs={{1,2},{3,4},{5,6},{7,8},{9,10},{11,12},{13,14},{15,16},{17,18},{19... | collective-permute-start | bytes 786440 | tf_op jit(solution)/shard_map/ppermute | solution.py:381
  4.3 6.4 %collective-permute-start = (s32[2]{0:T(128)S(1)}, s32[2]{0:T(128)S(1)}, u32[]{:S(2)}, u32[]{:S(2)}) collective-permute-start(s32[2]{0:T(128)S(1)} %copy-done.4), channel_id=1, source_target_pairs={{0,1},{1,0},{2,3},{3,2},{4,5},{5,4},{6,7},{7,6},{8,9},{9,8},{10,11... | collective-permute-start | bytes 32 | tf_op jit(solution)/shard_map/ppermute | solution.py:378
  10.7 10.2 %copy-start.3 = (f32[2,256,256]{2,1,0:T(8,128)S(1)}, f32[2,256,256]{2,1,0:T(8,128)}, u32[]{:S(2)}) copy-start(f32[2,256,256]{2,1,0:T(8,128)} %preconditioner.3) | copy-start | bytes 1572868
  12.5 15.3 %collective-permute-start.5 = (f32[256,256]{1,0:T(8,128)S(1)}, f32[256,256]{1,0:T(8,128)S(1)}, u32[]{:S(2)}, u32[]{:S(2)}) collective-permute-start(f32[256,256]{1,0:T(8,128)S(1)} %shard_map.70.image.own_image), channel_id=1, source_target_pairs={{1,2},{3,4},{5,6},{7,8},{9,10},{11,12},{13,14},{15,16},{17,18},{19... | collective-permute-start | bytes 786440 | tf_op jit(solution)/shard_map/ppermute | solution.py:381
  13.2 14.7 %collective-permute-start.4 = (f32[256,256]{1,0:T(8,128)S(1)}, f32[256,256]{1,0:T(8,128)S(1)}, u32[]{:S(2)}, u32[]{:S(2)}) collective-permute-start(f32[256,256]{1,0:T(8,128)S(1)} %shard_map.70.image.own_image), channel_id=1, source_target_pairs={{0,1},{1,0},{2,3},{3,2},{4,5},{5,4},{6,7},{7,6},{8,9},{9,8},{10,11... | collective-permute-start | bytes 786440 | tf_op jit(solution)/shard_map/ppermute | solution.py:378
  23.4 10.2 %collective-permute-start.8 = (f32[256,256]{1,0:T(8,128)S(1)}, f32[256,256]{1,0:T(8,128)S(1)}, u32[]{:S(2)}, u32[]{:S(2)}) collective-permute-start(f32[256,256]{1,0:T(8,128)S(1)} %get-tuple-element.45.side.own_side), channel_id=1, source_target_pairs={{1,2},{3,4},{5,6},{7,8},{9,10},{11,12},{13,14},{15,16},{17,18},{19... | collective-permute-start | bytes 786440 | tf_op jit(solution)/shard_map/ppermute | solution.py:381
  24.1 9.5 %collective-permute-start.7 = (f32[256,256]{1,0:T(8,128)S(1)}, f32[256,256]{1,0:T(8,128)S(1)}, u32[]{:S(2)}, u32[]{:S(2)}) collective-permute-start(f32[256,256]{1,0:T(8,128)S(1)} %get-tuple-element.45.side.own_side), channel_id=1, source_target_pairs={{0,1},{1,0},{2,3},{3,2},{4,5},{5,4},{6,7},{7,6},{8,9},{9,8},{10,11... | collective-permute-start | bytes 786440 | tf_op jit(solution)/shard_map/ppermute | solution.py:378
  30.0 17.7 %collective-permute-start.10 = (f32[256,256]{1,0:T(8,128)S(1)}, f32[256,256]{1,0:T(8,128)S(1)}, u32[]{:S(2)}, u32[]{:S(2)}) collective-permute-start(f32[256,256]{1,0:T(8,128)S(1)} %get-tuple-element.48.own_second), channel_id=1, source_target_pairs={{1,2},{3,4},{5,6},{7,8},{9,10},{11,12},{13,14},{15,16},{17,18},{19... | collective-permute-start | bytes 786440 | tf_op jit(solution)/shard_map/ppermute | solution.py:381
  30.7 17.0 %collective-permute-start.9 = (f32[256,256]{1,0:T(8,128)S(1)}, f32[256,256]{1,0:T(8,128)S(1)}, u32[]{:S(2)}, u32[]{:S(2)}) collective-permute-start(f32[256,256]{1,0:T(8,128)S(1)} %get-tuple-element.48.own_second), channel_id=1, source_target_pairs={{0,1},{1,0},{2,3},{3,2},{4,5},{5,4},{6,7},{7,6},{8,9},{9,8},{10,11... | collective-permute-start | bytes 786440 | tf_op jit(solution)/shard_map/ppermute | solution.py:378
  50.8 8.9 %collective-permute-start.11 = (f32[128,256]{1,0:T(8,128)S(1)}, f32[128,256]{1,0:T(8,128)S(1)}, u32[]{:S(2)}, u32[]{:S(2)}) collective-permute-start(f32[128,256]{1,0:T(8,128)S(1)} %get-tuple-element.53), channel_id=1, source_target_pairs={{0,1},{1,0},{2,3},{3,2},{4,5},{5,4},{6,7},{7,6},{8,9},{9,8},{10,11... | collective-permute-start | bytes 393224 | tf_op jit(solution)/shard_map/ppermute | solution.py:378

commit v6 on v5

--- a/solution.py
+++ b/solution.py
@@ -59,17 +59,24 @@
 
 def dot_split(lhs_high, lhs_low, rhs_high, rhs_low):
     dot = functools.partial(jnp.dot, preferred_element_type=jnp.float32)
-    return dot(lhs_high, rhs_high) + (dot(lhs_low, rhs_high) + dot(lhs_high, rhs_low))
+    rows = lhs_high.shape[0]
+    both = dot(jnp.concatenate([lhs_high, lhs_low], axis=0), rhs_high)
+    return both[:rows] + (both[rows:] + dot(lhs_high, rhs_low))
 
 
 def apply_terms(sources, vectors, left, right):
     left_high, left_low = left
     right_high, right_low = right
     vector_high, vector_low = vectors
+    inners = [
+        split(
+            dot_split(left_high[term], left_low[term], vector_high[source], vector_low[source])
+        )
+        for term, source in enumerate(sources)
+    ]
     image = None
-    for term, source in enumerate(sources):
-        inner = dot_split(left_high[term], left_low[term], vector_high[source], vector_low[source])
-        part = dot_split(*split(inner), right_high[term], right_low[term])
+    for term, inner in enumerate(inners):
+        part = dot_split(*inner, right_high[term], right_low[term])
         image = part if image is None else image + part
     return image
 
@@ -220,14 +227,9 @@
 
 
 def splitting_kernel(
-    wave, facing_wave, own_left, own_right, mate_left, mate_right, start_ref, high, low, left_high,
-    left_low, right_high, right_low,
-):
-    op = lax.axis_index("op")
-    for place, values in enumerate((wave[op], wave[1 - op], facing_wave[...])):
-        start = values * START_SCALE
-        start_ref[place] = start
-        high[place], low[place] = split(start)
+    own_left, own_right, mate_left, mate_right, left_high, left_low, right_high, right_low
+):
+    op = lax.axis_index("op")
     count = own_left.shape[0]
     for term in range(count):
         left_high[term], left_low[term] = split(own_left[term, op] * (1.0 / H_SCALE))
@@ -238,17 +240,23 @@
 
 
 def first_kernel(
-    own_shifts, mate_shifts, high, low, left_high, left_low, right_high, right_low, image_ref
-):
+    own_shifts, mate_shifts, wave, facing_wave, left_high, left_low, right_high, right_low,
+    image_ref, start_ref, high, low,
+):
+    op = lax.axis_index("op")
     sources = term_sources(own_shifts, mate_shifts)
+    for place, values in enumerate((wave[op], wave[1 - op], facing_wave[...])):
+        start = values * START_SCALE
+        start_ref[place] = start
+        high[place], low[place] = split(start)
     image_ref[...] = apply_terms(
         sources, (high, low), (left_high, left_low), (right_high, right_low)
     )
 
 
 def side_kernel(
-    own_shifts, mate_shifts, start, preconditioner, facing_preconditioner, image,
-    left_high, left_low, right_high, right_low, side_ref, row_ref, inverse_ref, high, low,
+    own_shifts, mate_shifts, start, preconditioner, facing_preconditioner,
+    left_high, left_low, right_high, right_low, side_ref, inverse_ref, high, low,
 ):
     op = lax.axis_index("op")
     sources = term_sources(own_shifts, mate_shifts)
@@ -257,10 +265,14 @@
         inverse = inverted(divisors[place])
         inverse_ref[place] = inverse
         high[place], low[place] = split(start[place] * inverse)
-    side = apply_terms(sources, (high, low), (left_high, left_low), (right_high, right_low))
-    side_ref[...] = side
-    arrays = {"w": start[0], "u": image[...], "a": side}
-    row_ref[...] = row_of_sums(moment_factors(EARLY_MOMENTS, arrays, inverse_ref[0]))
+    side_ref[...] = apply_terms(
+        sources, (high, low), (left_high, left_low), (right_high, right_low)
+    )
+
+
+def moments_kernel(start, image, side, inverse, row_ref):
+    arrays = {"w": start[0], "u": image[...], "a": side[...]}
+    row_ref[...] = row_of_sums(moment_factors(EARLY_MOMENTS, arrays, inverse[0]))
 
 
 def second_kernel(
@@ -419,30 +431,33 @@
     shifts = (term_shifts, mate(term_shifts))
 
     split_shape = (terms,) + left_blocks.shape[2:]
-    start, start_high, start_low, *blocks = call(
+    blocks = call(
         splitting_kernel,
-        (wave_start, facing_wave, left_blocks, right_blocks, mate_left, mate_right),
-        [((3,) + block, f32)] + [((3,) + block, bf16)] * 2 + [(split_shape, bf16)] * 4,
+        (left_blocks, right_blocks, mate_left, mate_right),
+        [(split_shape, bf16)] * 4,
         scratch=False,
     )
+
     def around(values):
         return (values, mate(values), facing(values))
 
-    (image,) = call(
+    image, start = call(
         first_kernel,
-        (*shifts, start_high, start_low, *blocks),
-        [(block, f32)],
+        (*shifts, wave_start, facing_wave, *blocks),
+        [(block, f32), ((3,) + block, f32)],
         scalars=2,
-        scratch=False,
     )
     images = around(image)
-    side, early_row, inverse = call(
+    side, inverse = call(
         side_kernel,
-        (*shifts, start, preconditioner, facing_preconditioner, image, *blocks),
-        [(block, f32), ((1, LANES), f32), ((3,) + block, f32)],
+        (*shifts, start, preconditioner, facing_preconditioner, *blocks),
+        [(block, f32), ((3,) + block, f32)],
         scalars=2,
     )
     sides = around(side)
+    (early_row,) = call(
+        moments_kernel, (start, image, side, inverse), [((1, LANES), f32)], scratch=False
+    )
     second, row, ratio = call(
         second_kernel,
         (*shifts, start, *images, inverse, side, early_row, *blocks),

time: 61.1 us -> 60 us (0.982)
  starting transfers between devices: 24.2 us -> 23.2 us
    ppermute x7, starting transfers between devices: 20.7 us -> 19.6 us  [mate(): return lax.ppermute(values, AXES, swap)]
    pallas_call x6 -> x7, Pallas kernels: 11.2 us -> 11 us  [call(): pl.pallas_call(kernel, out_shape=[jax.ShapeDtypeStruct(shape, kind) for s...]
  transfers between devices with their start and end apart: 12 -> 12, of which waited for: 1 -> 1; matrix products, arithmetic and copies ran while one was open for 0% -> 0% of each run, Pallas kernels for 11% -> 12%
where the time goes in v6:
time: 60 us; the launch traced here: 59.7 us
  starting transfers between devices  23.2 us (39%)
  blocking collectives  22.7 us (38%)
  Pallas kernels  12.6 us (21%)
  between operations  0.8 us (1%)
    all_to_all x2, blocking collectives, exchanged(): lax.all_to_all(spread, AXES, 0, 0, tiled=True).reshape(devices, LANES)  22.7 us
    ppermute x7, starting transfers between devices, mate(): return lax.ppermute(values, AXES, swap)  19.6 us
    pallas_call x7, Pallas kernels, call(): pl.pallas_call(kernel, out_shape=[jax.ShapeDtypeStruct(shape, kind) for s...  11 us
    ppermute x5, starting transfers between devices, facing(): return lax.ppermute(values, AXES, across)  3.64 us
    pallas_call x1, Pallas kernels, one_sector_body(): pl.pallas_call(picking_kernel, out_shape=[jax.ShapeDtypeStruct(shape, f32...  1.55 us
  transfers between devices with their start and end apart: 12, of which 1 were waited for; matrix products, arithmetic and copies ran while one was open for 0% of the time, Pallas kernels for 12%

profile of v6, /device:TPU:0, one launch (start us, length us, event | category | flops | bytes accessed | tf_op | source)
XLA Modules:
  0.0 59.7 jit_solution(18139700910822846477)
XLA Ops:
  0.6 1.5 %shard_map.68 = (f32[256,256]{1,0:T(8,128)S(1)}, f32[256,256]{1,0:T(8,128)S(1)}, f32[2,256,256]{2,1,0:T(8,128)S(1)}, f32[2,256,256]{2,1,0:T(8,128)S(1)}) custom-call(f32[2,256,256]{2,1,0:T(8,128)} %wave.3, f32[2,256,256]{2,1,0:T(8,128)} %preconditioner.3, f32[2,2,256,256]{3,2,1,0:T(8,128)} %own_left.1, f32[2,2,256,256]{3,2,1,0:T(8,128)} %own_right.1), custom_call_target="tpu_custom_call" | custom-call | tf_op jit(solution)/shard_map/pallas_call | solution.py:420
  2.2 0.5 collective-permute-start.2
  2.7 0.1 collective-permute-start.3
  2.8 0.8 %collective-permute-start.1 = (f32[256,256]{1,0:T(8,128)S(1)}, f32[256,256]{1,0:T(8,128)S(1)}, u32[]{:S(2)}, u32[]{:S(2)}) collective-permute-start(f32[256,256]{1,0:T(8,128)S(1)} %get-tuple-element.26), channel_id=1, source_target_pairs={{1,2},{3,4},{5,6},{7,8},{9,10},{11,12},{13,14},{15,16},{17,18},{19... | collective-permute-start | bytes 786440 | tf_op jit(solution)/shard_map/ppermute | solution.py:393
  3.6 0.0 copy-start.2
  3.6 0.8 %collective-permute-start.6 = (f32[256,256]{1,0:T(8,128)S(1)}, f32[256,256]{1,0:T(8,128)S(1)}, u32[]{:S(2)}, u32[]{:S(2)}) collective-permute-start(f32[256,256]{1,0:T(8,128)S(1)} %get-tuple-element.35), channel_id=1, source_target_pairs={{1,2},{3,4},{5,6},{7,8},{9,10},{11,12},{13,14},{15,16},{17,18},{19... | collective-permute-start | bytes 786440 | tf_op jit(solution)/shard_map/ppermute | solution.py:393
  4.4 5.6 %collective-permute-start = (s32[2]{0:T(128)S(1)}, s32[2]{0:T(128)S(1)}, u32[]{:S(2)}, u32[]{:S(2)}) collective-permute-start(s32[2]{0:T(128)S(1)} %copy-done.4), channel_id=1, source_target_pairs={{0,1},{1,0},{2,3},{3,2},{4,5},{5,4},{6,7},{7,6},{8,9},{9,8},{10,11... | collective-permute-start | bytes 32 | tf_op jit(solution)/shard_map/ppermute | solution.py:390
  10.0 0.0 collective-permute-done.2.mate_left
  10.0 0.0 collective-permute-done.3.mate_right
  10.0 0.4 shard_map.69
  10.5 0.4 collective-permute-done.mate_shifts
  10.8 0.0 collective-permute-done.1.facing_wave
  10.8 1.8 %shard_map.70 = (f32[256,256]{1,0:T(8,128)S(1)}, f32[3,256,256]{2,1,0:T(8,128)S(1)}) custom-call(s32[2]{0:T(128)S(1)} %copy-done.4, s32[2]{0:T(128)S(1)} %collective-permute-done.mate_shifts, f32[2,256,256]{2,1,0:T(8,128)S(1)} %copy-done.2, f32[256,256]{1,0:T(8,128)S(1)} %collective-permute-done.1.facing_wave, ...), custom_call_target="tpu_custom_call" | custom-call | tf_op jit(solution)/shard_map/pallas_call | solution.py:406
  12.6 0.7 %collective-permute-start.5 = (f32[256,256]{1,0:T(8,128)S(1)}, f32[256,256]{1,0:T(8,128)S(1)}, u32[]{:S(2)}, u32[]{:S(2)}) collective-permute-start(f32[256,256]{1,0:T(8,128)S(1)} %get-tuple-element.34.image.own_image), channel_id=1, source_target_pairs={{1,2},{3,4},{5,6},{7,8},{9,10},{11,12},{13,14},{15,16},{17,18},{19... | collective-permute-start | bytes 786440 | tf_op jit(solution)/shard_map/ppermute | solution.py:393
  13.3 6.9 %collective-permute-start.4 = (f32[256,256]{1,0:T(8,128)S(1)}, f32[256,256]{1,0:T(8,128)S(1)}, u32[]{:S(2)}, u32[]{:S(2)}) collective-permute-start(f32[256,256]{1,0:T(8,128)S(1)} %get-tuple-element.34.image.own_image), channel_id=1, source_target_pairs={{0,1},{1,0},{2,3},{3,2},{4,5},{5,4},{6,7},{7,6},{8,9},{9,8},{10,11... | collective-permute-start | bytes 786440 | tf_op jit(solution)/shard_map/ppermute | solution.py:390
  20.2 0.0 collective-permute-done.6.facing_preconditioner
  20.2 1.8 %shard_map.71 = (f32[256,256]{1,0:T(8,128)S(1)}, f32[3,256,256]{2,1,0:T(8,128)S(1)}) custom-call(s32[2]{0:T(128)S(1)} %copy-done.4, s32[2]{0:T(128)S(1)} %collective-permute-done.mate_shifts, f32[3,256,256]{2,1,0:T(8,128)S(1)} %get-tuple-element.33.start, f32[2,256,256]{2,1,0:T(8,128)S(1)} %copy-done.3, ...), custom_call_target="tpu_custom_call" | custom-call | tf_op jit(solution)/shard_map/pallas_call | solution.py:406
  22.1 0.7 %collective-permute-start.8 = (f32[256,256]{1,0:T(8,128)S(1)}, f32[256,256]{1,0:T(8,128)S(1)}, u32[]{:S(2)}, u32[]{:S(2)}) collective-permute-start(f32[256,256]{1,0:T(8,128)S(1)} %get-tuple-element.41.side.own_side), channel_id=1, source_target_pairs={{1,2},{3,4},{5,6},{7,8},{9,10},{11,12},{13,14},{15,16},{17,18},{19... | collective-permute-start | bytes 786440 | tf_op jit(solution)/shard_map/ppermute | solution.py:393
  22.8 3.8 %collective-permute-start.7 = (f32[256,256]{1,0:T(8,128)S(1)}, f32[256,256]{1,0:T(8,128)S(1)}, u32[]{:S(2)}, u32[]{:S(2)}) collective-permute-start(f32[256,256]{1,0:T(8,128)S(1)} %get-tuple-element.41.side.own_side), channel_id=1, source_target_pairs={{0,1},{1,0},{2,3},{3,2},{4,5},{5,4},{6,7},{7,6},{8,9},{9,8},{10,11... | collective-permute-start | bytes 786440 | tf_op jit(solution)/shard_map/ppermute | solution.py:390
  26.6 0.8 %shard_map.72.early_row = f32[1,128]{1,0:T(1,128)S(1)} custom-call(f32[3,256,256]{2,1,0:T(8,128)S(1)} %get-tuple-element.33.start, f32[256,256]{1,0:T(8,128)S(1)} %get-tuple-element.34.image.own_image, f32[256,256]{1,0:T(8,128)S(1)} %get-tuple-element.41.side.own_side, f32[3,256,256]{2,1,0:T(8,128)S(1)} %get-tuple-element.36.inverse), custom_call_target="tpu_custom_call" | custom-call | tf_op jit(solution)/shard_map/pallas_call | solution.py:406
  27.3 0.0 collective-permute-done.5.facing_image
  27.4 0.0 collective-permute-done.4.mate_image
  27.4 2.1 %shard_map.73 = (f32[256,256]{1,0:T(8,128)S(1)}, f32[32,128]{1,0:T(8,128)S(1)}, f32[3,256,256]{2,1,0:T(8,128)S(1)}) custom-call(s32[2]{0:T(128)S(1)} %copy-done.4, s32[2]{0:T(128)S(1)} %collective-permute-done.mate_shifts, f32[3,256,256]{2,1,0:T(8,128)S(1)} %get-tuple-element.33.start, f32[256,256]{1,0:T(8,128)S(1)} %get-tuple-element.34.image.own_image, ...), custom_call_target="tpu_custom_call" | custom-call | tf_op jit(solution)/shard_map/pallas_call | solution.py:406
  29.5 0.7 %collective-permute-start.10 = (f32[256,256]{1,0:T(8,128)S(1)}, f32[256,256]{1,0:T(8,128)S(1)}, u32[]{:S(2)}, u32[]{:S(2)}) collective-permute-start(f32[256,256]{1,0:T(8,128)S(1)} %get-tuple-element.44.own_second), channel_id=1, source_target_pairs={{1,2},{3,4},{5,6},{7,8},{9,10},{11,12},{13,14},{15,16},{17,18},{19... | collective-permute-start | bytes 786440 | tf_op jit(solution)/shard_map/ppermute | solution.py:393
  30.2 2.7 %collective-permute-start.9 = (f32[256,256]{1,0:T(8,128)S(1)}, f32[256,256]{1,0:T(8,128)S(1)}, u32[]{:S(2)}, u32[]{:S(2)}) collective-permute-start(f32[256,256]{1,0:T(8,128)S(1)} %get-tuple-element.44.own_second), channel_id=1, source_target_pairs={{0,1},{1,0},{2,3},{3,2},{4,5},{5,4},{6,7},{7,6},{8,9},{9,8},{10,11... | collective-permute-start | bytes 786440 | tf_op jit(solution)/shard_map/ppermute | solution.py:390
  32.8 0.0 collective-permute-done.8.facing_side
  32.8 13.8 %all_to_all.10 = f32[32,1,128]{2,1,0:T(1,128)S(1)} all-to-all(f32[32,1,128]{2,1,0:T(1,128)S(1)} %bitcast.11), channel_id=1, replica_groups=mesh['sector'=16,'op'=2] {'sector','op'}, dimensions={0} | all-to-all | bytes 32768 | tf_op jit(solution)/shard_map/all_to_all | solution.py:400
  46.7 3.0 %shard_map.74 = (f32[128,256]{1,0:T(8,128)S(1)}, f32[128,256]{1,0:T(8,128)S(1)}, f32[32,128]{1,0:T(8,128)S(1)}, f32[3,2,128,256]{3,2,1,0:T(8,128)S(1)}, f32[2,8,128]{2,1,0:T(8,128)S(1)}) custom-call(s32[2]{0:T(128)S(1)} %copy-done.4, s32[2]{0:T(128)S(1)} %collective-permute-done.mate_shifts, f32[32,128]{1,0:T(8,128)S(1)} %bitcast.8, ...), custom_call_target="tpu_custom_call" | custom-call | tf_op jit(solution)/shard_map/pallas_call | solution.py:406
  49.7 0.1 collective-permute-start.11
  49.8 8.8 %all_to_all.11 = f32[32,1,128]{2,1,0:T(1,128)S(1)} all-to-all(f32[32,1,128]{2,1,0:T(1,128)S(1)} %bitcast.10), channel_id=1, replica_groups=mesh['sector'=16,'op'=2] {'sector','op'}, dimensions={0} | all-to-all | bytes 32768 | tf_op jit(solution)/shard_map/all_to_all | solution.py:400
  58.6 0.0 collective-permute-done.11.mate_image
  58.6 1.1 %shard_map.75 = (f32[3,2,128,256]{3,2,1,0:T(8,128)}, f32[3]{0:T(128)}) custom-call(f32[32,128]{1,0:T(8,128)S(1)} %bitcast.9, f32[2,8,128]{2,1,0:T(8,128)S(1)} %get-tuple-element.46.thetas, f32[3,2,128,256]{3,2,1,0:T(8,128)S(1)} %get-tuple-element.47.members, f32[3,256,256]{2,1,0:T(8,128)S(1)} %get-tuple-element.36.inverse, ...), custom_call_target="tpu_custom_call" | custom-call | tf_op jit(solution)/shard_map/pallas_call | solution.py:406
  (12 shorter events, 0.0 us)
Async XLA Ops:
  0.6 9.4 %copy-start.1 = (f32[2,2,256,256]{3,2,1,0:T(8,128)S(1)}, f32[2,2,256,256]{3,2,1,0:T(8,128)}, u32[]{:S(2)}) copy-start(f32[2,2,256,256]{3,2,1,0:T(8,128)} %own_right.1) | copy-start | bytes 3145732
  0.6 9.4 %copy-start = (f32[2,2,256,256]{3,2,1,0:T(8,128)S(1)}, f32[2,2,256,256]{3,2,1,0:T(8,128)}, u32[]{:S(2)}) copy-start(f32[2,2,256,256]{3,2,1,0:T(8,128)} %own_left.1) | copy-start | bytes 3145732
  2.2 7.8 %collective-permute-start.2 = (f32[2,256,256]{2,1,0:T(8,128)S(1)}, f32[2,256,256]{2,1,0:T(8,128)S(1)}, u32[]{:S(2)}, u32[]{:S(2)}) collective-permute-start(f32[2,256,256]{2,1,0:T(8,128)S(1)} %get-tuple-element.27), channel_id=1, source_target_pairs={{0,1},{1,0},{2,3},{3,2},{4,5},{5,4},{6,7},{7,6},{8,9},{9,8},{10,11... | collective-permute-start | bytes 1572872 | tf_op jit(solution)/shard_map/ppermute | solution.py:390
  2.7 7.3 %collective-permute-start.3 = (f32[2,256,256]{2,1,0:T(8,128)S(1)}, f32[2,256,256]{2,1,0:T(8,128)S(1)}, u32[]{:S(2)}, u32[]{:S(2)}) collective-permute-start(f32[2,256,256]{2,1,0:T(8,128)S(1)} %get-tuple-element.28), channel_id=1, source_target_pairs={{0,1},{1,0},{2,3},{3,2},{4,5},{5,4},{6,7},{7,6},{8,9},{9,8},{10,11... | collective-permute-start | bytes 1572872 | tf_op jit(solution)/shard_map/ppermute | solution.py:390
  2.8 1.6 %copy-start.4 = (s32[2]{0:T(128)S(1)}, s32[2]{0:T(128)}, u32[]{:S(2)}) copy-start(s32[2]{0:T(128)} %own_shifts.7) | copy-start | bytes 28
  2.8 8.0 %collective-permute-start.1 = (f32[256,256]{1,0:T(8,128)S(1)}, f32[256,256]{1,0:T(8,128)S(1)}, u32[]{:S(2)}, u32[]{:S(2)}) collective-permute-start(f32[256,256]{1,0:T(8,128)S(1)} %get-tuple-element.26), channel_id=1, source_target_pairs={{1,2},{3,4},{5,6},{7,8},{9,10},{11,12},{13,14},{15,16},{17,18},{19... | collective-permute-start | bytes 786440 | tf_op jit(solution)/shard_map/ppermute | solution.py:393
  3.6 7.2 %copy-start.2 = (f32[2,256,256]{2,1,0:T(8,128)S(1)}, f32[2,256,256]{2,1,0:T(8,128)}, u32[]{:S(2)}) copy-start(f32[2,256,256]{2,1,0:T(8,128)} %wave.3) | copy-start | bytes 1572868
  3.6 16.6 %collective-permute-start.6 = (f32[256,256]{1,0:T(8,128)S(1)}, f32[256,256]{1,0:T(8,128)S(1)}, u32[]{:S(2)}, u32[]{:S(2)}) collective-permute-start(f32[256,256]{1,0:T(8,128)S(1)} %get-tuple-element.35), channel_id=1, source_target_pairs={{1,2},{3,4},{5,6},{7,8},{9,10},{11,12},{13,14},{15,16},{17,18},{19... | collective-permute-start | bytes 786440 | tf_op jit(solution)/shard_map/ppermute | solution.py:393
  4.4 6.4 %collective-permute-start = (s32[2]{0:T(128)S(1)}, s32[2]{0:T(128)S(1)}, u32[]{:S(2)}, u32[]{:S(2)}) collective-permute-start(s32[2]{0:T(128)S(1)} %copy-done.4), channel_id=1, source_target_pairs={{0,1},{1,0},{2,3},{3,2},{4,5},{5,4},{6,7},{7,6},{8,9},{9,8},{10,11... | collective-permute-start | bytes 32 | tf_op jit(solution)/shard_map/ppermute | solution.py:390
  10.8 9.4 %copy-start.3 = (f32[2,256,256]{2,1,0:T(8,128)S(1)}, f32[2,256,256]{2,1,0:T(8,128)}, u32[]{:S(2)}) copy-start(f32[2,256,256]{2,1,0:T(8,128)} %preconditioner.3) | copy-start | bytes 1572868
  12.6 14.7 %collective-permute-start.5 = (f32[256,256]{1,0:T(8,128)S(1)}, f32[256,256]{1,0:T(8,128)S(1)}, u32[]{:S(2)}, u32[]{:S(2)}) collective-permute-start(f32[256,256]{1,0:T(8,128)S(1)} %get-tuple-element.34.image.own_image), channel_id=1, source_target_pairs={{1,2},{3,4},{5,6},{7,8},{9,10},{11,12},{13,14},{15,16},{17,18},{19... | collective-permute-start | bytes 786440 | tf_op jit(solution)/shard_map/ppermute | solution.py:393
  13.3 14.0 %collective-permute-start.4 = (f32[256,256]{1,0:T(8,128)S(1)}, f32[256,256]{1,0:T(8,128)S(1)}, u32[]{:S(2)}, u32[]{:S(2)}) collective-permute-start(f32[256,256]{1,0:T(8,128)S(1)} %get-tuple-element.34.image.own_image), channel_id=1, source_target_pairs={{0,1},{1,0},{2,3},{3,2},{4,5},{5,4},{6,7},{7,6},{8,9},{9,8},{10,11... | collective-permute-start | bytes 786440 | tf_op jit(solution)/shard_map/ppermute | solution.py:390
  22.1 10.8 %collective-permute-start.8 = (f32[256,256]{1,0:T(8,128)S(1)}, f32[256,256]{1,0:T(8,128)S(1)}, u32[]{:S(2)}, u32[]{:S(2)}) collective-permute-start(f32[256,256]{1,0:T(8,128)S(1)} %get-tuple-element.41.side.own_side), channel_id=1, source_target_pairs={{1,2},{3,4},{5,6},{7,8},{9,10},{11,12},{13,14},{15,16},{17,18},{19... | collective-permute-start | bytes 786440 | tf_op jit(solution)/shard_map/ppermute | solution.py:393
  22.8 10.1 %collective-permute-start.7 = (f32[256,256]{1,0:T(8,128)S(1)}, f32[256,256]{1,0:T(8,128)S(1)}, u32[]{:S(2)}, u32[]{:S(2)}) collective-permute-start(f32[256,256]{1,0:T(8,128)S(1)} %get-tuple-element.41.side.own_side), channel_id=1, source_target_pairs={{0,1},{1,0},{2,3},{3,2},{4,5},{5,4},{6,7},{7,6},{8,9},{9,8},{10,11... | collective-permute-start | bytes 786440 | tf_op jit(solution)/shard_map/ppermute | solution.py:390
  29.5 17.2 %collective-permute-start.10 = (f32[256,256]{1,0:T(8,128)S(1)}, f32[256,256]{1,0:T(8,128)S(1)}, u32[]{:S(2)}, u32[]{:S(2)}) collective-permute-start(f32[256,256]{1,0:T(8,128)S(1)} %get-tuple-element.44.own_second), channel_id=1, source_target_pairs={{1,2},{3,4},{5,6},{7,8},{9,10},{11,12},{13,14},{15,16},{17,18},{19... | collective-permute-start | bytes 786440 | tf_op jit(solution)/shard_map/ppermute | solution.py:393
  30.2 16.5 %collective-permute-start.9 = (f32[256,256]{1,0:T(8,128)S(1)}, f32[256,256]{1,0:T(8,128)S(1)}, u32[]{:S(2)}, u32[]{:S(2)}) collective-permute-start(f32[256,256]{1,0:T(8,128)S(1)} %get-tuple-element.44.own_second), channel_id=1, source_target_pairs={{0,1},{1,0},{2,3},{3,2},{4,5},{5,4},{6,7},{7,6},{8,9},{9,8},{10,11... | collective-permute-start | bytes 786440 | tf_op jit(solution)/shard_map/ppermute | solution.py:390
  49.7 8.9 %collective-permute-start.11 = (f32[128,256]{1,0:T(8,128)S(1)}, f32[128,256]{1,0:T(8,128)S(1)}, u32[]{:S(2)}, u32[]{:S(2)}) collective-permute-start(f32[128,256]{1,0:T(8,128)S(1)} %get-tuple-element.49), channel_id=1, source_target_pairs={{0,1},{1,0},{2,3},{3,2},{4,5},{5,4},{6,7},{7,6},{8,9},{9,8},{10,11... | collective-permute-start | bytes 393224 | tf_op jit(solution)/shard_map/ppermute | solution.py:390

commit v7 on v6

--- a/solution.py
+++ b/solution.py
@@ -109,21 +109,15 @@
     return value[:1, :1]
 
 
-EARLY_MOMENTS = (
-    [("w", "w", n) for n in range(5)]
-    + [("u", "w", n) for n in range(5)]
-    + [("u", "u", n) for n in range(1, 5)]
-    + [("a", "w", n) for n in range(4)]
-    + [("a", "u", n) for n in range(1, 4)]
-    + [("a", "a", 2)]
-)
-LATE_MOMENTS = (
-    [("b", "w", n) for n in range(4)]
-    + [("b", "u", n) for n in range(1, 4)]
-    + [("a", "b", 2), ("b", "b", 2)]
-)
-
-H_OF = {("w", 0): "u", ("w", 1): "a", ("u", 1): "b"}
+H_OF = {
+    ("w", 0): "u",
+    ("w", 1): "a",
+    ("u", 1): "b",
+    ("w", 2): "c",
+    ("u", 2): "d",
+    ("a", 1): "e",
+    ("b", 1): "f",
+}
 
 START_SCALE = 2.0**10
 H_SCALE = 2.0**7
@@ -156,34 +150,48 @@
     return {(H_OF[word], 0): value * H_SCALE for word, value in vector.items()}
 
 
-def inner(one, other, moments):
+def inner(one, other, moment):
     result = None
     for (x, n), value in one.items():
         part = None
         for (y, m), factor in other.items():
-            term = factor * moments[tuple(sorted((x, y))) + (n + m,)]
+            term = factor * moment(*sorted((x, y)), n + m)
             part = term if part is None else part + term
         part = value * part
         result = part if result is None else result + part
     return result
 
 
-def first_two_steps(sums):
-    moments = dict(zip(EARLY_MOMENTS + LATE_MOMENTS, sums))
-    basis = [{("w", 0): lax.rsqrt(moments["w", "w", 0] + EPSILON * START_SCALE**2)}]
+def all_steps(moment, inverse_root):
+    basis = [{("w", 0): inverse_root(moment("w", "w", 0) + EPSILON * START_SCALE**2)}]
     thetas = []
-    for _ in range(2):
+    for _ in range(ITERS):
         latest = basis[-1]
         image = times_h(latest)
-        theta = inner(latest, image, moments)
+        theta = inner(latest, image, moment)
         correction = times_inverse(plus(image, latest, -theta))
         ortho = correction
         for member in basis:
-            ortho = plus(ortho, member, -inner(member, correction, moments))
-        scale = lax.rsqrt(inner(ortho, ortho, moments) + EPSILON)
+            ortho = plus(ortho, member, -inner(member, correction, moment))
+        scale = inverse_root(inner(ortho, ortho, moment) + EPSILON)
         basis.append({word: value * scale for word, value in ortho.items()})
         thetas.append(theta)
     return basis, thetas
+
+
+def needed_moments():
+    asked = {}
+
+    def moment(x, y, n):
+        asked[x, y, n] = True
+        return 1.0
+
+    all_steps(moment, lambda value: 1.0)
+    stages = ("wua", "bcd", "e", "f")
+    groups = [[] for _ in stages]
+    for key in asked:
+        groups[max(i for i, names in enumerate(stages) if set(key[:2]) & set(names))].append(key)
+    return groups
 
 
 def combined(vector, arrays, inverse):
@@ -200,6 +208,10 @@
     return result
 
 
+MOMENTS = needed_moments()
+FIRST_LANE = [sum(len(group) for group in MOMENTS[:i]) for i in range(len(MOMENTS) + 1)]
+
+
 def inverted(values):
     return jnp.where(values > 0.0, 1.0 / values, 0.0)
 
@@ -272,105 +284,111 @@
 
 def moments_kernel(start, image, side, inverse, row_ref):
     arrays = {"w": start[0], "u": image[...], "a": side[...]}
-    row_ref[...] = row_of_sums(moment_factors(EARLY_MOMENTS, arrays, inverse[0]))
+    row_ref[...] = row_of_sums(moment_factors(MOMENTS[0], arrays, inverse[0]))
 
 
 def second_kernel(
-    own_shifts, mate_shifts, start, own_image, mate_image, facing_image, inverse, side, early_row,
-    left_high, left_low, right_high, right_low, image_ref, row_ref, ratio_ref, high, low,
+    own_shifts, mate_shifts, own_image, mate_image, facing_image, inverse, _,
+    left_high, left_low, right_high, right_low, image_ref, ratio_ref, high, low,
 ):
     sources = term_sources(own_shifts, mate_shifts)
     for place, image in enumerate((own_image, mate_image, facing_image)):
         ratio = image[...] * inverse[place]
         ratio_ref[place] = ratio
         high[place], low[place] = split(ratio)
-    image = apply_terms(sources, (high, low), (left_high, left_low), (right_high, right_low))
-    image_ref[...] = image
-    arrays = {"w": start[0], "u": own_image[...], "a": side[...], "b": image}
-    factors = moment_factors(LATE_MOMENTS, arrays, inverse[0])
-    row = row_of_sums(factors, len(EARLY_MOMENTS), early_row[...])
+    image_ref[...] = apply_terms(
+        sources, (high, low), (left_high, left_low), (right_high, right_low)
+    )
+
+
+def halves(image, kept_ref, sent_ref):
+    op = lax.axis_index("op")
+    half = kept_ref.shape[0]
+    kept_ref[...] = jnp.where(op == 0, image[:half], image[half:])
+    sent_ref[...] = jnp.where(op == 0, image[half:], image[:half])
+
+
+def extra_kernel(
+    own_shifts, mate_shifts, start, ratio, inverse, image, side, second, early_row,
+    left_high, left_low, right_high, right_low, extra_ref, kept_ref, sent_ref, row_ref, high, low,
+):
+    sources = term_sources(own_shifts, mate_shifts)
+    arrays = {"w": start[0], "u": image[...], "a": side[...], "b": second[...]}
+    for i, name in enumerate("cd"):
+        for place in range(3):
+            once = start[place] * inverse[place] if name == "c" else ratio[place]
+            high[place], low[place] = split(once * inverse[place])
+        extra = apply_terms(sources, (high, low), (left_high, left_low), (right_high, right_low))
+        arrays[name] = extra
+        extra_ref[i] = extra
+        halves(extra, kept_ref.at[i], sent_ref.at[i])
+    factors = moment_factors(MOMENTS[1], arrays, inverse[0])
+    row_ref[...] = row_of_sums(factors, FIRST_LANE[1], early_row[...])
+
+
+def further_kernel(
+    own_shifts, mate_shifts, start, inverse, image, own_side, mate_side, facing_side, second,
+    extra, early_row, left_high, left_low, right_high, right_low, further_ref, kept_ref, sent_ref,
+    row_ref, high, low,
+):
+    sources = term_sources(own_shifts, mate_shifts)
+    for place, side in enumerate((own_side, mate_side, facing_side)):
+        high[place], low[place] = split(side[...] * inverse[place])
+    further = apply_terms(sources, (high, low), (left_high, left_low), (right_high, right_low))
+    further_ref[...] = further
+    halves(further, kept_ref, sent_ref)
+    arrays = {"w": start[0], "u": image[...], "a": own_side[...], "b": second[...]}
+    arrays.update(c=extra[0], d=extra[1], e=further)
+    factors = moment_factors(MOMENTS[2], arrays, inverse[0])
+    row_ref[...] = row_of_sums(factors, FIRST_LANE[2], early_row[...])
+
+
+def third_kernel(
+    own_shifts, mate_shifts, start, inverse, image, side, own_second, mate_second, facing_second,
+    extra, further, early_row, left_high, left_low, right_high, right_low,
+    kept_ref, sent_ref, row_ref, high, low,
+):
+    sources = term_sources(own_shifts, mate_shifts)
+    for place, second in enumerate((own_second, mate_second, facing_second)):
+        high[place], low[place] = split(second[...] * inverse[place])
+    last = apply_terms(sources, (high, low), (left_high, left_low), (right_high, right_low))
+    halves(last, kept_ref, sent_ref)
+    arrays = {"w": start[0], "u": image[...], "a": side[...], "b": own_second[...]}
+    arrays.update(c=extra[0], d=extra[1], e=further[...], f=last)
+    factors = moment_factors(MOMENTS[3], arrays, inverse[0])
+    row = row_of_sums(factors, FIRST_LANE[3], early_row[...])
     row_ref[...] = jnp.broadcast_to(row, row_ref.shape)
 
 
-MEMBER_PAIRS = [(i, j) for i in range(3) for j in range(i + 1)]
-
-
-def third_kernel(
-    total, own_shifts, mate_shifts, rows, start, inverse, ratio, own_side, mate_side,
-    facing_side, own_second, mate_second, facing_second, left_high, left_low, right_high, right_low,
-    kept_ref, sent_ref, row_ref, members_ref, theta_ref, high, low,
-):
-    op = lax.axis_index("op")
-    sources = term_sources(own_shifts, mate_shifts)
-    count = len(EARLY_MOMENTS + LATE_MOMENTS)
-    basis, thetas = first_two_steps(summed(rows, total, count))
-    for position, theta in enumerate(thetas):
-        theta_ref[position] = theta
-    half = kept_ref.shape[0]
-    sides = (own_side, mate_side, facing_side)
-    seconds = (own_second, mate_second, facing_second)
-
-    def mine(values):
-        return jnp.where(op == 0, values[:half], values[half:])
-
-    for place in range(3):
+def last_kernel(
+    total, rows, start, ratio, inverse, own_side, mate_side, own_second, mate_second, own_extra,
+    mate_extra, own_further, mate_further, own_last, mate_last, basis_ref, ritz_ref
+):
+    op = lax.axis_index("op")
+    keys = [key for group in MOMENTS for key in group]
+    moments = dict(zip(keys, summed(rows, total, len(keys))))
+    basis, thetas = all_steps(lambda *key: moments[key], lax.rsqrt)
+    half = own_last.shape[0]
+    mine = pl.ds(pl.multiple_of(op * half, half), half)
+    for place, (sector, side, second, extra, further, last) in enumerate(
+        (
+            (op, own_side, own_second, own_extra, own_further, own_last),
+            (1 - op, mate_side, mate_second, mate_extra, mate_further, mate_last),
+        )
+    ):
         arrays = {
-            ("w", 0): start[place],
-            ("u", 1): ratio[place],
-            ("a", 0): sides[place][...],
-            ("b", 0): seconds[place][...],
+            ("w", 0): start[place, mine],
+            ("u", 1): ratio[place, mine],
+            ("a", 0): side[mine],
+            ("b", 0): second[mine],
+            ("c", 0): extra[0],
+            ("d", 0): extra[1],
+            ("e", 0): further[...],
+            ("f", 0): last[...],
         }
-        latest = combined(basis[2], arrays, inverse[place])
-        high[place], low[place] = split(latest)
-        if place < 2:
-            members = [combined(vector, arrays, inverse[place]) for vector in basis[:2]] + [latest]
-            for position, member in enumerate(members):
-                members_ref[position, place] = mine(member)
-            if place == 0:
-                own_members = members
-    image = H_SCALE * apply_terms(
-        sources, (high, low), (left_high, left_low), (right_high, right_low)
-    )
-    kept_ref[...] = mine(image)
-    sent_ref[...] = jnp.where(op == 0, image[half:], image[:half])
-    members = own_members
-    ratio_image = image * inverse[0]
-    ratio_latest = members[-1] * inverse[0]
-    factors = [
-        (members[-1], image),
-        (ratio_image, ratio_image),
-        (ratio_image, ratio_latest),
-        (ratio_latest, ratio_latest),
-    ]
-    factors = factors + [(member, ratio_image) for member in members]
-    factors = factors + [(member, ratio_latest) for member in members]
-    factors = factors + [(members[i], members[j]) for i, j in MEMBER_PAIRS]
-    row_ref[...] = jnp.broadcast_to(row_of_sums(factors), row_ref.shape)
-
-
-def last_kernel(
-    total, rows, thetas, members, inverse, own_image, mate_image, basis_ref, ritz_ref
-):
-    op = lax.axis_index("op")
-    sums = summed(rows, total, 10 + len(MEMBER_PAIRS))
-    theta = sums[0]
-    correlations = [sums[4 + i] - theta * sums[7 + i] for i in range(3)]
-    length = sums[1] - 2.0 * theta * sums[2] + theta * theta * sums[3]
-    for correlation in correlations:
-        length = length - 2.0 * correlation * correlation
-    for (i, j), value in zip(MEMBER_PAIRS, sums[10:]):
-        length = length + (1.0 if i == j else 2.0) * correlations[i] * correlations[j] * value
-    scale = lax.rsqrt(length + EPSILON)
-    half = own_image.shape[0]
-    mine = pl.ds(pl.multiple_of(op * half, half), half)
-    for place, (image, sector) in enumerate(((own_image, op), (mate_image, 1 - op))):
-        basis_ref[0, sector] = members[1, place]
-        basis_ref[1, sector] = members[2, place]
-        ortho = (image[...] - one_of(theta) * members[2, place]) * inverse[place, mine]
-        for i, correlation in enumerate(correlations):
-            ortho = ortho - one_of(correlation) * members[i, place]
-        basis_ref[2, sector] = ortho * one_of(scale)
-    for position, value in enumerate((thetas[0], thetas[1], theta)):
+        for i in range(ITERS):
+            basis_ref[i, sector] = combined(basis[i + 1], arrays, inverse[place, mine])
+    for position, value in enumerate(thetas):
         ritz_ref[position] = value[0, 0]
 
 
@@ -458,24 +476,40 @@
     (early_row,) = call(
         moments_kernel, (start, image, side, inverse), [((1, LANES), f32)], scratch=False
     )
-    second, row, ratio = call(
+    second, ratio = call(
         second_kernel,
-        (*shifts, start, *images, inverse, side, early_row, *blocks),
-        [(block, f32), row_shape, ((3,) + block, f32)],
+        (*shifts, *images, inverse, early_row, *blocks),
+        [(block, f32), ((3,) + block, f32)],
         scalars=2,
     )
     seconds = around(second)
-    row, *sides = lax.optimization_barrier((row, *sides))
     half_block = (half, columns)
-    kept, sent, row, members, thetas = call(
-        functools.partial(third_kernel, total),
-        (*shifts, exchanged(row), start, inverse, ratio, *sides, *seconds, *blocks),
-        [(half_block, f32)] * 2 + [row_shape, ((3, 2) + half_block, f32), ((2, 8, LANES), f32)],
+    extra, kept_extra, sent_extra, early_row = call(
+        extra_kernel,
+        (*shifts, start, ratio, inverse, image, side, second, early_row, *blocks),
+        [((2,) + block, f32)] + [((2,) + half_block, f32)] * 2 + [((1, LANES), f32)],
         scalars=2,
     )
+    mate_extra = mate(sent_extra)
+    further, kept_further, sent_further, early_row = call(
+        further_kernel,
+        (*shifts, start, inverse, image, *sides, second, extra, early_row, *blocks),
+        [(block, f32)] + [(half_block, f32)] * 2 + [((1, LANES), f32)],
+        scalars=2,
+    )
+    mate_further = mate(sent_further)
+    kept, sent, row = call(
+        third_kernel,
+        (*shifts, start, inverse, image, side, *seconds, extra, further, early_row, *blocks),
+        [(half_block, f32)] * 2 + [row_shape],
+        scalars=2,
+    )
+    mate_last = mate(sent)
+    row, mate_extra, mate_further = lax.optimization_barrier((row, mate_extra, mate_further))
     basis, ritz = call(
         functools.partial(last_kernel, total),
-        (exchanged(row), thetas, members, inverse, kept, mate(sent)),
+        (exchanged(row), start, ratio, inverse, *sides[:2], *seconds[:2], kept_extra, mate_extra,
+         kept_further, mate_further, kept, mate_last),
         [((ITERS, 2) + half_block, f32), ((ITERS,), f32)],
         out_scalars=1,
         scratch=False,

time: 60 us -> 59 us (0.983)
  blocking collectives: 22.7 us -> 14 us
  Pallas kernels: 12.6 us -> 19.5 us
  starting transfers between devices: 23.2 us -> 23.9 us
    all_to_all x2 -> x1, blocking collectives: 22.7 us -> 14 us  [exchanged(): lax.all_to_all(spread, AXES, 0, 0, tiled=True).reshape(devices, LANES)]
    pallas_call x7 -> x9, Pallas kernels: 11 us -> 17.9 us  [call(): pl.pallas_call(kernel, out_shape=[jax.ShapeDtypeStruct(shape, kind) for s...]
    ppermute x7 -> x9, starting transfers between devices: 19.6 us -> 20 us  [mate(): return lax.ppermute(values, AXES, swap)]
  transfers between devices with their start and end apart: 12 -> 14, of which waited for: 1 -> 1; matrix products, arithmetic and copies ran while one was open for 0% -> 0% of each run, Pallas kernels for 12% -> 27%
where the time goes in v7:
time: 59 us; the launch traced here: 58.8 us
  starting transfers between devices  23.9 us (41%)
  Pallas kernels  19.5 us (33%)
  blocking collectives  14 us (24%)
  between operations  0.98 us (2%)
    ppermute x9, starting transfers between devices, mate(): return lax.ppermute(values, AXES, swap)  20 us
    pallas_call x9, Pallas kernels, call(): pl.pallas_call(kernel, out_shape=[jax.ShapeDtypeStruct(shape, kind) for s...  17.9 us
    all_to_all x1, blocking collectives, exchanged(): lax.all_to_all(spread, AXES, 0, 0, tiled=True).reshape(devices, LANES)  14 us
    ppermute x5, starting transfers between devices, facing(): return lax.ppermute(values, AXES, across)  3.82 us
    pallas_call x1, Pallas kernels, one_sector_body(): pl.pallas_call(picking_kernel, out_shape=[jax.ShapeDtypeStruct(shape, f32...  1.55 us
  transfers between devices with their start and end apart: 14, of which 1 were waited for; matrix products, arithmetic and copies ran while one was open for 0% of the time, Pallas kernels for 27%

profile of v7, /device:TPU:0, one launch (start us, length us, event | category | flops | bytes accessed | tf_op | source)
XLA Modules:
  0.0 58.8 jit_solution(14306081280158625456)
XLA Ops:
  0.6 1.5 %shard_map.68 = (f32[256,256]{1,0:T(8,128)S(1)}, f32[256,256]{1,0:T(8,128)S(1)}, f32[2,256,256]{2,1,0:T(8,128)S(1)}, f32[2,256,256]{2,1,0:T(8,128)S(1)}) custom-call(f32[2,256,256]{2,1,0:T(8,128)} %wave.3, f32[2,256,256]{2,1,0:T(8,128)} %preconditioner.3, f32[2,2,256,256]{3,2,1,0:T(8,128)} %own_left.1, f32[2,2,256,256]{3,2,1,0:T(8,128)} %own_right.1), custom_call_target="tpu_custom_call" | custom-call | tf_op jit(solution)/shard_map/pallas_call | solution.py:438
  2.2 0.5 collective-permute-start.2
  2.7 0.1 collective-permute-start.3
  2.8 0.8 %collective-permute-start.1 = (f32[256,256]{1,0:T(8,128)S(1)}, f32[256,256]{1,0:T(8,128)S(1)}, u32[]{:S(2)}, u32[]{:S(2)}) collective-permute-start(f32[256,256]{1,0:T(8,128)S(1)} %get-tuple-element.30), channel_id=1, source_target_pairs={{1,2},{3,4},{5,6},{7,8},{9,10},{11,12},{13,14},{15,16},{17,18},{19... | collective-permute-start | bytes 786440 | tf_op jit(solution)/shard_map/ppermute | solution.py:411
  3.6 0.0 copy-start.2
  3.6 0.8 %collective-permute-start.4 = (f32[256,256]{1,0:T(8,128)S(1)}, f32[256,256]{1,0:T(8,128)S(1)}, u32[]{:S(2)}, u32[]{:S(2)}) collective-permute-start(f32[256,256]{1,0:T(8,128)S(1)} %get-tuple-element.38), channel_id=1, source_target_pairs={{1,2},{3,4},{5,6},{7,8},{9,10},{11,12},{13,14},{15,16},{17,18},{19... | collective-permute-start | bytes 786440 | tf_op jit(solution)/shard_map/ppermute | solution.py:411
  4.4 5.6 %collective-permute-start = (s32[2]{0:T(128)S(1)}, s32[2]{0:T(128)S(1)}, u32[]{:S(2)}, u32[]{:S(2)}) collective-permute-start(s32[2]{0:T(128)S(1)} %copy-done.4), channel_id=1, source_target_pairs={{0,1},{1,0},{2,3},{3,2},{4,5},{5,4},{6,7},{7,6},{8,9},{9,8},{10,11... | collective-permute-start | bytes 32 | tf_op jit(solution)/shard_map/ppermute | solution.py:408
  10.0 0.0 collective-permute-done.2.mate_left
  10.0 0.4 shard_map.69
  10.5 0.4 collective-permute-done.mate_shifts
  10.8 1.8 %shard_map.70 = (f32[256,256]{1,0:T(8,128)S(1)}, f32[3,256,256]{2,1,0:T(8,128)S(1)}) custom-call(s32[2]{0:T(128)S(1)} %copy-done.4, s32[2]{0:T(128)S(1)} %collective-permute-done.mate_shifts, f32[2,256,256]{2,1,0:T(8,128)S(1)} %copy-done.2, f32[256,256]{1,0:T(8,128)S(1)} %collective-permute-done.1.facing_wave, ...), custom_call_target="tpu_custom_call" | custom-call | tf_op jit(solution)/shard_map/pallas_call | solution.py:424
  12.6 0.7 %collective-permute-start.6 = (f32[256,256]{1,0:T(8,128)S(1)}, f32[256,256]{1,0:T(8,128)S(1)}, u32[]{:S(2)}, u32[]{:S(2)}) collective-permute-start(f32[256,256]{1,0:T(8,128)S(1)} %get-tuple-element.40.image.own_image), channel_id=1, source_target_pairs={{1,2},{3,4},{5,6},{7,8},{9,10},{11,12},{13,14},{15,16},{17,18},{19... | collective-permute-start | bytes 786440 | tf_op jit(solution)/shard_map/ppermute | solution.py:411
  13.3 6.9 %collective-permute-start.5 = (f32[256,256]{1,0:T(8,128)S(1)}, f32[256,256]{1,0:T(8,128)S(1)}, u32[]{:S(2)}, u32[]{:S(2)}) collective-permute-start(f32[256,256]{1,0:T(8,128)S(1)} %get-tuple-element.40.image.own_image), channel_id=1, source_target_pairs={{0,1},{1,0},{2,3},{3,2},{4,5},{5,4},{6,7},{7,6},{8,9},{9,8},{10,11... | collective-permute-start | bytes 786440 | tf_op jit(solution)/shard_map/ppermute | solution.py:408
  20.2 0.0 collective-permute-done.4.facing_preconditioner
  20.2 1.8 %shard_map.71 = (f32[256,256]{1,0:T(8,128)S(1)}, f32[3,256,256]{2,1,0:T(8,128)S(1)}) custom-call(s32[2]{0:T(128)S(1)} %copy-done.4, s32[2]{0:T(128)S(1)} %collective-permute-done.mate_shifts, f32[3,256,256]{2,1,0:T(8,128)S(1)} %get-tuple-element.37.start, f32[2,256,256]{2,1,0:T(8,128)S(1)} %copy-done.3, ...), custom_call_target="tpu_custom_call" | custom-call | tf_op jit(solution)/shard_map/pallas_call | solution.py:424
  22.1 0.7 %collective-permute-start.10 = (f32[256,256]{1,0:T(8,128)S(1)}, f32[256,256]{1,0:T(8,128)S(1)}, u32[]{:S(2)}, u32[]{:S(2)}) collective-permute-start(f32[256,256]{1,0:T(8,128)S(1)} %get-tuple-element.41.side.own_side), channel_id=1, source_target_pairs={{1,2},{3,4},{5,6},{7,8},{9,10},{11,12},{13,14},{15,16},{17,18},{19... | collective-permute-start | bytes 786440 | tf_op jit(solution)/shard_map/ppermute | solution.py:411
  22.8 3.8 %collective-permute-start.9 = (f32[256,256]{1,0:T(8,128)S(1)}, f32[256,256]{1,0:T(8,128)S(1)}, u32[]{:S(2)}, u32[]{:S(2)}) collective-permute-start(f32[256,256]{1,0:T(8,128)S(1)} %get-tuple-element.41.side.own_side), channel_id=1, source_target_pairs={{0,1},{1,0},{2,3},{3,2},{4,5},{5,4},{6,7},{7,6},{8,9},{9,8},{10,11... | collective-permute-start | bytes 786440 | tf_op jit(solution)/shard_map/ppermute | solution.py:408
  26.6 1.3 %shard_map.72._.early_row = f32[1,128]{1,0:T(1,128)S(1)} custom-call(f32[3,256,256]{2,1,0:T(8,128)S(1)} %get-tuple-element.37.start, f32[256,256]{1,0:T(8,128)S(1)} %get-tuple-element.40.image.own_image, f32[256,256]{1,0:T(8,128)S(1)} %get-tuple-element.41.side.own_side, f32[3,256,256]{2,1,0:T(8,128)S(1)} %get-tuple-element.39.inverse), custom_call_target="tpu_custom_call" | custom-call | tf_op jit(solution)/shard_map/pallas_call | solution.py:424
  27.8 0.0 collective-permute-done.6.facing_image
  27.9 1.8 %shard_map.73 = (f32[256,256]{1,0:T(8,128)S(1)}, f32[3,256,256]{2,1,0:T(8,128)S(1)}) custom-call(s32[2]{0:T(128)S(1)} %copy-done.4, s32[2]{0:T(128)S(1)} %collective-permute-done.mate_shifts, f32[256,256]{1,0:T(8,128)S(1)} %get-tuple-element.40.image.own_image, f32[256,256]{1,0:T(8,128)S(1)} %collective-permute-done.5.mate_image, ...), custom_call_target="tpu_custom_call" | custom-call | tf_op jit(solution)/shard_map/pallas_call | solution.py:424
  29.7 0.9 %collective-permute-start.8 = (f32[256,256]{1,0:T(8,128)S(1)}, f32[256,256]{1,0:T(8,128)S(1)}, u32[]{:S(2)}, u32[]{:S(2)}) collective-permute-start(f32[256,256]{1,0:T(8,128)S(1)} %get-tuple-element.42.second.own_second), channel_id=1, source_target_pairs={{1,2},{3,4},{5,6},{7,8},{9,10},{11,12},{13,14},{15,16},{17,18},{19... | collective-permute-start | bytes 786440 | tf_op jit(solution)/shard_map/ppermute | solution.py:411
  30.5 2.5 %collective-permute-start.7 = (f32[256,256]{1,0:T(8,128)S(1)}, f32[256,256]{1,0:T(8,128)S(1)}, u32[]{:S(2)}, u32[]{:S(2)}) collective-permute-start(f32[256,256]{1,0:T(8,128)S(1)} %get-tuple-element.42.second.own_second), channel_id=1, source_target_pairs={{0,1},{1,0},{2,3},{3,2},{4,5},{5,4},{6,7},{7,6},{8,9},{9,8},{10,11... | collective-permute-start | bytes 786440 | tf_op jit(solution)/shard_map/ppermute | solution.py:408
  33.0 4.1 %shard_map.74 = (f32[2,256,256]{2,1,0:T(8,128)S(1)}, f32[2,128,256]{2,1,0:T(8,128)S(1)}, f32[2,128,256]{2,1,0:T(8,128)S(1)}, f32[1,128]{1,0:T(1,128)S(1)}) custom-call(s32[2]{0:T(128)S(1)} %copy-done.4, s32[2]{0:T(128)S(1)} %collective-permute-done.mate_shifts, f32[3,256,256]{2,1,0:T(8,128)S(1)} %get-tuple-element.37.start, ...), custom_call_target="tpu_custom_call" | custom-call | tf_op jit(solution)/shard_map/pallas_call | solution.py:424
  37.1 0.1 collective-permute-start.11
  37.2 2.5 %shard_map.75 = (f32[256,256]{1,0:T(8,128)S(1)}, f32[128,256]{1,0:T(8,128)S(1)}, f32[128,256]{1,0:T(8,128)S(1)}, f32[1,128]{1,0:T(1,128)S(1)}) custom-call(s32[2]{0:T(128)S(1)} %copy-done.4, s32[2]{0:T(128)S(1)} %collective-permute-done.mate_shifts, f32[3,256,256]{2,1,0:T(8,128)S(1)} %get-tuple-element.37.start, ...), custom_call_target="tpu_custom_call" | custom-call | tf_op jit(solution)/shard_map/pallas_call | solution.py:424
  39.7 0.5 collective-permute-start.12
  40.2 0.0 collective-permute-done.8.facing_second
  40.2 2.5 %shard_map.76 = (f32[128,256]{1,0:T(8,128)S(1)}, f32[128,256]{1,0:T(8,128)S(1)}, f32[32,128]{1,0:T(8,128)S(1)}) custom-call(s32[2]{0:T(128)S(1)} %copy-done.4, s32[2]{0:T(128)S(1)} %collective-permute-done.mate_shifts, f32[3,256,256]{2,1,0:T(8,128)S(1)} %get-tuple-element.37.start, f32[3,256,256]{2,1,0:T(8,128)S(1)} %get-tuple-element.39.inverse, ...), custom_call_target="tpu_custom_call" | custom-call | tf_op jit(solution)/shard_map/pallas_call | solution.py:424
  42.7 0.1 collective-permute-start.13
  42.8 0.0 collective-permute-done.12.mate_further
  42.8 14.0 %all_to_all.5 = f32[32,1,128]{2,1,0:T(1,128)S(1)} all-to-all(f32[32,1,128]{2,1,0:T(1,128)S(1)} %bitcast.5), channel_id=1, replica_groups=mesh['sector'=16,'op'=2] {'sector','op'}, dimensions={0} | all-to-all | bytes 32768 | tf_op jit(solution)/shard_map/all_to_all | solution.py:418
  56.8 1.8 %shard_map.77 = (f32[3,2,128,256]{3,2,1,0:T(8,128)}, f32[3]{0:T(128)}) custom-call(f32[32,128]{1,0:T(8,128)S(1)} %bitcast.4, f32[3,256,256]{2,1,0:T(8,128)S(1)} %get-tuple-element.37.start, f32[3,256,256]{2,1,0:T(8,128)S(1)} %get-tuple-element.43.ratio, f32[3,256,256]{2,1,0:T(8,128)S(1)} %get-tuple-element.39.inverse, ...), custom_call_target="tpu_custom_call" | custom-call | tf_op jit(solution)/shard_map/pallas_call | solution.py:424
  (17 shorter events, 0.0 us)
Async XLA Ops:
  0.6 9.4 %copy-start.1 = (f32[2,2,256,256]{3,2,1,0:T(8,128)S(1)}, f32[2,2,256,256]{3,2,1,0:T(8,128)}, u32[]{:S(2)}) copy-start(f32[2,2,256,256]{3,2,1,0:T(8,128)} %own_right.1) | copy-start | bytes 3145732
  0.6 9.4 %copy-start = (f32[2,2,256,256]{3,2,1,0:T(8,128)S(1)}, f32[2,2,256,256]{3,2,1,0:T(8,128)}, u32[]{:S(2)}) copy-start(f32[2,2,256,256]{3,2,1,0:T(8,128)} %own_left.1) | copy-start | bytes 3145732
  2.2 7.8 %collective-permute-start.2 = (f32[2,256,256]{2,1,0:T(8,128)S(1)}, f32[2,256,256]{2,1,0:T(8,128)S(1)}, u32[]{:S(2)}, u32[]{:S(2)}) collective-permute-start(f32[2,256,256]{2,1,0:T(8,128)S(1)} %get-tuple-element.31), channel_id=1, source_target_pairs={{0,1},{1,0},{2,3},{3,2},{4,5},{5,4},{6,7},{7,6},{8,9},{9,8},{10,11... | collective-permute-start | bytes 1572872 | tf_op jit(solution)/shard_map/ppermute | solution.py:408
  2.7 7.3 %collective-permute-start.3 = (f32[2,256,256]{2,1,0:T(8,128)S(1)}, f32[2,256,256]{2,1,0:T(8,128)S(1)}, u32[]{:S(2)}, u32[]{:S(2)}) collective-permute-start(f32[2,256,256]{2,1,0:T(8,128)S(1)} %get-tuple-element.32), channel_id=1, source_target_pairs={{0,1},{1,0},{2,3},{3,2},{4,5},{5,4},{6,7},{7,6},{8,9},{9,8},{10,11... | collective-permute-start | bytes 1572872 | tf_op jit(solution)/shard_map/ppermute | solution.py:408
  2.8 1.6 %copy-start.4 = (s32[2]{0:T(128)S(1)}, s32[2]{0:T(128)}, u32[]{:S(2)}) copy-start(s32[2]{0:T(128)} %own_shifts.11) | copy-start | bytes 28
  2.8 8.0 %collective-permute-start.1 = (f32[256,256]{1,0:T(8,128)S(1)}, f32[256,256]{1,0:T(8,128)S(1)}, u32[]{:S(2)}, u32[]{:S(2)}) collective-permute-start(f32[256,256]{1,0:T(8,128)S(1)} %get-tuple-element.30), channel_id=1, source_target_pairs={{1,2},{3,4},{5,6},{7,8},{9,10},{11,12},{13,14},{15,16},{17,18},{19... | collective-permute-start | bytes 786440 | tf_op jit(solution)/shard_map/ppermute | solution.py:411
  3.6 7.2 %copy-start.2 = (f32[2,256,256]{2,1,0:T(8,128)S(1)}, f32[2,256,256]{2,1,0:T(8,128)}, u32[]{:S(2)}) copy-start(f32[2,256,256]{2,1,0:T(8,128)} %wave.3) | copy-start | bytes 1572868
  3.6 16.6 %collective-permute-start.4 = (f32[256,256]{1,0:T(8,128)S(1)}, f32[256,256]{1,0:T(8,128)S(1)}, u32[]{:S(2)}, u32[]{:S(2)}) collective-permute-start(f32[256,256]{1,0:T(8,128)S(1)} %get-tuple-element.38), channel_id=1, source_target_pairs={{1,2},{3,4},{5,6},{7,8},{9,10},{11,12},{13,14},{15,16},{17,18},{19... | collective-permute-start | bytes 786440 | tf_op jit(solution)/shard_map/ppermute | solution.py:411
  4.4 6.4 %collective-permute-start = (s32[2]{0:T(128)S(1)}, s32[2]{0:T(128)S(1)}, u32[]{:S(2)}, u32[]{:S(2)}) collective-permute-start(s32[2]{0:T(128)S(1)} %copy-done.4), channel_id=1, source_target_pairs={{0,1},{1,0},{2,3},{3,2},{4,5},{5,4},{6,7},{7,6},{8,9},{9,8},{10,11... | collective-permute-start | bytes 32 | tf_op jit(solution)/shard_map/ppermute | solution.py:408
  10.8 9.4 %copy-start.3 = (f32[2,256,256]{2,1,0:T(8,128)S(1)}, f32[2,256,256]{2,1,0:T(8,128)}, u32[]{:S(2)}) copy-start(f32[2,256,256]{2,1,0:T(8,128)} %preconditioner.3) | copy-start | bytes 1572868
  12.6 15.2 %collective-permute-start.6 = (f32[256,256]{1,0:T(8,128)S(1)}, f32[256,256]{1,0:T(8,128)S(1)}, u32[]{:S(2)}, u32[]{:S(2)}) collective-permute-start(f32[256,256]{1,0:T(8,128)S(1)} %get-tuple-element.40.image.own_image), channel_id=1, source_target_pairs={{1,2},{3,4},{5,6},{7,8},{9,10},{11,12},{13,14},{15,16},{17,18},{19... | collective-permute-start | bytes 786440 | tf_op jit(solution)/shard_map/ppermute | solution.py:411
  13.3 14.5 %collective-permute-start.5 = (f32[256,256]{1,0:T(8,128)S(1)}, f32[256,256]{1,0:T(8,128)S(1)}, u32[]{:S(2)}, u32[]{:S(2)}) collective-permute-start(f32[256,256]{1,0:T(8,128)S(1)} %get-tuple-element.40.image.own_image), channel_id=1, source_target_pairs={{0,1},{1,0},{2,3},{3,2},{4,5},{5,4},{6,7},{7,6},{8,9},{9,8},{10,11... | collective-permute-start | bytes 786440 | tf_op jit(solution)/shard_map/ppermute | solution.py:408
  22.1 15.1 %collective-permute-start.10 = (f32[256,256]{1,0:T(8,128)S(1)}, f32[256,256]{1,0:T(8,128)S(1)}, u32[]{:S(2)}, u32[]{:S(2)}) collective-permute-start(f32[256,256]{1,0:T(8,128)S(1)} %get-tuple-element.41.side.own_side), channel_id=1, source_target_pairs={{1,2},{3,4},{5,6},{7,8},{9,10},{11,12},{13,14},{15,16},{17,18},{19... | collective-permute-start | bytes 786440 | tf_op jit(solution)/shard_map/ppermute | solution.py:411
  22.8 14.4 %collective-permute-start.9 = (f32[256,256]{1,0:T(8,128)S(1)}, f32[256,256]{1,0:T(8,128)S(1)}, u32[]{:S(2)}, u32[]{:S(2)}) collective-permute-start(f32[256,256]{1,0:T(8,128)S(1)} %get-tuple-element.41.side.own_side), channel_id=1, source_target_pairs={{0,1},{1,0},{2,3},{3,2},{4,5},{5,4},{6,7},{7,6},{8,9},{9,8},{10,11... | collective-permute-start | bytes 786440 | tf_op jit(solution)/shard_map/ppermute | solution.py:408
  29.7 10.5 %collective-permute-start.8 = (f32[256,256]{1,0:T(8,128)S(1)}, f32[256,256]{1,0:T(8,128)S(1)}, u32[]{:S(2)}, u32[]{:S(2)}) collective-permute-start(f32[256,256]{1,0:T(8,128)S(1)} %get-tuple-element.42.second.own_second), channel_id=1, source_target_pairs={{1,2},{3,4},{5,6},{7,8},{9,10},{11,12},{13,14},{15,16},{17,18},{19... | collective-permute-start | bytes 786440 | tf_op jit(solution)/shard_map/ppermute | solution.py:411
  30.5 9.7 %collective-permute-start.7 = (f32[256,256]{1,0:T(8,128)S(1)}, f32[256,256]{1,0:T(8,128)S(1)}, u32[]{:S(2)}, u32[]{:S(2)}) collective-permute-start(f32[256,256]{1,0:T(8,128)S(1)} %get-tuple-element.42.second.own_second), channel_id=1, source_target_pairs={{0,1},{1,0},{2,3},{3,2},{4,5},{5,4},{6,7},{7,6},{8,9},{9,8},{10,11... | collective-permute-start | bytes 786440 | tf_op jit(solution)/shard_map/ppermute | solution.py:408
  37.1 5.7 %collective-permute-start.11 = (f32[2,128,256]{2,1,0:T(8,128)S(1)}, f32[2,128,256]{2,1,0:T(8,128)S(1)}, u32[]{:S(2)}, u32[]{:S(2)}) collective-permute-start(f32[2,128,256]{2,1,0:T(8,128)S(1)} %get-tuple-element.49), channel_id=1, source_target_pairs={{0,1},{1,0},{2,3},{3,2},{4,5},{5,4},{6,7},{7,6},{8,9},{9,8},{10,11... | collective-permute-start | bytes 786440 | tf_op jit(solution)/shard_map/ppermute | solution.py:408
  39.7 3.1 %collective-permute-start.12 = (f32[128,256]{1,0:T(8,128)S(1)}, f32[128,256]{1,0:T(8,128)S(1)}, u32[]{:S(2)}, u32[]{:S(2)}) collective-permute-start(f32[128,256]{1,0:T(8,128)S(1)} %get-tuple-element.50), channel_id=1, source_target_pairs={{0,1},{1,0},{2,3},{3,2},{4,5},{5,4},{6,7},{7,6},{8,9},{9,8},{10,11... | collective-permute-start | bytes 393224 | tf_op jit(solution)/shard_map/ppermute | solution.py:408
  42.7 14.1 %collective-permute-start.13 = (f32[128,256]{1,0:T(8,128)S(1)}, f32[128,256]{1,0:T(8,128)S(1)}, u32[]{:S(2)}, u32[]{:S(2)}) collective-permute-start(f32[128,256]{1,0:T(8,128)S(1)} %get-tuple-element.57), channel_id=1, source_target_pairs={{0,1},{1,0},{2,3},{3,2},{4,5},{5,4},{6,7},{7,6},{8,9},{9,8},{10,11... | collective-permute-start | bytes 393224 | tf_op jit(solution)/shard_map/ppermute | solution.py:408

commit v8 on v7

--- a/solution.py
+++ b/solution.py
@@ -89,13 +89,32 @@
     ]
 
 
-def row_of_sums(factors, first=0, row=None):
+CHUNK = 32
+
+
+def row_of_sums(moments, refs, inverse, first=0, row=None):
+    rows, columns = inverse.shape
     lane = lax.broadcasted_iota(jnp.int32, (1, LANES), 1)
     if row is None:
         row = jnp.zeros((1, LANES), jnp.float32)
-    for position, (one, other) in enumerate(factors):
-        product = (one * other).reshape(-1, 8, one.shape[1])
-        whole = jnp.sum(jnp.sum(product, axis=0), axis=(0, 1), keepdims=True)
+    pairs = {}
+    for x, y, n in moments:
+        pairs.setdefault((x, y), []).append(n)
+    totals = {}
+    for top in range(0, rows, CHUNK):
+        here = pl.ds(top, CHUNK)
+        powers = [None, inverse[here]]
+        while len(powers) <= max(n for _, _, n in moments):
+            powers.append(powers[-1] * powers[1])
+        for (x, y), orders in pairs.items():
+            product = refs[x][here] * refs[y][here]
+            for n in orders:
+                weighted = product * powers[n] if n else product
+                part = jnp.sum(weighted.reshape(-1, 8, columns), axis=0)
+                part = sum(part[:, i : i + LANES] for i in range(0, columns, LANES))
+                totals[x, y, n] = totals[x, y, n] + part if top else part
+    for position, moment in enumerate(moments):
+        whole = jnp.sum(totals[moment], axis=(0, 1), keepdims=True)
         row = jnp.where(lane == first + position, whole, row)
     return row
 
@@ -121,17 +140,6 @@
 
 START_SCALE = 2.0**10
 H_SCALE = 2.0**7
-
-
-def moment_factors(moments, arrays, inverse):
-    powers = {(name, 0): values for name, values in arrays.items()}
-
-    def power(name, n):
-        if (name, n) not in powers:
-            powers[name, n] = power(name, n - 1) * inverse
-        return powers[name, n]
-
-    return [(power(x, n // 2), power(y, n - n // 2)) for x, y, n in moments]
 
 
 def plus(vector, other, factor):
@@ -283,8 +291,8 @@
 
 
 def moments_kernel(start, image, side, inverse, row_ref):
-    arrays = {"w": start[0], "u": image[...], "a": side[...]}
-    row_ref[...] = row_of_sums(moment_factors(MOMENTS[0], arrays, inverse[0]))
+    refs = {"w": start.at[0], "u": image, "a": side}
+    row_ref[...] = row_of_sums(MOMENTS[0], refs, inverse.at[0])
 
 
 def second_kernel(
@@ -313,17 +321,16 @@
     left_high, left_low, right_high, right_low, extra_ref, kept_ref, sent_ref, row_ref, high, low,
 ):
     sources = term_sources(own_shifts, mate_shifts)
-    arrays = {"w": start[0], "u": image[...], "a": side[...], "b": second[...]}
+    refs = {"w": start.at[0], "u": image, "a": side, "b": second}
     for i, name in enumerate("cd"):
         for place in range(3):
             once = start[place] * inverse[place] if name == "c" else ratio[place]
             high[place], low[place] = split(once * inverse[place])
         extra = apply_terms(sources, (high, low), (left_high, left_low), (right_high, right_low))
-        arrays[name] = extra
+        refs[name] = extra_ref.at[i]
         extra_ref[i] = extra
         halves(extra, kept_ref.at[i], sent_ref.at[i])
-    factors = moment_factors(MOMENTS[1], arrays, inverse[0])
-    row_ref[...] = row_of_sums(factors, FIRST_LANE[1], early_row[...])
+    row_ref[...] = row_of_sums(MOMENTS[1], refs, inverse.at[0], FIRST_LANE[1], early_row[...])
 
 
 def further_kernel(
@@ -337,26 +344,25 @@
     further = apply_terms(sources, (high, low), (left_high, left_low), (right_high, right_low))
     further_ref[...] = further
     halves(further, kept_ref, sent_ref)
-    arrays = {"w": start[0], "u": image[...], "a": own_side[...], "b": second[...]}
-    arrays.update(c=extra[0], d=extra[1], e=further)
-    factors = moment_factors(MOMENTS[2], arrays, inverse[0])
-    row_ref[...] = row_of_sums(factors, FIRST_LANE[2], early_row[...])
+    refs = {"w": start.at[0], "u": image, "a": own_side, "b": second}
+    refs.update(c=extra.at[0], d=extra.at[1], e=further_ref)
+    row_ref[...] = row_of_sums(MOMENTS[2], refs, inverse.at[0], FIRST_LANE[2], early_row[...])
 
 
 def third_kernel(
     own_shifts, mate_shifts, start, inverse, image, side, own_second, mate_second, facing_second,
     extra, further, early_row, left_high, left_low, right_high, right_low,
-    kept_ref, sent_ref, row_ref, high, low,
+    kept_ref, sent_ref, row_ref, high, low, last_ref,
 ):
     sources = term_sources(own_shifts, mate_shifts)
     for place, second in enumerate((own_second, mate_second, facing_second)):
         high[place], low[place] = split(second[...] * inverse[place])
     last = apply_terms(sources, (high, low), (left_high, left_low), (right_high, right_low))
     halves(last, kept_ref, sent_ref)
-    arrays = {"w": start[0], "u": image[...], "a": side[...], "b": own_second[...]}
-    arrays.update(c=extra[0], d=extra[1], e=further[...], f=last)
-    factors = moment_factors(MOMENTS[3], arrays, inverse[0])
-    row = row_of_sums(factors, FIRST_LANE[3], early_row[...])
+    last_ref[...] = last
+    refs = {"w": start.at[0], "u": image, "a": side, "b": own_second}
+    refs.update(c=extra.at[0], d=extra.at[1], e=further, f=last_ref)
+    row = row_of_sums(MOMENTS[3], refs, inverse.at[0], FIRST_LANE[3], early_row[...])
     row_ref[...] = jnp.broadcast_to(row, row_ref.shape)
 
 
@@ -420,13 +426,16 @@
     vmem = pl.BlockSpec(memory_space=pltpu.VMEM)
     smem = pl.BlockSpec(memory_space=pltpu.SMEM)
 
-    def call(kernel, operands, shapes, scalars=0, out_scalars=0, scratch=True):
+    def call(
+        kernel, operands, shapes, scalars=0, out_scalars=0, scratch=True, more_scratch=()
+    ):
         return pl.pallas_call(
             kernel,
             out_shape=[jax.ShapeDtypeStruct(shape, kind) for shape, kind in shapes],
             in_specs=[smem] * scalars + [vmem] * (len(operands) - scalars),
             out_specs=[vmem] * (len(shapes) - out_scalars) + [smem] * out_scalars,
-            scratch_shapes=[pltpu.VMEM((3, rows, columns), jnp.bfloat16)] * (2 if scratch else 0),
+            scratch_shapes=[pltpu.VMEM((3, rows, columns), jnp.bfloat16)] * (2 if scratch else 0)
+            + list(more_scratch),
             compiler_params=pltpu.CompilerParams(vmem_limit_bytes=16 * 2**20),
         )(*operands)
 
@@ -503,6 +512,7 @@
         (*shifts, start, inverse, image, side, *seconds, extra, further, early_row, *blocks),
         [(half_block, f32)] * 2 + [row_shape],
         scalars=2,
+        more_scratch=[pltpu.VMEM(block, f32)],
     )
     mate_last = mate(sent)
     row, mate_extra, mate_further = lax.optimization_barrier((row, mate_extra, mate_further))

time: 59 us -> 58 us (0.983)
  Pallas kernels: 19.5 us -> 18.8 us
    pallas_call x9, Pallas kernels: 17.9 us -> 17.3 us  [call(): pl.pallas_call(kernel, out_shape=[jax.ShapeDtypeStruct(shape, kind) for s...]
where the time goes in v8:
time: 58 us; the launch traced here: 57.7 us
  starting transfers between devices  23.8 us (41%)
  Pallas kernels  18.8 us (32%)
  blocking collectives  13.9 us (24%)
  between operations  0.83 us (1%)
    ppermute x9, starting transfers between devices, mate(): return lax.ppermute(values, AXES, swap)  20.2 us
    pallas_call x9, Pallas kernels, call(): pl.pallas_call(kernel, out_shape=[jax.ShapeDtypeStruct(shape, kind) for s...  17.3 us
    all_to_all x1, blocking collectives, exchanged(): lax.all_to_all(spread, AXES, 0, 0, tiled=True).reshape(devices, LANES)  13.9 us
    ppermute x5, starting transfers between devices, facing(): return lax.ppermute(values, AXES, across)  3.64 us
    pallas_call x1, Pallas kernels, one_sector_body(): pl.pallas_call(picking_kernel, out_shape=[jax.ShapeDtypeStruct(shape, f32...  1.55 us
  transfers between devices with their start and end apart: 14, of which 1 were waited for; matrix products, arithmetic and copies ran while one was open for 0% of the time, Pallas kernels for 27%

profile of v8, /device:TPU:0, one launch (start us, length us, event | category | flops | bytes accessed | tf_op | source)
XLA Modules:
  0.0 57.7 jit_solution(14373504998094718191)
XLA Ops:
  0.6 1.5 %shard_map.68 = (f32[256,256]{1,0:T(8,128)S(1)}, f32[256,256]{1,0:T(8,128)S(1)}, f32[2,256,256]{2,1,0:T(8,128)S(1)}, f32[2,256,256]{2,1,0:T(8,128)S(1)}) custom-call(f32[2,256,256]{2,1,0:T(8,128)} %wave.3, f32[2,256,256]{2,1,0:T(8,128)} %preconditioner.3, f32[2,2,256,256]{3,2,1,0:T(8,128)} %own_left.1, f32[2,2,256,256]{3,2,1,0:T(8,128)} %own_right.1), custom_call_target="tpu_custom_call" | custom-call | tf_op jit(solution)/shard_map/pallas_call | solution.py:447
  2.2 0.5 collective-permute-start.2
  2.7 0.1 collective-permute-start.3
  2.8 0.8 %collective-permute-start.1 = (f32[256,256]{1,0:T(8,128)S(1)}, f32[256,256]{1,0:T(8,128)S(1)}, u32[]{:S(2)}, u32[]{:S(2)}) collective-permute-start(f32[256,256]{1,0:T(8,128)S(1)} %get-tuple-element.30), channel_id=1, source_target_pairs={{1,2},{3,4},{5,6},{7,8},{9,10},{11,12},{13,14},{15,16},{17,18},{19... | collective-permute-start | bytes 786440 | tf_op jit(solution)/shard_map/ppermute | solution.py:417
  3.6 0.0 copy-start.2
  3.6 0.8 %collective-permute-start.4 = (f32[256,256]{1,0:T(8,128)S(1)}, f32[256,256]{1,0:T(8,128)S(1)}, u32[]{:S(2)}, u32[]{:S(2)}) collective-permute-start(f32[256,256]{1,0:T(8,128)S(1)} %get-tuple-element.38), channel_id=1, source_target_pairs={{1,2},{3,4},{5,6},{7,8},{9,10},{11,12},{13,14},{15,16},{17,18},{19... | collective-permute-start | bytes 786440 | tf_op jit(solution)/shard_map/ppermute | solution.py:417
  4.4 5.6 %collective-permute-start = (s32[2]{0:T(128)S(1)}, s32[2]{0:T(128)S(1)}, u32[]{:S(2)}, u32[]{:S(2)}) collective-permute-start(s32[2]{0:T(128)S(1)} %copy-done.4), channel_id=1, source_target_pairs={{0,1},{1,0},{2,3},{3,2},{4,5},{5,4},{6,7},{7,6},{8,9},{9,8},{10,11... | collective-permute-start | bytes 32 | tf_op jit(solution)/shard_map/ppermute | solution.py:414
  10.0 0.0 collective-permute-done.2.mate_left
  10.0 0.0 collective-permute-done.3.mate_right
  10.0 0.4 shard_map.69
  10.5 0.4 collective-permute-done.mate_shifts
  10.8 1.8 %shard_map.70 = (f32[256,256]{1,0:T(8,128)S(1)}, f32[3,256,256]{2,1,0:T(8,128)S(1)}) custom-call(s32[2]{0:T(128)S(1)} %copy-done.4, s32[2]{0:T(128)S(1)} %collective-permute-done.mate_shifts, f32[2,256,256]{2,1,0:T(8,128)S(1)} %copy-done.2, f32[256,256]{1,0:T(8,128)S(1)} %collective-permute-done.1.facing_wave, ...), custom_call_target="tpu_custom_call" | custom-call | tf_op jit(solution)/shard_map/pallas_call | solution.py:432
  12.6 0.7 %collective-permute-start.6 = (f32[256,256]{1,0:T(8,128)S(1)}, f32[256,256]{1,0:T(8,128)S(1)}, u32[]{:S(2)}, u32[]{:S(2)}) collective-permute-start(f32[256,256]{1,0:T(8,128)S(1)} %get-tuple-element.40.image.own_image), channel_id=1, source_target_pairs={{1,2},{3,4},{5,6},{7,8},{9,10},{11,12},{13,14},{15,16},{17,18},{19... | collective-permute-start | bytes 786440 | tf_op jit(solution)/shard_map/ppermute | solution.py:417
  13.3 6.9 %collective-permute-start.5 = (f32[256,256]{1,0:T(8,128)S(1)}, f32[256,256]{1,0:T(8,128)S(1)}, u32[]{:S(2)}, u32[]{:S(2)}) collective-permute-start(f32[256,256]{1,0:T(8,128)S(1)} %get-tuple-element.40.image.own_image), channel_id=1, source_target_pairs={{0,1},{1,0},{2,3},{3,2},{4,5},{5,4},{6,7},{7,6},{8,9},{9,8},{10,11... | collective-permute-start | bytes 786440 | tf_op jit(solution)/shard_map/ppermute | solution.py:414
  20.2 1.8 %shard_map.71 = (f32[256,256]{1,0:T(8,128)S(1)}, f32[3,256,256]{2,1,0:T(8,128)S(1)}) custom-call(s32[2]{0:T(128)S(1)} %copy-done.4, s32[2]{0:T(128)S(1)} %collective-permute-done.mate_shifts, f32[3,256,256]{2,1,0:T(8,128)S(1)} %get-tuple-element.37.start, f32[2,256,256]{2,1,0:T(8,128)S(1)} %copy-done.3, ...), custom_call_target="tpu_custom_call" | custom-call | tf_op jit(solution)/shard_map/pallas_call | solution.py:432
  22.1 0.7 %collective-permute-start.10 = (f32[256,256]{1,0:T(8,128)S(1)}, f32[256,256]{1,0:T(8,128)S(1)}, u32[]{:S(2)}, u32[]{:S(2)}) collective-permute-start(f32[256,256]{1,0:T(8,128)S(1)} %get-tuple-element.41.side.own_side), channel_id=1, source_target_pairs={{1,2},{3,4},{5,6},{7,8},{9,10},{11,12},{13,14},{15,16},{17,18},{19... | collective-permute-start | bytes 786440 | tf_op jit(solution)/shard_map/ppermute | solution.py:417
  22.8 3.8 %collective-permute-start.9 = (f32[256,256]{1,0:T(8,128)S(1)}, f32[256,256]{1,0:T(8,128)S(1)}, u32[]{:S(2)}, u32[]{:S(2)}) collective-permute-start(f32[256,256]{1,0:T(8,128)S(1)} %get-tuple-element.41.side.own_side), channel_id=1, source_target_pairs={{0,1},{1,0},{2,3},{3,2},{4,5},{5,4},{6,7},{7,6},{8,9},{9,8},{10,11... | collective-permute-start | bytes 786440 | tf_op jit(solution)/shard_map/ppermute | solution.py:414
  26.6 1.0 %shard_map.72._.early_row = f32[1,128]{1,0:T(1,128)S(1)} custom-call(f32[3,256,256]{2,1,0:T(8,128)S(1)} %get-tuple-element.37.start, f32[256,256]{1,0:T(8,128)S(1)} %get-tuple-element.40.image.own_image, f32[256,256]{1,0:T(8,128)S(1)} %get-tuple-element.41.side.own_side, f32[3,256,256]{2,1,0:T(8,128)S(1)} %get-tuple-element.39.inverse), custom_call_target="tpu_custom_call" | custom-call | tf_op jit(solution)/shard_map/pallas_call | solution.py:432
  27.5 0.0 collective-permute-done.5.mate_image
  27.6 1.8 %shard_map.73 = (f32[256,256]{1,0:T(8,128)S(1)}, f32[3,256,256]{2,1,0:T(8,128)S(1)}) custom-call(s32[2]{0:T(128)S(1)} %copy-done.4, s32[2]{0:T(128)S(1)} %collective-permute-done.mate_shifts, f32[256,256]{1,0:T(8,128)S(1)} %get-tuple-element.40.image.own_image, f32[256,256]{1,0:T(8,128)S(1)} %collective-permute-done.5.mate_image, ...), custom_call_target="tpu_custom_call" | custom-call | tf_op jit(solution)/shard_map/pallas_call | solution.py:432
  29.4 0.7 %collective-permute-start.8 = (f32[256,256]{1,0:T(8,128)S(1)}, f32[256,256]{1,0:T(8,128)S(1)}, u32[]{:S(2)}, u32[]{:S(2)}) collective-permute-start(f32[256,256]{1,0:T(8,128)S(1)} %get-tuple-element.42.second.own_second), channel_id=1, source_target_pairs={{1,2},{3,4},{5,6},{7,8},{9,10},{11,12},{13,14},{15,16},{17,18},{19... | collective-permute-start | bytes 786440 | tf_op jit(solution)/shard_map/ppermute | solution.py:417
  30.1 2.5 %collective-permute-start.7 = (f32[256,256]{1,0:T(8,128)S(1)}, f32[256,256]{1,0:T(8,128)S(1)}, u32[]{:S(2)}, u32[]{:S(2)}) collective-permute-start(f32[256,256]{1,0:T(8,128)S(1)} %get-tuple-element.42.second.own_second), channel_id=1, source_target_pairs={{0,1},{1,0},{2,3},{3,2},{4,5},{5,4},{6,7},{7,6},{8,9},{9,8},{10,11... | collective-permute-start | bytes 786440 | tf_op jit(solution)/shard_map/ppermute | solution.py:414
  32.6 3.9 %shard_map.74 = (f32[2,256,256]{2,1,0:T(8,128)S(1)}, f32[2,128,256]{2,1,0:T(8,128)S(1)}, f32[2,128,256]{2,1,0:T(8,128)S(1)}, f32[1,128]{1,0:T(1,128)S(1)}) custom-call(s32[2]{0:T(128)S(1)} %copy-done.4, s32[2]{0:T(128)S(1)} %collective-permute-done.mate_shifts, f32[3,256,256]{2,1,0:T(8,128)S(1)} %get-tuple-element.37.start, ...), custom_call_target="tpu_custom_call" | custom-call | tf_op jit(solution)/shard_map/pallas_call | solution.py:432
  36.5 0.1 collective-permute-start.11
  36.6 0.0 collective-permute-done.9.mate_side
  36.6 2.4 %shard_map.75 = (f32[256,256]{1,0:T(8,128)S(1)}, f32[128,256]{1,0:T(8,128)S(1)}, f32[128,256]{1,0:T(8,128)S(1)}, f32[1,128]{1,0:T(1,128)S(1)}) custom-call(s32[2]{0:T(128)S(1)} %copy-done.4, s32[2]{0:T(128)S(1)} %collective-permute-done.mate_shifts, f32[3,256,256]{2,1,0:T(8,128)S(1)} %get-tuple-element.37.start, ...), custom_call_target="tpu_custom_call" | custom-call | tf_op jit(solution)/shard_map/pallas_call | solution.py:432
  39.0 0.5 collective-permute-start.12
  39.5 0.0 collective-permute-done.8.facing_second
  39.5 2.4 %shard_map.76 = (f32[128,256]{1,0:T(8,128)S(1)}, f32[128,256]{1,0:T(8,128)S(1)}, f32[32,128]{1,0:T(8,128)S(1)}) custom-call(s32[2]{0:T(128)S(1)} %copy-done.4, s32[2]{0:T(128)S(1)} %collective-permute-done.mate_shifts, f32[3,256,256]{2,1,0:T(8,128)S(1)} %get-tuple-element.37.start, f32[3,256,256]{2,1,0:T(8,128)S(1)} %get-tuple-element.39.inverse, ...), custom_call_target="tpu_custom_call" | custom-call | tf_op jit(solution)/shard_map/pallas_call | solution.py:432
  41.9 0.2 collective-permute-start.13
  42.1 13.9 %all_to_all.5 = f32[32,1,128]{2,1,0:T(1,128)S(1)} all-to-all(f32[32,1,128]{2,1,0:T(1,128)S(1)} %bitcast.5), channel_id=1, replica_groups=mesh['sector'=16,'op'=2] {'sector','op'}, dimensions={0} | all-to-all | bytes 32768 | tf_op jit(solution)/shard_map/all_to_all | solution.py:424
  55.9 1.8 %shard_map.77 = (f32[3,2,128,256]{3,2,1,0:T(8,128)}, f32[3]{0:T(128)}) custom-call(f32[32,128]{1,0:T(8,128)S(1)} %bitcast.4, f32[3,256,256]{2,1,0:T(8,128)S(1)} %get-tuple-element.37.start, f32[3,256,256]{2,1,0:T(8,128)S(1)} %get-tuple-element.43.ratio, f32[3,256,256]{2,1,0:T(8,128)S(1)} %get-tuple-element.39.inverse, ...), custom_call_target="tpu_custom_call" | custom-call | tf_op jit(solution)/shard_map/pallas_call | solution.py:432
  (17 shorter events, 0.0 us)
Async XLA Ops:
  0.6 9.4 %copy-start.1 = (f32[2,2,256,256]{3,2,1,0:T(8,128)S(1)}, f32[2,2,256,256]{3,2,1,0:T(8,128)}, u32[]{:S(2)}) copy-start(f32[2,2,256,256]{3,2,1,0:T(8,128)} %own_right.1) | copy-start | bytes 3145732
  0.6 9.4 %copy-start = (f32[2,2,256,256]{3,2,1,0:T(8,128)S(1)}, f32[2,2,256,256]{3,2,1,0:T(8,128)}, u32[]{:S(2)}) copy-start(f32[2,2,256,256]{3,2,1,0:T(8,128)} %own_left.1) | copy-start | bytes 3145732
  2.2 7.8 %collective-permute-start.2 = (f32[2,256,256]{2,1,0:T(8,128)S(1)}, f32[2,256,256]{2,1,0:T(8,128)S(1)}, u32[]{:S(2)}, u32[]{:S(2)}) collective-permute-start(f32[2,256,256]{2,1,0:T(8,128)S(1)} %get-tuple-element.31), channel_id=1, source_target_pairs={{0,1},{1,0},{2,3},{3,2},{4,5},{5,4},{6,7},{7,6},{8,9},{9,8},{10,11... | collective-permute-start | bytes 1572872 | tf_op jit(solution)/shard_map/ppermute | solution.py:414
  2.7 7.3 %collective-permute-start.3 = (f32[2,256,256]{2,1,0:T(8,128)S(1)}, f32[2,256,256]{2,1,0:T(8,128)S(1)}, u32[]{:S(2)}, u32[]{:S(2)}) collective-permute-start(f32[2,256,256]{2,1,0:T(8,128)S(1)} %get-tuple-element.32), channel_id=1, source_target_pairs={{0,1},{1,0},{2,3},{3,2},{4,5},{5,4},{6,7},{7,6},{8,9},{9,8},{10,11... | collective-permute-start | bytes 1572872 | tf_op jit(solution)/shard_map/ppermute | solution.py:414
  2.8 1.6 %copy-start.4 = (s32[2]{0:T(128)S(1)}, s32[2]{0:T(128)}, u32[]{:S(2)}) copy-start(s32[2]{0:T(128)} %own_shifts.11) | copy-start | bytes 28
  2.8 8.0 %collective-permute-start.1 = (f32[256,256]{1,0:T(8,128)S(1)}, f32[256,256]{1,0:T(8,128)S(1)}, u32[]{:S(2)}, u32[]{:S(2)}) collective-permute-start(f32[256,256]{1,0:T(8,128)S(1)} %get-tuple-element.30), channel_id=1, source_target_pairs={{1,2},{3,4},{5,6},{7,8},{9,10},{11,12},{13,14},{15,16},{17,18},{19... | collective-permute-start | bytes 786440 | tf_op jit(solution)/shard_map/ppermute | solution.py:417
  3.6 7.2 %copy-start.2 = (f32[2,256,256]{2,1,0:T(8,128)S(1)}, f32[2,256,256]{2,1,0:T(8,128)}, u32[]{:S(2)}) copy-start(f32[2,256,256]{2,1,0:T(8,128)} %wave.3) | copy-start | bytes 1572868
  3.6 16.6 %collective-permute-start.4 = (f32[256,256]{1,0:T(8,128)S(1)}, f32[256,256]{1,0:T(8,128)S(1)}, u32[]{:S(2)}, u32[]{:S(2)}) collective-permute-start(f32[256,256]{1,0:T(8,128)S(1)} %get-tuple-element.38), channel_id=1, source_target_pairs={{1,2},{3,4},{5,6},{7,8},{9,10},{11,12},{13,14},{15,16},{17,18},{19... | collective-permute-start | bytes 786440 | tf_op jit(solution)/shard_map/ppermute | solution.py:417
  4.4 6.4 %collective-permute-start = (s32[2]{0:T(128)S(1)}, s32[2]{0:T(128)S(1)}, u32[]{:S(2)}, u32[]{:S(2)}) collective-permute-start(s32[2]{0:T(128)S(1)} %copy-done.4), channel_id=1, source_target_pairs={{0,1},{1,0},{2,3},{3,2},{4,5},{5,4},{6,7},{7,6},{8,9},{9,8},{10,11... | collective-permute-start | bytes 32 | tf_op jit(solution)/shard_map/ppermute | solution.py:414
  10.8 9.4 %copy-start.3 = (f32[2,256,256]{2,1,0:T(8,128)S(1)}, f32[2,256,256]{2,1,0:T(8,128)}, u32[]{:S(2)}) copy-start(f32[2,256,256]{2,1,0:T(8,128)} %preconditioner.3) | copy-start | bytes 1572868
  12.6 14.9 %collective-permute-start.6 = (f32[256,256]{1,0:T(8,128)S(1)}, f32[256,256]{1,0:T(8,128)S(1)}, u32[]{:S(2)}, u32[]{:S(2)}) collective-permute-start(f32[256,256]{1,0:T(8,128)S(1)} %get-tuple-element.40.image.own_image), channel_id=1, source_target_pairs={{1,2},{3,4},{5,6},{7,8},{9,10},{11,12},{13,14},{15,16},{17,18},{19... | collective-permute-start | bytes 786440 | tf_op jit(solution)/shard_map/ppermute | solution.py:417
  13.3 14.2 %collective-permute-start.5 = (f32[256,256]{1,0:T(8,128)S(1)}, f32[256,256]{1,0:T(8,128)S(1)}, u32[]{:S(2)}, u32[]{:S(2)}) collective-permute-start(f32[256,256]{1,0:T(8,128)S(1)} %get-tuple-element.40.image.own_image), channel_id=1, source_target_pairs={{0,1},{1,0},{2,3},{3,2},{4,5},{5,4},{6,7},{7,6},{8,9},{9,8},{10,11... | collective-permute-start | bytes 786440 | tf_op jit(solution)/shard_map/ppermute | solution.py:414
  22.1 14.4 %collective-permute-start.10 = (f32[256,256]{1,0:T(8,128)S(1)}, f32[256,256]{1,0:T(8,128)S(1)}, u32[]{:S(2)}, u32[]{:S(2)}) collective-permute-start(f32[256,256]{1,0:T(8,128)S(1)} %get-tuple-element.41.side.own_side), channel_id=1, source_target_pairs={{1,2},{3,4},{5,6},{7,8},{9,10},{11,12},{13,14},{15,16},{17,18},{19... | collective-permute-start | bytes 786440 | tf_op jit(solution)/shard_map/ppermute | solution.py:417
  22.8 13.8 %collective-permute-start.9 = (f32[256,256]{1,0:T(8,128)S(1)}, f32[256,256]{1,0:T(8,128)S(1)}, u32[]{:S(2)}, u32[]{:S(2)}) collective-permute-start(f32[256,256]{1,0:T(8,128)S(1)} %get-tuple-element.41.side.own_side), channel_id=1, source_target_pairs={{0,1},{1,0},{2,3},{3,2},{4,5},{5,4},{6,7},{7,6},{8,9},{9,8},{10,11... | collective-permute-start | bytes 786440 | tf_op jit(solution)/shard_map/ppermute | solution.py:414
  29.4 10.1 %collective-permute-start.8 = (f32[256,256]{1,0:T(8,128)S(1)}, f32[256,256]{1,0:T(8,128)S(1)}, u32[]{:S(2)}, u32[]{:S(2)}) collective-permute-start(f32[256,256]{1,0:T(8,128)S(1)} %get-tuple-element.42.second.own_second), channel_id=1, source_target_pairs={{1,2},{3,4},{5,6},{7,8},{9,10},{11,12},{13,14},{15,16},{17,18},{19... | collective-permute-start | bytes 786440 | tf_op jit(solution)/shard_map/ppermute | solution.py:417
  30.1 9.4 %collective-permute-start.7 = (f32[256,256]{1,0:T(8,128)S(1)}, f32[256,256]{1,0:T(8,128)S(1)}, u32[]{:S(2)}, u32[]{:S(2)}) collective-permute-start(f32[256,256]{1,0:T(8,128)S(1)} %get-tuple-element.42.second.own_second), channel_id=1, source_target_pairs={{0,1},{1,0},{2,3},{3,2},{4,5},{5,4},{6,7},{7,6},{8,9},{9,8},{10,11... | collective-permute-start | bytes 786440 | tf_op jit(solution)/shard_map/ppermute | solution.py:414
  36.5 5.6 %collective-permute-start.11 = (f32[2,128,256]{2,1,0:T(8,128)S(1)}, f32[2,128,256]{2,1,0:T(8,128)S(1)}, u32[]{:S(2)}, u32[]{:S(2)}) collective-permute-start(f32[2,128,256]{2,1,0:T(8,128)S(1)} %get-tuple-element.49), channel_id=1, source_target_pairs={{0,1},{1,0},{2,3},{3,2},{4,5},{5,4},{6,7},{7,6},{8,9},{9,8},{10,11... | collective-permute-start | bytes 786440 | tf_op jit(solution)/shard_map/ppermute | solution.py:414
  39.0 3.1 %collective-permute-start.12 = (f32[128,256]{1,0:T(8,128)S(1)}, f32[128,256]{1,0:T(8,128)S(1)}, u32[]{:S(2)}, u32[]{:S(2)}) collective-permute-start(f32[128,256]{1,0:T(8,128)S(1)} %get-tuple-element.50), channel_id=1, source_target_pairs={{0,1},{1,0},{2,3},{3,2},{4,5},{5,4},{6,7},{7,6},{8,9},{9,8},{10,11... | collective-permute-start | bytes 393224 | tf_op jit(solution)/shard_map/ppermute | solution.py:414
  41.9 14.1 %collective-permute-start.13 = (f32[128,256]{1,0:T(8,128)S(1)}, f32[128,256]{1,0:T(8,128)S(1)}, u32[]{:S(2)}, u32[]{:S(2)}) collective-permute-start(f32[128,256]{1,0:T(8,128)S(1)} %get-tuple-element.57), channel_id=1, source_target_pairs={{0,1},{1,0},{2,3},{3,2},{4,5},{5,4},{6,7},{7,6},{8,9},{9,8},{10,11... | collective-permute-start | bytes 393224 | tf_op jit(solution)/shard_map/ppermute | solution.py:414

commit v9 on v8

--- a/solution.py
+++ b/solution.py
@@ -453,9 +453,12 @@
         compiler_params=pltpu.CompilerParams(vmem_limit_bytes=52 * 2**20),
     )(wave_start, preconditioner, left_blocks, right_blocks)
     facing_wave = facing(own_wave)
+    mate_left, mate_right = mate(sent_left), mate(sent_right)
+    mate_shifts, own_preconditioner = lax.optimization_barrier(
+        (mate(term_shifts), own_preconditioner)
+    )
     facing_preconditioner = facing(own_preconditioner)
-    mate_left, mate_right = mate(sent_left), mate(sent_right)
-    shifts = (term_shifts, mate(term_shifts))
+    shifts = (term_shifts, mate_shifts)
 
     split_shape = (terms,) + left_blocks.shape[2:]
     blocks = call(

time: 58 us -> 56.2 us (0.969)
  blocking collectives: 13.9 us -> 12.4 us
  starting transfers between devices: 23.8 us -> 23.2 us
    all_to_all x1, blocking collectives: 13.9 us -> 12.4 us  [exchanged(): lax.all_to_all(spread, AXES, 0, 0, tiled=True).reshape(devices, LANES)]
  transfers between devices with their start and end apart: 14 -> 14, of which waited for: 1 -> 1; matrix products, arithmetic and copies ran while one was open for 0% -> 0% of each run, Pallas kernels for 27% -> 28%
where the time goes in v9:
time: 56.2 us; the launch traced here: 56 us
  starting transfers between devices  23.2 us (41%)
  Pallas kernels  18.8 us (33%)
  blocking collectives  12.4 us (22%)
  waiting for transfers between devices  0.85 us (2%)
  between operations  0.85 us (2%)
    ppermute x9, starting transfers between devices, mate(): return lax.ppermute(values, AXES, swap)  19.7 us
    pallas_call x9, Pallas kernels, call(): pl.pallas_call(kernel, out_shape=[jax.ShapeDtypeStruct(shape, kind) for s...  17.2 us
    all_to_all x1, blocking collectives, exchanged(): lax.all_to_all(spread, AXES, 0, 0, tiled=True).reshape(devices, LANES)  12.4 us
    ppermute x5, starting transfers between devices, facing(): return lax.ppermute(values, AXES, across)  3.49 us
    pallas_call x1, Pallas kernels, one_sector_body(): pl.pallas_call(picking_kernel, out_shape=[jax.ShapeDtypeStruct(shape, f32...  1.55 us
  transfers between devices with their start and end apart: 14, of which 1 were waited for; matrix products, arithmetic and copies ran while one was open for 0% of the time, Pallas kernels for 28%

profile of v9, /device:TPU:0, one launch (start us, length us, event | category | flops | bytes accessed | tf_op | source)
XLA Modules:
  0.0 56.0 jit_solution(9380859535036200863)
XLA Ops:
  0.6 1.5 %shard_map.68 = (f32[256,256]{1,0:T(8,128)S(1)}, f32[256,256]{1,0:T(8,128)S(1)}, f32[2,256,256]{2,1,0:T(8,128)S(1)}, f32[2,256,256]{2,1,0:T(8,128)S(1)}) custom-call(f32[2,256,256]{2,1,0:T(8,128)} %wave.3, f32[2,256,256]{2,1,0:T(8,128)} %preconditioner.3, f32[2,2,256,256]{3,2,1,0:T(8,128)} %own_left.1, f32[2,2,256,256]{3,2,1,0:T(8,128)} %own_right.1), custom_call_target="tpu_custom_call" | custom-call | tf_op jit(solution)/shard_map/pallas_call | solution.py:447
  2.2 0.5 collective-permute-start.2
  2.7 0.1 collective-permute-start.3
  2.8 0.7 %collective-permute-start.1 = (f32[256,256]{1,0:T(8,128)S(1)}, f32[256,256]{1,0:T(8,128)S(1)}, u32[]{:S(2)}, u32[]{:S(2)}) collective-permute-start(f32[256,256]{1,0:T(8,128)S(1)} %get-tuple-element.34), channel_id=1, source_target_pairs={{1,2},{3,4},{5,6},{7,8},{9,10},{11,12},{13,14},{15,16},{17,18},{19... | collective-permute-start | bytes 786440 | tf_op jit(solution)/shard_map/ppermute | solution.py:417
  3.5 4.3 %collective-permute-start = (s32[2]{0:T(128)S(1)}, s32[2]{0:T(128)S(1)}, u32[]{:S(2)}, u32[]{:S(2)}) collective-permute-start(s32[2]{0:T(128)S(1)} %copy-done.4), channel_id=1, source_target_pairs={{0,1},{1,0},{2,3},{3,2},{4,5},{5,4},{6,7},{7,6},{8,9},{9,8},{10,11... | collective-permute-start | bytes 32 | tf_op jit(solution)/shard_map/ppermute | solution.py:414
  7.8 0.8 %collective-permute-done.mate_shifts = s32[2]{0:T(128)S(1)} collective-permute-done((s32[2]{0:T(128)S(1)}, s32[2]{0:T(128)S(1)}, u32[]{:S(2)}, u32[]{:S(2)}) %collective-permute-start) | collective-permute-done | bytes 40 | tf_op jit(solution)/shard_map/ppermute | solution.py:414
  8.6 0.8 %collective-permute-start.4 = (f32[256,256]{1,0:T(8,128)S(1)}, f32[256,256]{1,0:T(8,128)S(1)}, u32[]{:S(2)}, u32[]{:S(2)}) collective-permute-start(f32[256,256]{1,0:T(8,128)S(1)} %get-tuple-element.42), channel_id=1, source_target_pairs={{1,2},{3,4},{5,6},{7,8},{9,10},{11,12},{13,14},{15,16},{17,18},{19... | collective-permute-start | bytes 786440 | tf_op jit(solution)/shard_map/ppermute | solution.py:417
  9.5 0.0 collective-permute-done.3.mate_right
  9.5 0.4 shard_map.69
  9.9 0.0 copy-start.3
  9.9 1.8 %shard_map.70 = (f32[256,256]{1,0:T(8,128)S(1)}, f32[3,256,256]{2,1,0:T(8,128)S(1)}) custom-call(s32[2]{0:T(128)S(1)} %copy-done.4, s32[2]{0:T(128)S(1)} %collective-permute-done.mate_shifts, f32[2,256,256]{2,1,0:T(8,128)S(1)} %copy-done.2, f32[256,256]{1,0:T(8,128)S(1)} %collective-permute-done.1.facing_wave, ...), custom_call_target="tpu_custom_call" | custom-call | tf_op jit(solution)/shard_map/pallas_call | solution.py:432
  11.7 0.7 %collective-permute-start.6 = (f32[256,256]{1,0:T(8,128)S(1)}, f32[256,256]{1,0:T(8,128)S(1)}, u32[]{:S(2)}, u32[]{:S(2)}) collective-permute-start(f32[256,256]{1,0:T(8,128)S(1)} %get-tuple-element.44.image.own_image), channel_id=1, source_target_pairs={{1,2},{3,4},{5,6},{7,8},{9,10},{11,12},{13,14},{15,16},{17,18},{19... | collective-permute-start | bytes 786440 | tf_op jit(solution)/shard_map/ppermute | solution.py:417
  12.4 7.7 %collective-permute-start.5 = (f32[256,256]{1,0:T(8,128)S(1)}, f32[256,256]{1,0:T(8,128)S(1)}, u32[]{:S(2)}, u32[]{:S(2)}) collective-permute-start(f32[256,256]{1,0:T(8,128)S(1)} %get-tuple-element.44.image.own_image), channel_id=1, source_target_pairs={{0,1},{1,0},{2,3},{3,2},{4,5},{5,4},{6,7},{7,6},{8,9},{9,8},{10,11... | collective-permute-start | bytes 786440 | tf_op jit(solution)/shard_map/ppermute | solution.py:414
  20.1 1.8 %shard_map.71 = (f32[256,256]{1,0:T(8,128)S(1)}, f32[3,256,256]{2,1,0:T(8,128)S(1)}) custom-call(s32[2]{0:T(128)S(1)} %copy-done.4, s32[2]{0:T(128)S(1)} %collective-permute-done.mate_shifts, f32[3,256,256]{2,1,0:T(8,128)S(1)} %get-tuple-element.41.start, f32[2,256,256]{2,1,0:T(8,128)S(1)} %copy-done.3, ...), custom_call_target="tpu_custom_call" | custom-call | tf_op jit(solution)/shard_map/pallas_call | solution.py:432
  22.0 0.7 %collective-permute-start.10 = (f32[256,256]{1,0:T(8,128)S(1)}, f32[256,256]{1,0:T(8,128)S(1)}, u32[]{:S(2)}, u32[]{:S(2)}) collective-permute-start(f32[256,256]{1,0:T(8,128)S(1)} %get-tuple-element.45.side.own_side), channel_id=1, source_target_pairs={{1,2},{3,4},{5,6},{7,8},{9,10},{11,12},{13,14},{15,16},{17,18},{19... | collective-permute-start | bytes 786440 | tf_op jit(solution)/shard_map/ppermute | solution.py:417
  22.6 3.5 %collective-permute-start.9 = (f32[256,256]{1,0:T(8,128)S(1)}, f32[256,256]{1,0:T(8,128)S(1)}, u32[]{:S(2)}, u32[]{:S(2)}) collective-permute-start(f32[256,256]{1,0:T(8,128)S(1)} %get-tuple-element.45.side.own_side), channel_id=1, source_target_pairs={{0,1},{1,0},{2,3},{3,2},{4,5},{5,4},{6,7},{7,6},{8,9},{9,8},{10,11... | collective-permute-start | bytes 786440 | tf_op jit(solution)/shard_map/ppermute | solution.py:414
  26.1 1.0 %shard_map.72._.early_row = f32[1,128]{1,0:T(1,128)S(1)} custom-call(f32[3,256,256]{2,1,0:T(8,128)S(1)} %get-tuple-element.41.start, f32[256,256]{1,0:T(8,128)S(1)} %get-tuple-element.44.image.own_image, f32[256,256]{1,0:T(8,128)S(1)} %get-tuple-element.45.side.own_side, f32[3,256,256]{2,1,0:T(8,128)S(1)} %get-tuple-element.43.inverse), custom_call_target="tpu_custom_call" | custom-call | tf_op jit(solution)/shard_map/pallas_call | solution.py:432
  27.1 0.0 collective-permute-done.5.mate_image
  27.1 1.8 %shard_map.73 = (f32[256,256]{1,0:T(8,128)S(1)}, f32[3,256,256]{2,1,0:T(8,128)S(1)}) custom-call(s32[2]{0:T(128)S(1)} %copy-done.4, s32[2]{0:T(128)S(1)} %collective-permute-done.mate_shifts, f32[256,256]{1,0:T(8,128)S(1)} %get-tuple-element.44.image.own_image, f32[256,256]{1,0:T(8,128)S(1)} %collective-permute-done.5.mate_image, ...), custom_call_target="tpu_custom_call" | custom-call | tf_op jit(solution)/shard_map/pallas_call | solution.py:432
  28.9 0.7 %collective-permute-start.8 = (f32[256,256]{1,0:T(8,128)S(1)}, f32[256,256]{1,0:T(8,128)S(1)}, u32[]{:S(2)}, u32[]{:S(2)}) collective-permute-start(f32[256,256]{1,0:T(8,128)S(1)} %get-tuple-element.46.second.own_second), channel_id=1, source_target_pairs={{1,2},{3,4},{5,6},{7,8},{9,10},{11,12},{13,14},{15,16},{17,18},{19... | collective-permute-start | bytes 786440 | tf_op jit(solution)/shard_map/ppermute | solution.py:417
  29.6 2.8 %collective-permute-start.7 = (f32[256,256]{1,0:T(8,128)S(1)}, f32[256,256]{1,0:T(8,128)S(1)}, u32[]{:S(2)}, u32[]{:S(2)}) collective-permute-start(f32[256,256]{1,0:T(8,128)S(1)} %get-tuple-element.46.second.own_second), channel_id=1, source_target_pairs={{0,1},{1,0},{2,3},{3,2},{4,5},{5,4},{6,7},{7,6},{8,9},{9,8},{10,11... | collective-permute-start | bytes 786440 | tf_op jit(solution)/shard_map/ppermute | solution.py:414
  32.4 3.9 %shard_map.74 = (f32[2,256,256]{2,1,0:T(8,128)S(1)}, f32[2,128,256]{2,1,0:T(8,128)S(1)}, f32[2,128,256]{2,1,0:T(8,128)S(1)}, f32[1,128]{1,0:T(1,128)S(1)}) custom-call(s32[2]{0:T(128)S(1)} %copy-done.4, s32[2]{0:T(128)S(1)} %collective-permute-done.mate_shifts, f32[3,256,256]{2,1,0:T(8,128)S(1)} %get-tuple-element.41.start, ...), custom_call_target="tpu_custom_call" | custom-call | tf_op jit(solution)/shard_map/pallas_call | solution.py:432
  36.3 0.1 collective-permute-start.11
  36.4 0.0 collective-permute-done.10.facing_side
  36.4 0.0 collective-permute-done.9.mate_side
  36.4 2.4 %shard_map.75 = (f32[256,256]{1,0:T(8,128)S(1)}, f32[128,256]{1,0:T(8,128)S(1)}, f32[128,256]{1,0:T(8,128)S(1)}, f32[1,128]{1,0:T(1,128)S(1)}) custom-call(s32[2]{0:T(128)S(1)} %copy-done.4, s32[2]{0:T(128)S(1)} %collective-permute-done.mate_shifts, f32[3,256,256]{2,1,0:T(8,128)S(1)} %get-tuple-element.41.start, ...), custom_call_target="tpu_custom_call" | custom-call | tf_op jit(solution)/shard_map/pallas_call | solution.py:432
  38.8 0.5 collective-permute-start.12
  39.3 0.0 collective-permute-done.8.facing_second
  39.3 2.4 %shard_map.76 = (f32[128,256]{1,0:T(8,128)S(1)}, f32[128,256]{1,0:T(8,128)S(1)}, f32[32,128]{1,0:T(8,128)S(1)}) custom-call(s32[2]{0:T(128)S(1)} %copy-done.4, s32[2]{0:T(128)S(1)} %collective-permute-done.mate_shifts, f32[3,256,256]{2,1,0:T(8,128)S(1)} %get-tuple-element.41.start, f32[3,256,256]{2,1,0:T(8,128)S(1)} %get-tuple-element.43.inverse, ...), custom_call_target="tpu_custom_call" | custom-call | tf_op jit(solution)/shard_map/pallas_call | solution.py:432
  41.7 0.1 collective-permute-start.13
  41.8 12.4 %all_to_all.5 = f32[32,1,128]{2,1,0:T(1,128)S(1)} all-to-all(f32[32,1,128]{2,1,0:T(1,128)S(1)} %bitcast.5), channel_id=1, replica_groups=mesh['sector'=16,'op'=2] {'sector','op'}, dimensions={0} | all-to-all | bytes 32768 | tf_op jit(solution)/shard_map/all_to_all | solution.py:424
  54.2 1.8 %shard_map.77 = (f32[3,2,128,256]{3,2,1,0:T(8,128)}, f32[3]{0:T(128)}) custom-call(f32[32,128]{1,0:T(8,128)S(1)} %bitcast.4, f32[3,256,256]{2,1,0:T(8,128)S(1)} %get-tuple-element.41.start, f32[3,256,256]{2,1,0:T(8,128)S(1)} %get-tuple-element.47.ratio, f32[3,256,256]{2,1,0:T(8,128)S(1)} %get-tuple-element.43.inverse, ...), custom_call_target="tpu_custom_call" | custom-call | tf_op jit(solution)/shard_map/pallas_call | solution.py:432
  (17 shorter events, 0.0 us)
Async XLA Ops:
  0.6 8.8 %copy-start.1 = (f32[2,2,256,256]{3,2,1,0:T(8,128)S(1)}, f32[2,2,256,256]{3,2,1,0:T(8,128)}, u32[]{:S(2)}) copy-start(f32[2,2,256,256]{3,2,1,0:T(8,128)} %own_right.1) | copy-start | bytes 3145732
  0.6 8.8 %copy-start = (f32[2,2,256,256]{3,2,1,0:T(8,128)S(1)}, f32[2,2,256,256]{3,2,1,0:T(8,128)}, u32[]{:S(2)}) copy-start(f32[2,2,256,256]{3,2,1,0:T(8,128)} %own_left.1) | copy-start | bytes 3145732
  2.2 7.2 %collective-permute-start.2 = (f32[2,256,256]{2,1,0:T(8,128)S(1)}, f32[2,256,256]{2,1,0:T(8,128)S(1)}, u32[]{:S(2)}, u32[]{:S(2)}) collective-permute-start(f32[2,256,256]{2,1,0:T(8,128)S(1)} %get-tuple-element.35), channel_id=1, source_target_pairs={{0,1},{1,0},{2,3},{3,2},{4,5},{5,4},{6,7},{7,6},{8,9},{9,8},{10,11... | collective-permute-start | bytes 1572872 | tf_op jit(solution)/shard_map/ppermute | solution.py:414
  2.7 0.8 %copy-start.4 = (s32[2]{0:T(128)S(1)}, s32[2]{0:T(128)}, u32[]{:S(2)}) copy-start(s32[2]{0:T(128)} %own_shifts.11) | copy-start | bytes 28
  2.7 6.7 %collective-permute-start.3 = (f32[2,256,256]{2,1,0:T(8,128)S(1)}, f32[2,256,256]{2,1,0:T(8,128)S(1)}, u32[]{:S(2)}, u32[]{:S(2)}) collective-permute-start(f32[2,256,256]{2,1,0:T(8,128)S(1)} %get-tuple-element.36), channel_id=1, source_target_pairs={{0,1},{1,0},{2,3},{3,2},{4,5},{5,4},{6,7},{7,6},{8,9},{9,8},{10,11... | collective-permute-start | bytes 1572872 | tf_op jit(solution)/shard_map/ppermute | solution.py:414
  2.8 7.1 %collective-permute-start.1 = (f32[256,256]{1,0:T(8,128)S(1)}, f32[256,256]{1,0:T(8,128)S(1)}, u32[]{:S(2)}, u32[]{:S(2)}) collective-permute-start(f32[256,256]{1,0:T(8,128)S(1)} %get-tuple-element.34), channel_id=1, source_target_pairs={{1,2},{3,4},{5,6},{7,8},{9,10},{11,12},{13,14},{15,16},{17,18},{19... | collective-permute-start | bytes 786440 | tf_op jit(solution)/shard_map/ppermute | solution.py:417
  3.5 5.1 %collective-permute-start = (s32[2]{0:T(128)S(1)}, s32[2]{0:T(128)S(1)}, u32[]{:S(2)}, u32[]{:S(2)}) collective-permute-start(s32[2]{0:T(128)S(1)} %copy-done.4), channel_id=1, source_target_pairs={{0,1},{1,0},{2,3},{3,2},{4,5},{5,4},{6,7},{7,6},{8,9},{9,8},{10,11... | collective-permute-start | bytes 32 | tf_op jit(solution)/shard_map/ppermute | solution.py:414
  8.6 1.3 %copy-start.2 = (f32[2,256,256]{2,1,0:T(8,128)S(1)}, f32[2,256,256]{2,1,0:T(8,128)}, u32[]{:S(2)}) copy-start(f32[2,256,256]{2,1,0:T(8,128)} %wave.3) | copy-start | bytes 1572868
  8.6 11.5 %collective-permute-start.4 = (f32[256,256]{1,0:T(8,128)S(1)}, f32[256,256]{1,0:T(8,128)S(1)}, u32[]{:S(2)}, u32[]{:S(2)}) collective-permute-start(f32[256,256]{1,0:T(8,128)S(1)} %get-tuple-element.42), channel_id=1, source_target_pairs={{1,2},{3,4},{5,6},{7,8},{9,10},{11,12},{13,14},{15,16},{17,18},{19... | collective-permute-start | bytes 786440 | tf_op jit(solution)/shard_map/ppermute | solution.py:417
  9.9 10.2 %copy-start.3 = (f32[2,256,256]{2,1,0:T(8,128)S(1)}, f32[2,256,256]{2,1,0:T(8,128)}, u32[]{:S(2)}) copy-start(f32[2,256,256]{2,1,0:T(8,128)} %preconditioner.3) | copy-start | bytes 1572868
  11.7 15.4 %collective-permute-start.6 = (f32[256,256]{1,0:T(8,128)S(1)}, f32[256,256]{1,0:T(8,128)S(1)}, u32[]{:S(2)}, u32[]{:S(2)}) collective-permute-start(f32[256,256]{1,0:T(8,128)S(1)} %get-tuple-element.44.image.own_image), channel_id=1, source_target_pairs={{1,2},{3,4},{5,6},{7,8},{9,10},{11,12},{13,14},{15,16},{17,18},{19... | collective-permute-start | bytes 786440 | tf_op jit(solution)/shard_map/ppermute | solution.py:417
  12.4 14.7 %collective-permute-start.5 = (f32[256,256]{1,0:T(8,128)S(1)}, f32[256,256]{1,0:T(8,128)S(1)}, u32[]{:S(2)}, u32[]{:S(2)}) collective-permute-start(f32[256,256]{1,0:T(8,128)S(1)} %get-tuple-element.44.image.own_image), channel_id=1, source_target_pairs={{0,1},{1,0},{2,3},{3,2},{4,5},{5,4},{6,7},{7,6},{8,9},{9,8},{10,11... | collective-permute-start | bytes 786440 | tf_op jit(solution)/shard_map/ppermute | solution.py:414
  22.0 14.4 %collective-permute-start.10 = (f32[256,256]{1,0:T(8,128)S(1)}, f32[256,256]{1,0:T(8,128)S(1)}, u32[]{:S(2)}, u32[]{:S(2)}) collective-permute-start(f32[256,256]{1,0:T(8,128)S(1)} %get-tuple-element.45.side.own_side), channel_id=1, source_target_pairs={{1,2},{3,4},{5,6},{7,8},{9,10},{11,12},{13,14},{15,16},{17,18},{19... | collective-permute-start | bytes 786440 | tf_op jit(solution)/shard_map/ppermute | solution.py:417
  22.6 13.8 %collective-permute-start.9 = (f32[256,256]{1,0:T(8,128)S(1)}, f32[256,256]{1,0:T(8,128)S(1)}, u32[]{:S(2)}, u32[]{:S(2)}) collective-permute-start(f32[256,256]{1,0:T(8,128)S(1)} %get-tuple-element.45.side.own_side), channel_id=1, source_target_pairs={{0,1},{1,0},{2,3},{3,2},{4,5},{5,4},{6,7},{7,6},{8,9},{9,8},{10,11... | collective-permute-start | bytes 786440 | tf_op jit(solution)/shard_map/ppermute | solution.py:414
  28.9 10.4 %collective-permute-start.8 = (f32[256,256]{1,0:T(8,128)S(1)}, f32[256,256]{1,0:T(8,128)S(1)}, u32[]{:S(2)}, u32[]{:S(2)}) collective-permute-start(f32[256,256]{1,0:T(8,128)S(1)} %get-tuple-element.46.second.own_second), channel_id=1, source_target_pairs={{1,2},{3,4},{5,6},{7,8},{9,10},{11,12},{13,14},{15,16},{17,18},{19... | collective-permute-start | bytes 786440 | tf_op jit(solution)/shard_map/ppermute | solution.py:417
  29.6 9.7 %collective-permute-start.7 = (f32[256,256]{1,0:T(8,128)S(1)}, f32[256,256]{1,0:T(8,128)S(1)}, u32[]{:S(2)}, u32[]{:S(2)}) collective-permute-start(f32[256,256]{1,0:T(8,128)S(1)} %get-tuple-element.46.second.own_second), channel_id=1, source_target_pairs={{0,1},{1,0},{2,3},{3,2},{4,5},{5,4},{6,7},{7,6},{8,9},{9,8},{10,11... | collective-permute-start | bytes 786440 | tf_op jit(solution)/shard_map/ppermute | solution.py:414
  36.3 5.5 %collective-permute-start.11 = (f32[2,128,256]{2,1,0:T(8,128)S(1)}, f32[2,128,256]{2,1,0:T(8,128)S(1)}, u32[]{:S(2)}, u32[]{:S(2)}) collective-permute-start(f32[2,128,256]{2,1,0:T(8,128)S(1)} %get-tuple-element.53), channel_id=1, source_target_pairs={{0,1},{1,0},{2,3},{3,2},{4,5},{5,4},{6,7},{7,6},{8,9},{9,8},{10,11... | collective-permute-start | bytes 786440 | tf_op jit(solution)/shard_map/ppermute | solution.py:414
  38.8 3.0 %collective-permute-start.12 = (f32[128,256]{1,0:T(8,128)S(1)}, f32[128,256]{1,0:T(8,128)S(1)}, u32[]{:S(2)}, u32[]{:S(2)}) collective-permute-start(f32[128,256]{1,0:T(8,128)S(1)} %get-tuple-element.54), channel_id=1, source_target_pairs={{0,1},{1,0},{2,3},{3,2},{4,5},{5,4},{6,7},{7,6},{8,9},{9,8},{10,11... | collective-permute-start | bytes 393224 | tf_op jit(solution)/shard_map/ppermute | solution.py:414
  41.7 12.5 %collective-permute-start.13 = (f32[128,256]{1,0:T(8,128)S(1)}, f32[128,256]{1,0:T(8,128)S(1)}, u32[]{:S(2)}, u32[]{:S(2)}) collective-permute-start(f32[128,256]{1,0:T(8,128)S(1)} %get-tuple-element.61), channel_id=1, source_target_pairs={{0,1},{1,0},{2,3},{3,2},{4,5},{5,4},{6,7},{7,6},{8,9},{9,8},{10,11... | collective-permute-start | bytes 393224 | tf_op jit(solution)/shard_map/ppermute | solution.py:414

commit v10 on v9

--- a/solution.py
+++ b/solution.py
@@ -89,7 +89,7 @@
     ]
 
 
-CHUNK = 32
+CHUNK = 16
 
 
 def row_of_sums(moments, refs, inverse, first=0, row=None):
@@ -358,8 +358,10 @@
     for place, second in enumerate((own_second, mate_second, facing_second)):
         high[place], low[place] = split(second[...] * inverse[place])
     last = apply_terms(sources, (high, low), (left_high, left_low), (right_high, right_low))
-    halves(last, kept_ref, sent_ref)
     last_ref[...] = last
+    op, half = lax.axis_index("op"), kept_ref.shape[0]
+    kept_ref[...] = last_ref[pl.ds(pl.multiple_of(op * half, half), half)]
+    sent_ref[...] = last_ref[pl.ds(pl.multiple_of((1 - op) * half, half), half)]
     refs = {"w": start.at[0], "u": image, "a": side, "b": own_second}
     refs.update(c=extra.at[0], d=extra.at[1], e=further, f=last_ref)
     row = row_of_sums(MOMENTS[3], refs, inverse.at[0], FIRST_LANE[3], early_row[...])
@@ -484,10 +486,11 @@
         [(block, f32), ((3,) + block, f32)],
         scalars=2,
     )
-    sides = around(side)
     (early_row,) = call(
         moments_kernel, (start, image, side, inverse), [((1, LANES), f32)], scratch=False
     )
+    side, early_row = lax.optimization_barrier((side, early_row))
+    sides = around(side)
     second, ratio = call(
         second_kernel,
         (*shifts, *images, inverse, early_row, *blocks),

time: 56.2 us -> 56.3 us (level)
  no operation moved by 1% of the time
where the time goes in v10:
time: 56.3 us; the launch traced here: 56 us
  starting transfers between devices  23.1 us (41%)
  Pallas kernels  18.9 us (34%)
  blocking collectives  12.3 us (22%)
  waiting for transfers between devices  0.85 us (2%)
  between operations  0.85 us (2%)
    ppermute x9, starting transfers between devices, mate(): return lax.ppermute(values, AXES, swap)  19.6 us
    pallas_call x9, Pallas kernels, call(): pl.pallas_call(kernel, out_shape=[jax.ShapeDtypeStruct(shape, kind) for s...  17.3 us
    all_to_all x1, blocking collectives, exchanged(): lax.all_to_all(spread, AXES, 0, 0, tiled=True).reshape(devices, LANES)  12.3 us
    ppermute x5, starting transfers between devices, facing(): return lax.ppermute(values, AXES, across)  3.49 us
    pallas_call x1, Pallas kernels, one_sector_body(): pl.pallas_call(picking_kernel, out_shape=[jax.ShapeDtypeStruct(shape, f32...  1.55 us
  transfers between devices with their start and end apart: 14, of which 1 were waited for; matrix products, arithmetic and copies ran while one was open for 0% of the time, Pallas kernels for 28%

profile of v10, /device:TPU:0, one launch (start us, length us, event | category | flops | bytes accessed | tf_op | source)
XLA Modules:
  0.0 56.0 jit_solution(7537899916030805750)
XLA Ops:
  0.6 1.5 %shard_map.68 = (f32[256,256]{1,0:T(8,128)S(1)}, f32[256,256]{1,0:T(8,128)S(1)}, f32[2,256,256]{2,1,0:T(8,128)S(1)}, f32[2,256,256]{2,1,0:T(8,128)S(1)}) custom-call(f32[2,256,256]{2,1,0:T(8,128)} %wave.3, f32[2,256,256]{2,1,0:T(8,128)} %preconditioner.3, f32[2,2,256,256]{3,2,1,0:T(8,128)} %own_left.1, f32[2,2,256,256]{3,2,1,0:T(8,128)} %own_right.1), custom_call_target="tpu_custom_call" | custom-call | tf_op jit(solution)/shard_map/pallas_call | solution.py:449
  2.2 0.5 collective-permute-start.2
  2.7 0.1 collective-permute-start.3
  2.8 0.7 %collective-permute-start.1 = (f32[256,256]{1,0:T(8,128)S(1)}, f32[256,256]{1,0:T(8,128)S(1)}, u32[]{:S(2)}, u32[]{:S(2)}) collective-permute-start(f32[256,256]{1,0:T(8,128)S(1)} %get-tuple-element.36), channel_id=1, source_target_pairs={{1,2},{3,4},{5,6},{7,8},{9,10},{11,12},{13,14},{15,16},{17,18},{19... | collective-permute-start | bytes 786440 | tf_op jit(solution)/shard_map/ppermute | solution.py:419
  3.5 4.3 %collective-permute-start = (s32[2]{0:T(128)S(1)}, s32[2]{0:T(128)S(1)}, u32[]{:S(2)}, u32[]{:S(2)}) collective-permute-start(s32[2]{0:T(128)S(1)} %copy-done.4), channel_id=1, source_target_pairs={{0,1},{1,0},{2,3},{3,2},{4,5},{5,4},{6,7},{7,6},{8,9},{9,8},{10,11... | collective-permute-start | bytes 32 | tf_op jit(solution)/shard_map/ppermute | solution.py:416
  7.8 0.8 %collective-permute-done.mate_shifts = s32[2]{0:T(128)S(1)} collective-permute-done((s32[2]{0:T(128)S(1)}, s32[2]{0:T(128)S(1)}, u32[]{:S(2)}, u32[]{:S(2)}) %collective-permute-start) | collective-permute-done | bytes 40 | tf_op jit(solution)/shard_map/ppermute | solution.py:416
  8.6 0.8 %collective-permute-start.4 = (f32[256,256]{1,0:T(8,128)S(1)}, f32[256,256]{1,0:T(8,128)S(1)}, u32[]{:S(2)}, u32[]{:S(2)}) collective-permute-start(f32[256,256]{1,0:T(8,128)S(1)} %get-tuple-element.44), channel_id=1, source_target_pairs={{1,2},{3,4},{5,6},{7,8},{9,10},{11,12},{13,14},{15,16},{17,18},{19... | collective-permute-start | bytes 786440 | tf_op jit(solution)/shard_map/ppermute | solution.py:419
  9.5 0.0 collective-permute-done.3.mate_right
  9.5 0.4 shard_map.69
  9.9 0.0 copy-start.3
  9.9 1.8 %shard_map.70 = (f32[256,256]{1,0:T(8,128)S(1)}, f32[3,256,256]{2,1,0:T(8,128)S(1)}) custom-call(s32[2]{0:T(128)S(1)} %copy-done.4, s32[2]{0:T(128)S(1)} %collective-permute-done.mate_shifts, f32[2,256,256]{2,1,0:T(8,128)S(1)} %copy-done.2, f32[256,256]{1,0:T(8,128)S(1)} %collective-permute-done.1.facing_wave, ...), custom_call_target="tpu_custom_call" | custom-call | tf_op jit(solution)/shard_map/pallas_call | solution.py:434
  11.7 0.7 %collective-permute-start.6 = (f32[256,256]{1,0:T(8,128)S(1)}, f32[256,256]{1,0:T(8,128)S(1)}, u32[]{:S(2)}, u32[]{:S(2)}) collective-permute-start(f32[256,256]{1,0:T(8,128)S(1)} %get-tuple-element.46.image.own_image), channel_id=1, source_target_pairs={{1,2},{3,4},{5,6},{7,8},{9,10},{11,12},{13,14},{15,16},{17,18},{19... | collective-permute-start | bytes 786440 | tf_op jit(solution)/shard_map/ppermute | solution.py:419
  12.4 7.7 %collective-permute-start.5 = (f32[256,256]{1,0:T(8,128)S(1)}, f32[256,256]{1,0:T(8,128)S(1)}, u32[]{:S(2)}, u32[]{:S(2)}) collective-permute-start(f32[256,256]{1,0:T(8,128)S(1)} %get-tuple-element.46.image.own_image), channel_id=1, source_target_pairs={{0,1},{1,0},{2,3},{3,2},{4,5},{5,4},{6,7},{7,6},{8,9},{9,8},{10,11... | collective-permute-start | bytes 786440 | tf_op jit(solution)/shard_map/ppermute | solution.py:416
  20.1 1.8 %shard_map.71 = (f32[256,256]{1,0:T(8,128)S(1)}, f32[3,256,256]{2,1,0:T(8,128)S(1)}) custom-call(s32[2]{0:T(128)S(1)} %copy-done.4, s32[2]{0:T(128)S(1)} %collective-permute-done.mate_shifts, f32[3,256,256]{2,1,0:T(8,128)S(1)} %get-tuple-element.43.start, f32[2,256,256]{2,1,0:T(8,128)S(1)} %copy-done.3, ...), custom_call_target="tpu_custom_call" | custom-call | tf_op jit(solution)/shard_map/pallas_call | solution.py:434
  22.0 1.0 %shard_map.72._.early_row = f32[1,128]{1,0:T(1,128)S(1)} custom-call(f32[3,256,256]{2,1,0:T(8,128)S(1)} %get-tuple-element.43.start, f32[256,256]{1,0:T(8,128)S(1)} %get-tuple-element.46.image.own_image, f32[256,256]{1,0:T(8,128)S(1)} %get-tuple-element.48.side.own_side, f32[3,256,256]{2,1,0:T(8,128)S(1)} %get-tuple-element.45.inverse), custom_call_target="tpu_custom_call" | custom-call | tf_op jit(solution)/shard_map/pallas_call | solution.py:434
  23.0 0.7 %collective-permute-start.10 = (f32[256,256]{1,0:T(8,128)S(1)}, f32[256,256]{1,0:T(8,128)S(1)}, u32[]{:S(2)}, u32[]{:S(2)}) collective-permute-start(f32[256,256]{1,0:T(8,128)S(1)} %get-tuple-element.48.side.own_side), channel_id=1, source_target_pairs={{1,2},{3,4},{5,6},{7,8},{9,10},{11,12},{13,14},{15,16},{17,18},{19... | collective-permute-start | bytes 786440 | tf_op jit(solution)/shard_map/ppermute | solution.py:419
  23.7 3.5 %collective-permute-start.9 = (f32[256,256]{1,0:T(8,128)S(1)}, f32[256,256]{1,0:T(8,128)S(1)}, u32[]{:S(2)}, u32[]{:S(2)}) collective-permute-start(f32[256,256]{1,0:T(8,128)S(1)} %get-tuple-element.48.side.own_side), channel_id=1, source_target_pairs={{0,1},{1,0},{2,3},{3,2},{4,5},{5,4},{6,7},{7,6},{8,9},{9,8},{10,11... | collective-permute-start | bytes 786440 | tf_op jit(solution)/shard_map/ppermute | solution.py:416
  27.1 1.8 %shard_map.73 = (f32[256,256]{1,0:T(8,128)S(1)}, f32[3,256,256]{2,1,0:T(8,128)S(1)}) custom-call(s32[2]{0:T(128)S(1)} %copy-done.4, s32[2]{0:T(128)S(1)} %collective-permute-done.mate_shifts, f32[256,256]{1,0:T(8,128)S(1)} %get-tuple-element.46.image.own_image, f32[256,256]{1,0:T(8,128)S(1)} %collective-permute-done.5.mate_image, ...), custom_call_target="tpu_custom_call" | custom-call | tf_op jit(solution)/shard_map/pallas_call | solution.py:434
  29.0 0.7 %collective-permute-start.8 = (f32[256,256]{1,0:T(8,128)S(1)}, f32[256,256]{1,0:T(8,128)S(1)}, u32[]{:S(2)}, u32[]{:S(2)}) collective-permute-start(f32[256,256]{1,0:T(8,128)S(1)} %get-tuple-element.50.second.own_second), channel_id=1, source_target_pairs={{1,2},{3,4},{5,6},{7,8},{9,10},{11,12},{13,14},{15,16},{17,18},{19... | collective-permute-start | bytes 786440 | tf_op jit(solution)/shard_map/ppermute | solution.py:419
  29.7 2.8 %collective-permute-start.7 = (f32[256,256]{1,0:T(8,128)S(1)}, f32[256,256]{1,0:T(8,128)S(1)}, u32[]{:S(2)}, u32[]{:S(2)}) collective-permute-start(f32[256,256]{1,0:T(8,128)S(1)} %get-tuple-element.50.second.own_second), channel_id=1, source_target_pairs={{0,1},{1,0},{2,3},{3,2},{4,5},{5,4},{6,7},{7,6},{8,9},{9,8},{10,11... | collective-permute-start | bytes 786440 | tf_op jit(solution)/shard_map/ppermute | solution.py:416
  32.5 3.9 %shard_map.74 = (f32[2,256,256]{2,1,0:T(8,128)S(1)}, f32[2,128,256]{2,1,0:T(8,128)S(1)}, f32[2,128,256]{2,1,0:T(8,128)S(1)}, f32[1,128]{1,0:T(1,128)S(1)}) custom-call(s32[2]{0:T(128)S(1)} %copy-done.4, s32[2]{0:T(128)S(1)} %collective-permute-done.mate_shifts, f32[3,256,256]{2,1,0:T(8,128)S(1)} %get-tuple-element.43.start, ...), custom_call_target="tpu_custom_call" | custom-call | tf_op jit(solution)/shard_map/pallas_call | solution.py:434
  36.3 0.1 collective-permute-start.11
  36.4 0.0 collective-permute-done.9.mate_side
  36.4 2.4 %shard_map.75 = (f32[256,256]{1,0:T(8,128)S(1)}, f32[128,256]{1,0:T(8,128)S(1)}, f32[128,256]{1,0:T(8,128)S(1)}, f32[1,128]{1,0:T(1,128)S(1)}) custom-call(s32[2]{0:T(128)S(1)} %copy-done.4, s32[2]{0:T(128)S(1)} %collective-permute-done.mate_shifts, f32[3,256,256]{2,1,0:T(8,128)S(1)} %get-tuple-element.43.start, ...), custom_call_target="tpu_custom_call" | custom-call | tf_op jit(solution)/shard_map/pallas_call | solution.py:434
  38.8 0.5 collective-permute-start.12
  39.4 0.0 collective-permute-done.8.facing_second
  39.4 0.0 collective-permute-done.7.mate_second
  39.4 2.4 %shard_map.76 = (f32[128,256]{1,0:T(8,128)S(1)}, f32[128,256]{1,0:T(8,128)S(1)}, f32[32,128]{1,0:T(8,128)S(1)}) custom-call(s32[2]{0:T(128)S(1)} %copy-done.4, s32[2]{0:T(128)S(1)} %collective-permute-done.mate_shifts, f32[3,256,256]{2,1,0:T(8,128)S(1)} %get-tuple-element.43.start, f32[3,256,256]{2,1,0:T(8,128)S(1)} %get-tuple-element.45.inverse, ...), custom_call_target="tpu_custom_call" | custom-call | tf_op jit(solution)/shard_map/pallas_call | solution.py:434
  41.8 0.1 collective-permute-start.13
  41.9 12.3 %all_to_all.5 = f32[32,1,128]{2,1,0:T(1,128)S(1)} all-to-all(f32[32,1,128]{2,1,0:T(1,128)S(1)} %bitcast.5), channel_id=1, replica_groups=mesh['sector'=16,'op'=2] {'sector','op'}, dimensions={0} | all-to-all | bytes 32768 | tf_op jit(solution)/shard_map/all_to_all | solution.py:426
  54.2 0.0 collective-permute-done.13.mate_last
  54.2 1.8 %shard_map.77 = (f32[3,2,128,256]{3,2,1,0:T(8,128)}, f32[3]{0:T(128)}) custom-call(f32[32,128]{1,0:T(8,128)S(1)} %bitcast.4, f32[3,256,256]{2,1,0:T(8,128)S(1)} %get-tuple-element.43.start, f32[3,256,256]{2,1,0:T(8,128)S(1)} %get-tuple-element.51.ratio, f32[3,256,256]{2,1,0:T(8,128)S(1)} %get-tuple-element.45.inverse, ...), custom_call_target="tpu_custom_call" | custom-call | tf_op jit(solution)/shard_map/pallas_call | solution.py:434
  (17 shorter events, 0.0 us)
Async XLA Ops:
  0.6 8.8 %copy-start.1 = (f32[2,2,256,256]{3,2,1,0:T(8,128)S(1)}, f32[2,2,256,256]{3,2,1,0:T(8,128)}, u32[]{:S(2)}) copy-start(f32[2,2,256,256]{3,2,1,0:T(8,128)} %own_right.1) | copy-start | bytes 3145732
  0.6 8.8 %copy-start = (f32[2,2,256,256]{3,2,1,0:T(8,128)S(1)}, f32[2,2,256,256]{3,2,1,0:T(8,128)}, u32[]{:S(2)}) copy-start(f32[2,2,256,256]{3,2,1,0:T(8,128)} %own_left.1) | copy-start | bytes 3145732
  2.2 7.2 %collective-permute-start.2 = (f32[2,256,256]{2,1,0:T(8,128)S(1)}, f32[2,256,256]{2,1,0:T(8,128)S(1)}, u32[]{:S(2)}, u32[]{:S(2)}) collective-permute-start(f32[2,256,256]{2,1,0:T(8,128)S(1)} %get-tuple-element.37), channel_id=1, source_target_pairs={{0,1},{1,0},{2,3},{3,2},{4,5},{5,4},{6,7},{7,6},{8,9},{9,8},{10,11... | collective-permute-start | bytes 1572872 | tf_op jit(solution)/shard_map/ppermute | solution.py:416
  2.7 0.8 %copy-start.4 = (s32[2]{0:T(128)S(1)}, s32[2]{0:T(128)}, u32[]{:S(2)}) copy-start(s32[2]{0:T(128)} %own_shifts.11) | copy-start | bytes 28
  2.7 6.7 %collective-permute-start.3 = (f32[2,256,256]{2,1,0:T(8,128)S(1)}, f32[2,256,256]{2,1,0:T(8,128)S(1)}, u32[]{:S(2)}, u32[]{:S(2)}) collective-permute-start(f32[2,256,256]{2,1,0:T(8,128)S(1)} %get-tuple-element.38), channel_id=1, source_target_pairs={{0,1},{1,0},{2,3},{3,2},{4,5},{5,4},{6,7},{7,6},{8,9},{9,8},{10,11... | collective-permute-start | bytes 1572872 | tf_op jit(solution)/shard_map/ppermute | solution.py:416
  2.8 7.1 %collective-permute-start.1 = (f32[256,256]{1,0:T(8,128)S(1)}, f32[256,256]{1,0:T(8,128)S(1)}, u32[]{:S(2)}, u32[]{:S(2)}) collective-permute-start(f32[256,256]{1,0:T(8,128)S(1)} %get-tuple-element.36), channel_id=1, source_target_pairs={{1,2},{3,4},{5,6},{7,8},{9,10},{11,12},{13,14},{15,16},{17,18},{19... | collective-permute-start | bytes 786440 | tf_op jit(solution)/shard_map/ppermute | solution.py:419
  3.5 5.1 %collective-permute-start = (s32[2]{0:T(128)S(1)}, s32[2]{0:T(128)S(1)}, u32[]{:S(2)}, u32[]{:S(2)}) collective-permute-start(s32[2]{0:T(128)S(1)} %copy-done.4), channel_id=1, source_target_pairs={{0,1},{1,0},{2,3},{3,2},{4,5},{5,4},{6,7},{7,6},{8,9},{9,8},{10,11... | collective-permute-start | bytes 32 | tf_op jit(solution)/shard_map/ppermute | solution.py:416
  8.6 1.3 %copy-start.2 = (f32[2,256,256]{2,1,0:T(8,128)S(1)}, f32[2,256,256]{2,1,0:T(8,128)}, u32[]{:S(2)}) copy-start(f32[2,256,256]{2,1,0:T(8,128)} %wave.3) | copy-start | bytes 1572868
  8.6 11.5 %collective-permute-start.4 = (f32[256,256]{1,0:T(8,128)S(1)}, f32[256,256]{1,0:T(8,128)S(1)}, u32[]{:S(2)}, u32[]{:S(2)}) collective-permute-start(f32[256,256]{1,0:T(8,128)S(1)} %get-tuple-element.44), channel_id=1, source_target_pairs={{1,2},{3,4},{5,6},{7,8},{9,10},{11,12},{13,14},{15,16},{17,18},{19... | collective-permute-start | bytes 786440 | tf_op jit(solution)/shard_map/ppermute | solution.py:419
  9.9 10.2 %copy-start.3 = (f32[2,256,256]{2,1,0:T(8,128)S(1)}, f32[2,256,256]{2,1,0:T(8,128)}, u32[]{:S(2)}) copy-start(f32[2,256,256]{2,1,0:T(8,128)} %preconditioner.3) | copy-start | bytes 1572868
  11.7 15.4 %collective-permute-start.6 = (f32[256,256]{1,0:T(8,128)S(1)}, f32[256,256]{1,0:T(8,128)S(1)}, u32[]{:S(2)}, u32[]{:S(2)}) collective-permute-start(f32[256,256]{1,0:T(8,128)S(1)} %get-tuple-element.46.image.own_image), channel_id=1, source_target_pairs={{1,2},{3,4},{5,6},{7,8},{9,10},{11,12},{13,14},{15,16},{17,18},{19... | collective-permute-start | bytes 786440 | tf_op jit(solution)/shard_map/ppermute | solution.py:419
  12.4 14.7 %collective-permute-start.5 = (f32[256,256]{1,0:T(8,128)S(1)}, f32[256,256]{1,0:T(8,128)S(1)}, u32[]{:S(2)}, u32[]{:S(2)}) collective-permute-start(f32[256,256]{1,0:T(8,128)S(1)} %get-tuple-element.46.image.own_image), channel_id=1, source_target_pairs={{0,1},{1,0},{2,3},{3,2},{4,5},{5,4},{6,7},{7,6},{8,9},{9,8},{10,11... | collective-permute-start | bytes 786440 | tf_op jit(solution)/shard_map/ppermute | solution.py:416
  23.0 13.4 %collective-permute-start.10 = (f32[256,256]{1,0:T(8,128)S(1)}, f32[256,256]{1,0:T(8,128)S(1)}, u32[]{:S(2)}, u32[]{:S(2)}) collective-permute-start(f32[256,256]{1,0:T(8,128)S(1)} %get-tuple-element.48.side.own_side), channel_id=1, source_target_pairs={{1,2},{3,4},{5,6},{7,8},{9,10},{11,12},{13,14},{15,16},{17,18},{19... | collective-permute-start | bytes 786440 | tf_op jit(solution)/shard_map/ppermute | solution.py:419
  23.7 12.8 %collective-permute-start.9 = (f32[256,256]{1,0:T(8,128)S(1)}, f32[256,256]{1,0:T(8,128)S(1)}, u32[]{:S(2)}, u32[]{:S(2)}) collective-permute-start(f32[256,256]{1,0:T(8,128)S(1)} %get-tuple-element.48.side.own_side), channel_id=1, source_target_pairs={{0,1},{1,0},{2,3},{3,2},{4,5},{5,4},{6,7},{7,6},{8,9},{9,8},{10,11... | collective-permute-start | bytes 786440 | tf_op jit(solution)/shard_map/ppermute | solution.py:416
  29.0 10.4 %collective-permute-start.8 = (f32[256,256]{1,0:T(8,128)S(1)}, f32[256,256]{1,0:T(8,128)S(1)}, u32[]{:S(2)}, u32[]{:S(2)}) collective-permute-start(f32[256,256]{1,0:T(8,128)S(1)} %get-tuple-element.50.second.own_second), channel_id=1, source_target_pairs={{1,2},{3,4},{5,6},{7,8},{9,10},{11,12},{13,14},{15,16},{17,18},{19... | collective-permute-start | bytes 786440 | tf_op jit(solution)/shard_map/ppermute | solution.py:419
  29.7 9.7 %collective-permute-start.7 = (f32[256,256]{1,0:T(8,128)S(1)}, f32[256,256]{1,0:T(8,128)S(1)}, u32[]{:S(2)}, u32[]{:S(2)}) collective-permute-start(f32[256,256]{1,0:T(8,128)S(1)} %get-tuple-element.50.second.own_second), channel_id=1, source_target_pairs={{0,1},{1,0},{2,3},{3,2},{4,5},{5,4},{6,7},{7,6},{8,9},{9,8},{10,11... | collective-permute-start | bytes 786440 | tf_op jit(solution)/shard_map/ppermute | solution.py:416
  36.3 5.6 %collective-permute-start.11 = (f32[2,128,256]{2,1,0:T(8,128)S(1)}, f32[2,128,256]{2,1,0:T(8,128)S(1)}, u32[]{:S(2)}, u32[]{:S(2)}) collective-permute-start(f32[2,128,256]{2,1,0:T(8,128)S(1)} %get-tuple-element.57), channel_id=1, source_target_pairs={{0,1},{1,0},{2,3},{3,2},{4,5},{5,4},{6,7},{7,6},{8,9},{9,8},{10,11... | collective-permute-start | bytes 786440 | tf_op jit(solution)/shard_map/ppermute | solution.py:416
  38.8 3.1 %collective-permute-start.12 = (f32[128,256]{1,0:T(8,128)S(1)}, f32[128,256]{1,0:T(8,128)S(1)}, u32[]{:S(2)}, u32[]{:S(2)}) collective-permute-start(f32[128,256]{1,0:T(8,128)S(1)} %get-tuple-element.58), channel_id=1, source_target_pairs={{0,1},{1,0},{2,3},{3,2},{4,5},{5,4},{6,7},{7,6},{8,9},{9,8},{10,11... | collective-permute-start | bytes 393224 | tf_op jit(solution)/shard_map/ppermute | solution.py:416
  41.8 12.4 %collective-permute-start.13 = (f32[128,256]{1,0:T(8,128)S(1)}, f32[128,256]{1,0:T(8,128)S(1)}, u32[]{:S(2)}, u32[]{:S(2)}) collective-permute-start(f32[128,256]{1,0:T(8,128)S(1)} %get-tuple-element.65), channel_id=1, source_target_pairs={{0,1},{1,0},{2,3},{3,2},{4,5},{5,4},{6,7},{7,6},{8,9},{9,8},{10,11... | collective-permute-start | bytes 393224 | tf_op jit(solution)/shard_map/ppermute | solution.py:416

commit v11 on v9

--- a/solution.py
+++ b/solution.py
@@ -484,10 +484,11 @@
         [(block, f32), ((3,) + block, f32)],
         scalars=2,
     )
-    sides = around(side)
     (early_row,) = call(
         moments_kernel, (start, image, side, inverse), [((1, LANES), f32)], scratch=False
     )
+    side, early_row = lax.optimization_barrier((side, early_row))
+    sides = around(side)
     second, ratio = call(
         second_kernel,
         (*shifts, *images, inverse, early_row, *blocks),

time: 56.2 us -> 56.2 us (level)
  no operation moved by 1% of the time
where the time goes in v11:
time: 56.2 us; the launch traced here: 56 us
  starting transfers between devices  23.2 us (41%)
  Pallas kernels  18.7 us (33%)
  blocking collectives  12.4 us (22%)
  waiting for transfers between devices  0.85 us (2%)
  between operations  0.83 us (1%)
    ppermute x9, starting transfers between devices, mate(): return lax.ppermute(values, AXES, swap)  19.7 us
    pallas_call x9, Pallas kernels, call(): pl.pallas_call(kernel, out_shape=[jax.ShapeDtypeStruct(shape, kind) for s...  17.2 us
    all_to_all x1, blocking collectives, exchanged(): lax.all_to_all(spread, AXES, 0, 0, tiled=True).reshape(devices, LANES)  12.4 us
    ppermute x5, starting transfers between devices, facing(): return lax.ppermute(values, AXES, across)  3.49 us
    pallas_call x1, Pallas kernels, one_sector_body(): pl.pallas_call(picking_kernel, out_shape=[jax.ShapeDtypeStruct(shape, f32...  1.55 us
  transfers between devices with their start and end apart: 14, of which 1 were waited for; matrix products, arithmetic and copies ran while one was open for 0% of the time, Pallas kernels for 28%

profile of v11, /device:TPU:0, one launch (start us, length us, event | category | flops | bytes accessed | tf_op | source)
XLA Modules:
  0.0 56.0 jit_solution(12034303195016318259)
XLA Ops:
  0.6 1.5 %shard_map.68 = (f32[256,256]{1,0:T(8,128)S(1)}, f32[256,256]{1,0:T(8,128)S(1)}, f32[2,256,256]{2,1,0:T(8,128)S(1)}, f32[2,256,256]{2,1,0:T(8,128)S(1)}) custom-call(f32[2,256,256]{2,1,0:T(8,128)} %wave.3, f32[2,256,256]{2,1,0:T(8,128)} %preconditioner.3, f32[2,2,256,256]{3,2,1,0:T(8,128)} %own_left.1, f32[2,2,256,256]{3,2,1,0:T(8,128)} %own_right.1), custom_call_target="tpu_custom_call" | custom-call | tf_op jit(solution)/shard_map/pallas_call | solution.py:447
  2.2 0.5 collective-permute-start.2
  2.7 0.1 collective-permute-start.3
  2.8 0.7 %collective-permute-start.1 = (f32[256,256]{1,0:T(8,128)S(1)}, f32[256,256]{1,0:T(8,128)S(1)}, u32[]{:S(2)}, u32[]{:S(2)}) collective-permute-start(f32[256,256]{1,0:T(8,128)S(1)} %get-tuple-element.36), channel_id=1, source_target_pairs={{1,2},{3,4},{5,6},{7,8},{9,10},{11,12},{13,14},{15,16},{17,18},{19... | collective-permute-start | bytes 786440 | tf_op jit(solution)/shard_map/ppermute | solution.py:417
  3.5 4.3 %collective-permute-start = (s32[2]{0:T(128)S(1)}, s32[2]{0:T(128)S(1)}, u32[]{:S(2)}, u32[]{:S(2)}) collective-permute-start(s32[2]{0:T(128)S(1)} %copy-done.4), channel_id=1, source_target_pairs={{0,1},{1,0},{2,3},{3,2},{4,5},{5,4},{6,7},{7,6},{8,9},{9,8},{10,11... | collective-permute-start | bytes 32 | tf_op jit(solution)/shard_map/ppermute | solution.py:414
  7.8 0.8 %collective-permute-done.mate_shifts = s32[2]{0:T(128)S(1)} collective-permute-done((s32[2]{0:T(128)S(1)}, s32[2]{0:T(128)S(1)}, u32[]{:S(2)}, u32[]{:S(2)}) %collective-permute-start) | collective-permute-done | bytes 40 | tf_op jit(solution)/shard_map/ppermute | solution.py:414
  8.6 0.8 %collective-permute-start.4 = (f32[256,256]{1,0:T(8,128)S(1)}, f32[256,256]{1,0:T(8,128)S(1)}, u32[]{:S(2)}, u32[]{:S(2)}) collective-permute-start(f32[256,256]{1,0:T(8,128)S(1)} %get-tuple-element.44), channel_id=1, source_target_pairs={{1,2},{3,4},{5,6},{7,8},{9,10},{11,12},{13,14},{15,16},{17,18},{19... | collective-permute-start | bytes 786440 | tf_op jit(solution)/shard_map/ppermute | solution.py:417
  9.5 0.0 collective-permute-done.3.mate_right
  9.5 0.4 shard_map.69
  9.9 0.0 copy-start.3
  9.9 1.8 %shard_map.70 = (f32[256,256]{1,0:T(8,128)S(1)}, f32[3,256,256]{2,1,0:T(8,128)S(1)}) custom-call(s32[2]{0:T(128)S(1)} %copy-done.4, s32[2]{0:T(128)S(1)} %collective-permute-done.mate_shifts, f32[2,256,256]{2,1,0:T(8,128)S(1)} %copy-done.2, f32[256,256]{1,0:T(8,128)S(1)} %collective-permute-done.1.facing_wave, ...), custom_call_target="tpu_custom_call" | custom-call | tf_op jit(solution)/shard_map/pallas_call | solution.py:432
  11.7 0.7 %collective-permute-start.6 = (f32[256,256]{1,0:T(8,128)S(1)}, f32[256,256]{1,0:T(8,128)S(1)}, u32[]{:S(2)}, u32[]{:S(2)}) collective-permute-start(f32[256,256]{1,0:T(8,128)S(1)} %get-tuple-element.46.image.own_image), channel_id=1, source_target_pairs={{1,2},{3,4},{5,6},{7,8},{9,10},{11,12},{13,14},{15,16},{17,18},{19... | collective-permute-start | bytes 786440 | tf_op jit(solution)/shard_map/ppermute | solution.py:417
  12.4 7.7 %collective-permute-start.5 = (f32[256,256]{1,0:T(8,128)S(1)}, f32[256,256]{1,0:T(8,128)S(1)}, u32[]{:S(2)}, u32[]{:S(2)}) collective-permute-start(f32[256,256]{1,0:T(8,128)S(1)} %get-tuple-element.46.image.own_image), channel_id=1, source_target_pairs={{0,1},{1,0},{2,3},{3,2},{4,5},{5,4},{6,7},{7,6},{8,9},{9,8},{10,11... | collective-permute-start | bytes 786440 | tf_op jit(solution)/shard_map/ppermute | solution.py:414
  20.1 1.8 %shard_map.71 = (f32[256,256]{1,0:T(8,128)S(1)}, f32[3,256,256]{2,1,0:T(8,128)S(1)}) custom-call(s32[2]{0:T(128)S(1)} %copy-done.4, s32[2]{0:T(128)S(1)} %collective-permute-done.mate_shifts, f32[3,256,256]{2,1,0:T(8,128)S(1)} %get-tuple-element.43.start, f32[2,256,256]{2,1,0:T(8,128)S(1)} %copy-done.3, ...), custom_call_target="tpu_custom_call" | custom-call | tf_op jit(solution)/shard_map/pallas_call | solution.py:432
  22.0 1.0 %shard_map.72._.early_row = f32[1,128]{1,0:T(1,128)S(1)} custom-call(f32[3,256,256]{2,1,0:T(8,128)S(1)} %get-tuple-element.43.start, f32[256,256]{1,0:T(8,128)S(1)} %get-tuple-element.46.image.own_image, f32[256,256]{1,0:T(8,128)S(1)} %get-tuple-element.48.side.own_side, f32[3,256,256]{2,1,0:T(8,128)S(1)} %get-tuple-element.45.inverse), custom_call_target="tpu_custom_call" | custom-call | tf_op jit(solution)/shard_map/pallas_call | solution.py:432
  22.9 0.7 %collective-permute-start.10 = (f32[256,256]{1,0:T(8,128)S(1)}, f32[256,256]{1,0:T(8,128)S(1)}, u32[]{:S(2)}, u32[]{:S(2)}) collective-permute-start(f32[256,256]{1,0:T(8,128)S(1)} %get-tuple-element.48.side.own_side), channel_id=1, source_target_pairs={{1,2},{3,4},{5,6},{7,8},{9,10},{11,12},{13,14},{15,16},{17,18},{19... | collective-permute-start | bytes 786440 | tf_op jit(solution)/shard_map/ppermute | solution.py:417
  23.6 3.5 %collective-permute-start.9 = (f32[256,256]{1,0:T(8,128)S(1)}, f32[256,256]{1,0:T(8,128)S(1)}, u32[]{:S(2)}, u32[]{:S(2)}) collective-permute-start(f32[256,256]{1,0:T(8,128)S(1)} %get-tuple-element.48.side.own_side), channel_id=1, source_target_pairs={{0,1},{1,0},{2,3},{3,2},{4,5},{5,4},{6,7},{7,6},{8,9},{9,8},{10,11... | collective-permute-start | bytes 786440 | tf_op jit(solution)/shard_map/ppermute | solution.py:414
  27.1 0.0 collective-permute-done.6.facing_image
  27.1 0.0 collective-permute-done.5.mate_image
  27.1 1.8 %shard_map.73 = (f32[256,256]{1,0:T(8,128)S(1)}, f32[3,256,256]{2,1,0:T(8,128)S(1)}) custom-call(s32[2]{0:T(128)S(1)} %copy-done.4, s32[2]{0:T(128)S(1)} %collective-permute-done.mate_shifts, f32[256,256]{1,0:T(8,128)S(1)} %get-tuple-element.46.image.own_image, f32[256,256]{1,0:T(8,128)S(1)} %collective-permute-done.5.mate_image, ...), custom_call_target="tpu_custom_call" | custom-call | tf_op jit(solution)/shard_map/pallas_call | solution.py:432
  28.9 0.7 %collective-permute-start.8 = (f32[256,256]{1,0:T(8,128)S(1)}, f32[256,256]{1,0:T(8,128)S(1)}, u32[]{:S(2)}, u32[]{:S(2)}) collective-permute-start(f32[256,256]{1,0:T(8,128)S(1)} %get-tuple-element.50.second.own_second), channel_id=1, source_target_pairs={{1,2},{3,4},{5,6},{7,8},{9,10},{11,12},{13,14},{15,16},{17,18},{19... | collective-permute-start | bytes 786440 | tf_op jit(solution)/shard_map/ppermute | solution.py:417
  29.6 2.8 %collective-permute-start.7 = (f32[256,256]{1,0:T(8,128)S(1)}, f32[256,256]{1,0:T(8,128)S(1)}, u32[]{:S(2)}, u32[]{:S(2)}) collective-permute-start(f32[256,256]{1,0:T(8,128)S(1)} %get-tuple-element.50.second.own_second), channel_id=1, source_target_pairs={{0,1},{1,0},{2,3},{3,2},{4,5},{5,4},{6,7},{7,6},{8,9},{9,8},{10,11... | collective-permute-start | bytes 786440 | tf_op jit(solution)/shard_map/ppermute | solution.py:414
  32.4 3.9 %shard_map.74 = (f32[2,256,256]{2,1,0:T(8,128)S(1)}, f32[2,128,256]{2,1,0:T(8,128)S(1)}, f32[2,128,256]{2,1,0:T(8,128)S(1)}, f32[1,128]{1,0:T(1,128)S(1)}) custom-call(s32[2]{0:T(128)S(1)} %copy-done.4, s32[2]{0:T(128)S(1)} %collective-permute-done.mate_shifts, f32[3,256,256]{2,1,0:T(8,128)S(1)} %get-tuple-element.43.start, ...), custom_call_target="tpu_custom_call" | custom-call | tf_op jit(solution)/shard_map/pallas_call | solution.py:432
  36.3 0.1 collective-permute-start.11
  36.4 0.0 collective-permute-done.10.facing_side
  36.4 0.0 collective-permute-done.9.mate_side
  36.4 2.4 %shard_map.75 = (f32[256,256]{1,0:T(8,128)S(1)}, f32[128,256]{1,0:T(8,128)S(1)}, f32[128,256]{1,0:T(8,128)S(1)}, f32[1,128]{1,0:T(1,128)S(1)}) custom-call(s32[2]{0:T(128)S(1)} %copy-done.4, s32[2]{0:T(128)S(1)} %collective-permute-done.mate_shifts, f32[3,256,256]{2,1,0:T(8,128)S(1)} %get-tuple-element.43.start, ...), custom_call_target="tpu_custom_call" | custom-call | tf_op jit(solution)/shard_map/pallas_call | solution.py:432
  38.8 0.5 collective-permute-start.12
  39.3 2.4 %shard_map.76 = (f32[128,256]{1,0:T(8,128)S(1)}, f32[128,256]{1,0:T(8,128)S(1)}, f32[32,128]{1,0:T(8,128)S(1)}) custom-call(s32[2]{0:T(128)S(1)} %copy-done.4, s32[2]{0:T(128)S(1)} %collective-permute-done.mate_shifts, f32[3,256,256]{2,1,0:T(8,128)S(1)} %get-tuple-element.43.start, f32[3,256,256]{2,1,0:T(8,128)S(1)} %get-tuple-element.45.inverse, ...), custom_call_target="tpu_custom_call" | custom-call | tf_op jit(solution)/shard_map/pallas_call | solution.py:432
  41.7 0.1 collective-permute-start.13
  41.8 12.4 %all_to_all.5 = f32[32,1,128]{2,1,0:T(1,128)S(1)} all-to-all(f32[32,1,128]{2,1,0:T(1,128)S(1)} %bitcast.5), channel_id=1, replica_groups=mesh['sector'=16,'op'=2] {'sector','op'}, dimensions={0} | all-to-all | bytes 32768 | tf_op jit(solution)/shard_map/all_to_all | solution.py:424
  54.2 1.8 %shard_map.77 = (f32[3,2,128,256]{3,2,1,0:T(8,128)}, f32[3]{0:T(128)}) custom-call(f32[32,128]{1,0:T(8,128)S(1)} %bitcast.4, f32[3,256,256]{2,1,0:T(8,128)S(1)} %get-tuple-element.43.start, f32[3,256,256]{2,1,0:T(8,128)S(1)} %get-tuple-element.51.ratio, f32[3,256,256]{2,1,0:T(8,128)S(1)} %get-tuple-element.45.inverse, ...), custom_call_target="tpu_custom_call" | custom-call | tf_op jit(solution)/shard_map/pallas_call | solution.py:432
  (17 shorter events, 0.0 us)
Async XLA Ops:
  0.6 8.8 %copy-start.1 = (f32[2,2,256,256]{3,2,1,0:T(8,128)S(1)}, f32[2,2,256,256]{3,2,1,0:T(8,128)}, u32[]{:S(2)}) copy-start(f32[2,2,256,256]{3,2,1,0:T(8,128)} %own_right.1) | copy-start | bytes 3145732
  0.6 8.8 %copy-start = (f32[2,2,256,256]{3,2,1,0:T(8,128)S(1)}, f32[2,2,256,256]{3,2,1,0:T(8,128)}, u32[]{:S(2)}) copy-start(f32[2,2,256,256]{3,2,1,0:T(8,128)} %own_left.1) | copy-start | bytes 3145732
  2.2 7.2 %collective-permute-start.2 = (f32[2,256,256]{2,1,0:T(8,128)S(1)}, f32[2,256,256]{2,1,0:T(8,128)S(1)}, u32[]{:S(2)}, u32[]{:S(2)}) collective-permute-start(f32[2,256,256]{2,1,0:T(8,128)S(1)} %get-tuple-element.37), channel_id=1, source_target_pairs={{0,1},{1,0},{2,3},{3,2},{4,5},{5,4},{6,7},{7,6},{8,9},{9,8},{10,11... | collective-permute-start | bytes 1572872 | tf_op jit(solution)/shard_map/ppermute | solution.py:414
  2.7 0.8 %copy-start.4 = (s32[2]{0:T(128)S(1)}, s32[2]{0:T(128)}, u32[]{:S(2)}) copy-start(s32[2]{0:T(128)} %own_shifts.11) | copy-start | bytes 28
  2.7 6.7 %collective-permute-start.3 = (f32[2,256,256]{2,1,0:T(8,128)S(1)}, f32[2,256,256]{2,1,0:T(8,128)S(1)}, u32[]{:S(2)}, u32[]{:S(2)}) collective-permute-start(f32[2,256,256]{2,1,0:T(8,128)S(1)} %get-tuple-element.38), channel_id=1, source_target_pairs={{0,1},{1,0},{2,3},{3,2},{4,5},{5,4},{6,7},{7,6},{8,9},{9,8},{10,11... | collective-permute-start | bytes 1572872 | tf_op jit(solution)/shard_map/ppermute | solution.py:414
  2.8 7.1 %collective-permute-start.1 = (f32[256,256]{1,0:T(8,128)S(1)}, f32[256,256]{1,0:T(8,128)S(1)}, u32[]{:S(2)}, u32[]{:S(2)}) collective-permute-start(f32[256,256]{1,0:T(8,128)S(1)} %get-tuple-element.36), channel_id=1, source_target_pairs={{1,2},{3,4},{5,6},{7,8},{9,10},{11,12},{13,14},{15,16},{17,18},{19... | collective-permute-start | bytes 786440 | tf_op jit(solution)/shard_map/ppermute | solution.py:417
  3.5 5.1 %collective-permute-start = (s32[2]{0:T(128)S(1)}, s32[2]{0:T(128)S(1)}, u32[]{:S(2)}, u32[]{:S(2)}) collective-permute-start(s32[2]{0:T(128)S(1)} %copy-done.4), channel_id=1, source_target_pairs={{0,1},{1,0},{2,3},{3,2},{4,5},{5,4},{6,7},{7,6},{8,9},{9,8},{10,11... | collective-permute-start | bytes 32 | tf_op jit(solution)/shard_map/ppermute | solution.py:414
  8.6 1.3 %copy-start.2 = (f32[2,256,256]{2,1,0:T(8,128)S(1)}, f32[2,256,256]{2,1,0:T(8,128)}, u32[]{:S(2)}) copy-start(f32[2,256,256]{2,1,0:T(8,128)} %wave.3) | copy-start | bytes 1572868
  8.6 11.5 %collective-permute-start.4 = (f32[256,256]{1,0:T(8,128)S(1)}, f32[256,256]{1,0:T(8,128)S(1)}, u32[]{:S(2)}, u32[]{:S(2)}) collective-permute-start(f32[256,256]{1,0:T(8,128)S(1)} %get-tuple-element.44), channel_id=1, source_target_pairs={{1,2},{3,4},{5,6},{7,8},{9,10},{11,12},{13,14},{15,16},{17,18},{19... | collective-permute-start | bytes 786440 | tf_op jit(solution)/shard_map/ppermute | solution.py:417
  9.9 10.2 %copy-start.3 = (f32[2,256,256]{2,1,0:T(8,128)S(1)}, f32[2,256,256]{2,1,0:T(8,128)}, u32[]{:S(2)}) copy-start(f32[2,256,256]{2,1,0:T(8,128)} %preconditioner.3) | copy-start | bytes 1572868
  11.7 15.4 %collective-permute-start.6 = (f32[256,256]{1,0:T(8,128)S(1)}, f32[256,256]{1,0:T(8,128)S(1)}, u32[]{:S(2)}, u32[]{:S(2)}) collective-permute-start(f32[256,256]{1,0:T(8,128)S(1)} %get-tuple-element.46.image.own_image), channel_id=1, source_target_pairs={{1,2},{3,4},{5,6},{7,8},{9,10},{11,12},{13,14},{15,16},{17,18},{19... | collective-permute-start | bytes 786440 | tf_op jit(solution)/shard_map/ppermute | solution.py:417
  12.4 14.7 %collective-permute-start.5 = (f32[256,256]{1,0:T(8,128)S(1)}, f32[256,256]{1,0:T(8,128)S(1)}, u32[]{:S(2)}, u32[]{:S(2)}) collective-permute-start(f32[256,256]{1,0:T(8,128)S(1)} %get-tuple-element.46.image.own_image), channel_id=1, source_target_pairs={{0,1},{1,0},{2,3},{3,2},{4,5},{5,4},{6,7},{7,6},{8,9},{9,8},{10,11... | collective-permute-start | bytes 786440 | tf_op jit(solution)/shard_map/ppermute | solution.py:414
  22.9 13.5 %collective-permute-start.10 = (f32[256,256]{1,0:T(8,128)S(1)}, f32[256,256]{1,0:T(8,128)S(1)}, u32[]{:S(2)}, u32[]{:S(2)}) collective-permute-start(f32[256,256]{1,0:T(8,128)S(1)} %get-tuple-element.48.side.own_side), channel_id=1, source_target_pairs={{1,2},{3,4},{5,6},{7,8},{9,10},{11,12},{13,14},{15,16},{17,18},{19... | collective-permute-start | bytes 786440 | tf_op jit(solution)/shard_map/ppermute | solution.py:417
  23.6 12.8 %collective-permute-start.9 = (f32[256,256]{1,0:T(8,128)S(1)}, f32[256,256]{1,0:T(8,128)S(1)}, u32[]{:S(2)}, u32[]{:S(2)}) collective-permute-start(f32[256,256]{1,0:T(8,128)S(1)} %get-tuple-element.48.side.own_side), channel_id=1, source_target_pairs={{0,1},{1,0},{2,3},{3,2},{4,5},{5,4},{6,7},{7,6},{8,9},{9,8},{10,11... | collective-permute-start | bytes 786440 | tf_op jit(solution)/shard_map/ppermute | solution.py:414
  28.9 10.4 %collective-permute-start.8 = (f32[256,256]{1,0:T(8,128)S(1)}, f32[256,256]{1,0:T(8,128)S(1)}, u32[]{:S(2)}, u32[]{:S(2)}) collective-permute-start(f32[256,256]{1,0:T(8,128)S(1)} %get-tuple-element.50.second.own_second), channel_id=1, source_target_pairs={{1,2},{3,4},{5,6},{7,8},{9,10},{11,12},{13,14},{15,16},{17,18},{19... | collective-permute-start | bytes 786440 | tf_op jit(solution)/shard_map/ppermute | solution.py:417
  29.6 9.7 %collective-permute-start.7 = (f32[256,256]{1,0:T(8,128)S(1)}, f32[256,256]{1,0:T(8,128)S(1)}, u32[]{:S(2)}, u32[]{:S(2)}) collective-permute-start(f32[256,256]{1,0:T(8,128)S(1)} %get-tuple-element.50.second.own_second), channel_id=1, source_target_pairs={{0,1},{1,0},{2,3},{3,2},{4,5},{5,4},{6,7},{7,6},{8,9},{9,8},{10,11... | collective-permute-start | bytes 786440 | tf_op jit(solution)/shard_map/ppermute | solution.py:414
  36.3 5.5 %collective-permute-start.11 = (f32[2,128,256]{2,1,0:T(8,128)S(1)}, f32[2,128,256]{2,1,0:T(8,128)S(1)}, u32[]{:S(2)}, u32[]{:S(2)}) collective-permute-start(f32[2,128,256]{2,1,0:T(8,128)S(1)} %get-tuple-element.57), channel_id=1, source_target_pairs={{0,1},{1,0},{2,3},{3,2},{4,5},{5,4},{6,7},{7,6},{8,9},{9,8},{10,11... | collective-permute-start | bytes 786440 | tf_op jit(solution)/shard_map/ppermute | solution.py:414
  38.8 3.0 %collective-permute-start.12 = (f32[128,256]{1,0:T(8,128)S(1)}, f32[128,256]{1,0:T(8,128)S(1)}, u32[]{:S(2)}, u32[]{:S(2)}) collective-permute-start(f32[128,256]{1,0:T(8,128)S(1)} %get-tuple-element.58), channel_id=1, source_target_pairs={{0,1},{1,0},{2,3},{3,2},{4,5},{5,4},{6,7},{7,6},{8,9},{9,8},{10,11... | collective-permute-start | bytes 393224 | tf_op jit(solution)/shard_map/ppermute | solution.py:414
  41.7 12.5 %collective-permute-start.13 = (f32[128,256]{1,0:T(8,128)S(1)}, f32[128,256]{1,0:T(8,128)S(1)}, u32[]{:S(2)}, u32[]{:S(2)}) collective-permute-start(f32[128,256]{1,0:T(8,128)S(1)} %get-tuple-element.65), channel_id=1, source_target_pairs={{0,1},{1,0},{2,3},{3,2},{4,5},{5,4},{6,7},{7,6},{8,9},{9,8},{10,11... | collective-permute-start | bytes 393224 | tf_op jit(solution)/shard_map/ppermute | solution.py:414
